TPU v7x, 32 devices: a whole 2x2x4 slice. The times are simulated.
32 devices in a mesh: dp: 8 (over z, x), fsdp: 4 (over y, core).
Axes of the slice: x: 2, y: 2, z: 4, core: 2. Of those that a mesh axis runs over, the one named last changes fastest.
Arguments:
- tokens: bfloat16 [64, 1200, 512], P(('dp', 'fsdp')), may hold values from -6 to 6
- known_flags: int32 [64, 1200], P(('dp', 'fsdp')), may hold values 0 or 1
- query_proj: bfloat16 [512, 512], P('fsdp'), may hold values from -0.25 to 0.25
- query_bias: bfloat16 [512], P('fsdp'), may hold values from -3 to 3
- key_proj: bfloat16 [512, 512], P('fsdp'), may hold values from -0.25 to 0.25
- value_proj: bfloat16 [512, 512], P('fsdp'), may hold values from -0.25 to 0.25
- value_bias: bfloat16 [512], P('fsdp'), may hold values from -3 to 3
- out_proj: bfloat16 [512, 512], P('fsdp'), may hold values from -4 to 4
- out_bias: bfloat16 [512], P('fsdp'), may hold values from -3 to 3
- gain_first: bfloat16 [512], P('fsdp'), may hold values from 0.5 to 1.5
- shift_first: bfloat16 [512], P('fsdp'), may hold values from -3 to 3
- up_proj: bfloat16 [512, 512], P('fsdp'), may hold values from -0.25 to 0.25
- up_bias: bfloat16 [512], P('fsdp'), may hold values from -3 to 3
- down_proj: bfloat16 [512, 512], P('fsdp'), may hold values from -0.25 to 0.25
- down_bias: bfloat16 [512], P('fsdp'), may hold values from -3 to 3
- gain_second: bfloat16 [512], P('fsdp'), may hold values from 0.5 to 1.5
- shift_second: bfloat16 [512], P('fsdp'), may hold values from -3 to 3
- cotangent: bfloat16 [64, 1200, 512], P(('dp', 'fsdp')), may hold values from -6 to 6
Outputs:
- result: bfloat16 [64, 1200, 512], P(('dp', 'fsdp'))
- tokens_grad: bfloat16 [64, 1200, 512], P(('dp', 'fsdp'))
- query_proj_grad: float32 [512, 512], P('fsdp')
- query_bias_grad: float32 [512], P('fsdp')
- key_proj_grad: float32 [512, 512], P('fsdp')
- value_proj_grad: float32 [512, 512], P('fsdp')
- value_bias_grad: float32 [512], P('fsdp')
- out_proj_grad: float32 [512, 512], P('fsdp')
- out_bias_grad: float32 [512], P('fsdp')
- gain_first_grad: float32 [512], P('fsdp')
- shift_first_grad: float32 [512], P('fsdp')
- up_proj_grad: float32 [512, 512], P('fsdp')
- up_bias_grad: float32 [512], P('fsdp')
- down_proj_grad: float32 [512, 512], P('fsdp')
- down_bias_grad: float32 [512], P('fsdp')
- gain_second_grad: float32 [512], P('fsdp')
- shift_second_grad: float32 [512], P('fsdp')
All inputs are finite; a program needn't handle non-finite values. No bound on the sum of `known_flags` on one device may be relied on, other than what follows from the above.
Results may differ from a plain program's by a relative error of at most 0.014.
Values may be sent and summed in bfloat16 or wider, within the bound.
No kernel may reach another device: no remote copies, remote signals or barrier semaphores. Data moves between devices by JAX's collectives and lax.ppermute only.
A program may use at most 128 MiB of HBM per device.

v0:
```python
import jax
import jax.numpy as jnp
from jax import lax
from jax.sharding import PartitionSpec as P

H = 8
HD = 64


NORM_EPSILON = 1e-05
MASK_FILL = -1e30


def norm_rows(rows_in, gain, shift):
    row_mean = jnp.mean(rows_in, axis=-1, keepdims=True)
    centred = rows_in - row_mean
    row_var = jnp.mean(centred * centred, axis=-1, keepdims=True)
    return centred * lax.rsqrt(row_var + NORM_EPSILON) * gain + shift


def gelu_exact(inputs):
    return jax.nn.gelu(inputs, approximate=False)


def dot_plain(left, right):
    return jnp.dot(left, right, preferred_element_type=jnp.float32)


def dot_last(left, right):
    return lax.dot_general(
        left, right, (((1,), (1,)), ((), ())), preferred_element_type=jnp.float32
    )


def dot_first(left, right):
    return lax.dot_general(
        left, right, (((0,), (0,)), ((), ())), preferred_element_type=jnp.float32
    )


def split_heads(matrix):
    return matrix.reshape(matrix.shape[0], H, HD).transpose(1, 0, 2)


def merge_heads(stacked):
    return stacked.transpose(1, 0, 2).reshape(stacked.shape[1], H * HD)


def allowed_keys(known_row):
    places = jnp.arange(known_row.shape[0])
    return (known_row[None, :] > 0) | (places[:, None] == places[None, :])


def head_scores(head_query, head_keys, allowed):
    return jnp.where(allowed, dot_last(head_query, head_keys) * HD ** (-0.5), MASK_FILL)


def attend_cell(items):
    cell_query, cell_keys, cell_values, known_row = items
    allowed = allowed_keys(known_row)

    def attend_one_head(head_items):
        head_query, head_keys, head_values = head_items
        scores = head_scores(head_query, head_keys, allowed)
        row_max = jnp.max(scores, axis=-1, keepdims=True)
        exp_scores = jnp.exp(scores - row_max)
        row_total = jnp.sum(exp_scores, axis=-1, keepdims=True)
        attn_prob = (exp_scores / row_total).astype(jnp.bfloat16)
        head_out = dot_plain(attn_prob, head_values)
        return (head_out, (row_max + jnp.log(row_total))[:, 0])

    head_outs, log_totals = lax.map(
        attend_one_head, (split_heads(cell_query), split_heads(cell_keys), split_heads(cell_values))
    )
    return (merge_heads(head_outs).astype(jnp.bfloat16), log_totals)


def back_cell(items):
    cell_query, cell_keys, cell_values, cell_grad, log_totals, known_row = items
    allowed = allowed_keys(known_row)

    def back_one_head(head_items):
        head_query, head_keys, head_values, head_grad, log_total = head_items
        scores = head_scores(head_query, head_keys, allowed)
        attn_prob = jnp.exp(scores - log_total[:, None])
        grad_prob = dot_last(head_grad, head_values)
        delta_row = jnp.sum(attn_prob * grad_prob, axis=-1, keepdims=True)
        grad_score = (attn_prob * (grad_prob - delta_row) * HD ** (-0.5)).astype(jnp.bfloat16)
        grad_query = dot_plain(grad_score, head_keys)
        grad_keys = dot_first(grad_score, head_query)
        grad_values = dot_first(attn_prob.astype(jnp.bfloat16), head_grad)
        return (grad_query, grad_keys, grad_values)

    grad_query, grad_keys, grad_values = lax.map(
        back_one_head,
        (
            split_heads(cell_query),
            split_heads(cell_keys),
            split_heads(cell_values),
            split_heads(cell_grad),
            log_totals,
        ),
    )
    return (
        merge_heads(grad_query).astype(jnp.bfloat16),
        merge_heads(grad_keys).astype(jnp.bfloat16),
        merge_heads(grad_values).astype(jnp.bfloat16),
    )


def column_sum(matrix):
    return jnp.sum(matrix.astype(jnp.float32), axis=0)


def body(
    tokens,
    known_flags,
    query_proj,
    query_bias,
    key_proj,
    value_proj,
    value_bias,
    out_proj,
    out_bias,
    gain_first,
    shift_first,
    up_proj,
    up_bias,
    down_proj,
    down_bias,
    gain_second,
    shift_second,
    cotangent,
):
    forward_weights = (
        lax.all_gather(query_proj, "fsdp", axis=0, tiled=True),
        lax.all_gather(query_bias, "fsdp", axis=0, tiled=True),
        lax.all_gather(key_proj, "fsdp", axis=0, tiled=True),
        lax.all_gather(value_proj, "fsdp", axis=0, tiled=True),
        lax.all_gather(value_bias, "fsdp", axis=0, tiled=True),
        lax.all_gather(out_proj, "fsdp", axis=0, tiled=True),
        lax.all_gather(out_bias, "fsdp", axis=0, tiled=True),
        lax.all_gather(gain_first, "fsdp", axis=0, tiled=True),
        lax.all_gather(shift_first, "fsdp", axis=0, tiled=True),
        lax.all_gather(up_proj, "fsdp", axis=0, tiled=True),
        lax.all_gather(up_bias, "fsdp", axis=0, tiled=True),
        lax.all_gather(down_proj, "fsdp", axis=0, tiled=True),
        lax.all_gather(down_bias, "fsdp", axis=0, tiled=True),
        lax.all_gather(gain_second, "fsdp", axis=0, tiled=True),
        lax.all_gather(shift_second, "fsdp", axis=0, tiled=True),
    )
    (
        full_query,
        full_query_bias,
        full_keys,
        full_values,
        full_value_bias,
        full_out,
        full_out_bias,
        full_gain_one,
        full_shift_one,
        full_up,
        full_up_bias,
        full_down,
        full_down_bias,
        full_gain_two,
        full_shift_two,
    ) = forward_weights
    cell_count, length, width = tokens.shape
    rows_in = tokens.reshape(cell_count * length, width)
    inputs_float = rows_in.astype(jnp.float32)
    queries = (dot_plain(rows_in, full_query) + full_query_bias.astype(jnp.float32)).astype(
        jnp.bfloat16
    )
    keys_all = dot_plain(rows_in, full_keys).astype(jnp.bfloat16)
    values_all = (dot_plain(rows_in, full_values) + full_value_bias.astype(jnp.float32)).astype(
        jnp.bfloat16
    )
    attended, log_totals = lax.map(
        attend_cell,
        (
            queries.reshape(cell_count, length, width),
            keys_all.reshape(cell_count, length, width),
            values_all.reshape(cell_count, length, width),
            known_flags,
        ),
    )
    attended = attended.reshape(cell_count * length, width)
    attn_out = dot_plain(attended, full_out) + full_out_bias.astype(jnp.float32)
    first_in = inputs_float + attn_out
    first_norm = norm_rows(
        first_in, full_gain_one.astype(jnp.float32), full_shift_one.astype(jnp.float32)
    )
    first_low = first_norm.astype(jnp.bfloat16)
    pre_act = dot_plain(first_low, full_up) + full_up_bias.astype(jnp.float32)
    activated = gelu_exact(pre_act).astype(jnp.bfloat16)
    ff_out = dot_plain(activated, full_down) + full_down_bias.astype(jnp.float32)
    second_in = first_norm + ff_out
    second_out = norm_rows(
        second_in, full_gain_two.astype(jnp.float32), full_shift_two.astype(jnp.float32)
    )
    result = second_out.astype(jnp.bfloat16).reshape(cell_count, length, width)
    back_weights = (
        lax.all_gather(query_proj, "fsdp", axis=0, tiled=True),
        lax.all_gather(query_bias, "fsdp", axis=0, tiled=True),
        lax.all_gather(key_proj, "fsdp", axis=0, tiled=True),
        lax.all_gather(value_proj, "fsdp", axis=0, tiled=True),
        lax.all_gather(value_bias, "fsdp", axis=0, tiled=True),
        lax.all_gather(out_proj, "fsdp", axis=0, tiled=True),
        lax.all_gather(out_bias, "fsdp", axis=0, tiled=True),
        lax.all_gather(gain_first, "fsdp", axis=0, tiled=True),
        lax.all_gather(shift_first, "fsdp", axis=0, tiled=True),
        lax.all_gather(up_proj, "fsdp", axis=0, tiled=True),
        lax.all_gather(up_bias, "fsdp", axis=0, tiled=True),
        lax.all_gather(down_proj, "fsdp", axis=0, tiled=True),
        lax.all_gather(down_bias, "fsdp", axis=0, tiled=True),
        lax.all_gather(gain_second, "fsdp", axis=0, tiled=True),
        lax.all_gather(shift_second, "fsdp", axis=0, tiled=True),
    )
    (
        back_query,
        back_query_bias,
        back_keys,
        back_values,
        back_value_bias,
        back_out,
        back_out_bias,
        back_gain_one,
        back_shift_one,
        back_up,
        back_up_bias,
        back_down,
        back_down_bias,
        back_gain_two,
        back_shift_two,
    ) = back_weights
    grad_rows = cotangent.reshape(cell_count * length, width).astype(jnp.float32)
    norm_value, pull_second = jax.vjp(
        norm_rows, second_in, back_gain_two.astype(jnp.float32), back_shift_two.astype(jnp.float32)
    )
    d_second, gain_two_grad, shift_two_grad = pull_second(grad_rows)
    d_ff = d_second.astype(jnp.bfloat16)
    down_bias_grad = column_sum(d_ff)
    down_proj_grad = dot_first(activated, d_ff)
    gelu_value, pull_gelu = jax.vjp(gelu_exact, pre_act)
    d_pre = pull_gelu(dot_last(d_ff, back_down))[0].astype(jnp.bfloat16)
    up_bias_grad = column_sum(d_pre)
    up_proj_grad = dot_first(first_low, d_pre)
    d_first = d_second + dot_last(d_pre, back_up)
    norm_first, pull_first = jax.vjp(
        norm_rows, first_in, back_gain_one.astype(jnp.float32), back_shift_one.astype(jnp.float32)
    )
    d_hidden, gain_one_grad, shift_one_grad = pull_first(d_first)
    d_attn = d_hidden.astype(jnp.bfloat16)
    out_bias_grad = column_sum(d_attn)
    out_proj_grad = dot_first(attended, d_attn)
    d_att = dot_last(d_attn, back_out).astype(jnp.bfloat16)
    d_queries, d_keys, d_values = lax.map(
        back_cell,
        (
            queries.reshape(cell_count, length, width),
            keys_all.reshape(cell_count, length, width),
            values_all.reshape(cell_count, length, width),
            d_att.reshape(cell_count, length, width),
            log_totals,
            known_flags,
        ),
    )
    d_queries = d_queries.reshape(cell_count * length, width)
    d_keys = d_keys.reshape(cell_count * length, width)
    d_values = d_values.reshape(cell_count * length, width)
    query_bias_grad = column_sum(d_queries)
    value_bias_grad = column_sum(d_values)
    query_proj_grad = dot_first(rows_in, d_queries)
    key_proj_grad = dot_first(rows_in, d_keys)
    value_proj_grad = dot_first(rows_in, d_values)
    input_grad = (
        d_hidden
        + dot_last(d_queries, back_query)
        + dot_last(d_keys, back_keys)
        + dot_last(d_values, back_values)
    )
    tokens_grad = input_grad.astype(jnp.bfloat16).reshape(cell_count, length, width)
    owned = (
        lax.psum_scatter(query_proj_grad, "fsdp", scatter_dimension=0, tiled=True),
        lax.psum_scatter(query_bias_grad, "fsdp", scatter_dimension=0, tiled=True),
        lax.psum_scatter(key_proj_grad, "fsdp", scatter_dimension=0, tiled=True),
        lax.psum_scatter(value_proj_grad, "fsdp", scatter_dimension=0, tiled=True),
        lax.psum_scatter(value_bias_grad, "fsdp", scatter_dimension=0, tiled=True),
        lax.psum_scatter(out_proj_grad, "fsdp", scatter_dimension=0, tiled=True),
        lax.psum_scatter(out_bias_grad, "fsdp", scatter_dimension=0, tiled=True),
        lax.psum_scatter(gain_one_grad, "fsdp", scatter_dimension=0, tiled=True),
        lax.psum_scatter(shift_one_grad, "fsdp", scatter_dimension=0, tiled=True),
        lax.psum_scatter(up_proj_grad, "fsdp", scatter_dimension=0, tiled=True),
        lax.psum_scatter(up_bias_grad, "fsdp", scatter_dimension=0, tiled=True),
        lax.psum_scatter(down_proj_grad, "fsdp", scatter_dimension=0, tiled=True),
        lax.psum_scatter(down_bias_grad, "fsdp", scatter_dimension=0, tiled=True),
        lax.psum_scatter(gain_two_grad, "fsdp", scatter_dimension=0, tiled=True),
        lax.psum_scatter(shift_two_grad, "fsdp", scatter_dimension=0, tiled=True),
    )
    (
        owned_query,
        owned_query_bias,
        owned_keys,
        owned_values,
        owned_value_bias,
        owned_out,
        owned_out_bias,
        owned_gain_one,
        owned_shift_one,
        owned_up,
        owned_up_bias,
        owned_down,
        owned_down_bias,
        owned_gain_two,
        owned_shift_two,
    ) = owned
    summed = lax.psum(
        (
            owned_query,
            owned_query_bias,
            owned_keys,
            owned_values,
            owned_value_bias,
            owned_out,
            owned_out_bias,
            owned_gain_one,
            owned_shift_one,
            owned_up,
            owned_up_bias,
            owned_down,
            owned_down_bias,
            owned_gain_two,
            owned_shift_two,
        ),
        "dp",
    )
    return (
        result,
        tokens_grad,
        summed[0],
        summed[1],
        summed[2],
        summed[3],
        summed[4],
        summed[5],
        summed[6],
        summed[7],
        summed[8],
        summed[9],
        summed[10],
        summed[11],
        summed[12],
        summed[13],
        summed[14],
    )


def solution(mesh):
    in_specs = (
        P(("dp", "fsdp"), None, None),
        P(("dp", "fsdp"), None),
        P("fsdp", None),
        P("fsdp"),
        P("fsdp", None),
        P("fsdp", None),
        P("fsdp"),
        P("fsdp", None),
        P("fsdp"),
        P("fsdp"),
        P("fsdp"),
        P("fsdp", None),
        P("fsdp"),
        P("fsdp", None),
        P("fsdp"),
        P("fsdp"),
        P("fsdp"),
        P(("dp", "fsdp"), None, None),
    )
    out_specs = (
        P(("dp", "fsdp"), None, None),
        P(("dp", "fsdp"), None, None),
        P("fsdp", None),
        P("fsdp"),
        P("fsdp", None),
        P("fsdp", None),
        P("fsdp"),
        P("fsdp", None),
        P("fsdp"),
        P("fsdp"),
        P("fsdp"),
        P("fsdp", None),
        P("fsdp"),
        P("fsdp", None),
        P("fsdp"),
        P("fsdp"),
        P("fsdp"),
    )
    return jax.shard_map(body, mesh=mesh, in_specs=in_specs, out_specs=out_specs, check_vma=False)
```

profile of v0, /device:TPU:0, one launch (start us, length us, event | category | flops | bytes accessed | tf_op | source)
XLA Modules:
  0.0 712.8 jit_solution(4285067591893442840)
XLA Ops:
  7.3 6.2 all-gather
  13.4 5.4 all-gather.1
  18.8 5.2 all-gather.2
  24.6 5.2 all-gather.3
  30.3 5.2 all-gather.4
  36.0 5.2 all-gather.5
  41.8 5.2 all-gather.6
  47.5 5.2 all-gather.7
  53.3 5.2 all-gather.8
  59.0 7.6 %all_gather.53 = bf16[512,512]{1,0:T(8,128)(2,1)S(1)} all-gather(bf16[128,512]{1,0:T(8,128)(2,1)} %param.28), channel_id=1, replica_groups=mesh['dp'=8,'fsdp'=4] {'fsdp'}, dimensions={0}, use_global_device_ids=true | all-gather | bytes 655360 | tf_op jit(solution)/shard_map/all_gather | solution.py:136
  66.7 7.5 %all_gather.55 = bf16[512,512]{1,0:T(8,128)(2,1)S(1)} all-gather(bf16[128,512]{1,0:T(8,128)(2,1)} %param.30), channel_id=1, replica_groups=mesh['dp'=8,'fsdp'=4] {'fsdp'}, dimensions={0}, use_global_device_ids=true | all-gather | bytes 655360 | tf_op jit(solution)/shard_map/all_gather | solution.py:138
  74.2 7.5 %all_gather.56 = bf16[512,512]{1,0:T(8,128)(2,1)S(1)} all-gather(bf16[128,512]{1,0:T(8,128)(2,1)} %param.31), channel_id=1, replica_groups=mesh['dp'=8,'fsdp'=4] {'fsdp'}, dimensions={0}, use_global_device_ids=true | all-gather | bytes 655360 | tf_op jit(solution)/shard_map/all_gather | solution.py:139
  81.7 9.3 %all_gather.58 = bf16[512,512]{1,0:T(8,128)(2,1)} all-gather(bf16[128,512]{1,0:T(8,128)(2,1)} %param.33), channel_id=1, replica_groups=mesh['dp'=8,'fsdp'=4] {'fsdp'}, dimensions={0}, use_global_device_ids=true | all-gather | bytes 655360 | tf_op jit(solution)/shard_map/all_gather | solution.py:141
  91.0 8.2 %all_gather.62 = bf16[512,512]{1,0:T(8,128)(2,1)} all-gather(bf16[128,512]{1,0:T(8,128)(2,1)} %param.37), channel_id=1, replica_groups=mesh['dp'=8,'fsdp'=4] {'fsdp'}, dimensions={0}, use_global_device_ids=true | all-gather | bytes 655360 | tf_op jit(solution)/shard_map/all_gather | solution.py:145
  99.2 9.5 %all_gather.64 = bf16[512,512]{1,0:T(8,128)(2,1)} all-gather(bf16[128,512]{1,0:T(8,128)(2,1)} %param.39), channel_id=1, replica_groups=mesh['dp'=8,'fsdp'=4] {'fsdp'}, dimensions={0}, use_global_device_ids=true | all-gather | bytes 655360 | tf_op jit(solution)/shard_map/all_gather | solution.py:147
  125.9 99.8 %while.55 = (s32[]{:T(128)}, bf16[2,1200,512]{2,1,0:T(8,128)(2,1)}, f32[2,8,1200]{2,1,0:T(8,128)}, bf16[2,1200,512]{1,2,0:T(8,128)(2,1)}, bf16[2,1200,512]{1,2,0...) while((s32[]{:T(128)}, bf16[2,1200,512]{2,1,0:T(8,128)(2,1)}, ...), condition=%wide.region_5.6_spmd, body=%wide.region_0.5_spmd.sunk | while | flops 383040000 | bytes 30924512 | solution.py:179
  131.9 41.6 %while.58 = (s32[]{:T(128)}, bf16[8,1200,64]{1,2,0:T(8,128)(2,1)S(1)}, f32[8,1200]{1,0:T(8,128)S(1)}, bf16[8,1200,64]{1,2,0:T(8,128)(2,1)}, bf16[8,1200,64]{1,2,...) while((s32[]{:T(128)}, ...), condition=%wide.region_4.4_spmd.clone, body=%wide.region_1.3_spmd.clone.sunk | while | flops 383038784 | bytes 18550936 | solution.py:72
  181.7 41.6 %while.58 = (s32[]{:T(128)}, bf16[8,1200,64]{1,2,0:T(8,128)(2,1)S(1)}, f32[8,1200]{1,0:T(8,128)S(1)}, bf16[8,1200,64]{1,2,0:T(8,128)(2,1)}, bf16[8,1200,64]{1,2,...) while((s32[]{:T(128)}, ...), condition=%wide.region_4.4_spmd.clone, body=%wide.region_1.3_spmd.clone.sunk | while | flops 383038784 | bytes 18550936 | solution.py:72
  232.4 13.5 %multiply_convert_fusion.1 = (bf16[2400,512]{1,0:T(8,128)(2,1)S(1)}, f32[2400,512]{1,0:T(8,128)}, f32[2400,512]{1,0:T(8,128)}) fusion(f32[512]{0:T(512)S(1)} %bitcast.276, bf16[2400,512]{1,0:T(8,128)(2,1)S(1)} %fusion.63, bf16[512,512]{1,0:T(8,128)(2,1)S(1)} %copy-done.18), kind=kOutput, calls=%fused_computation.101 | convolution fusion | flops 1339392000 | bytes 15271936 | tf_op jit(solution)/shard_map/dot_general | solution.py:26
  264.6 6.0 convert_reduce_fusion.4
  279.0 9.3 %multiply_reduce_fusion.1 = (f32[512]{0:T(512)}, f32[2400]{0:T(1024)S(1)}, f32[512]{0:T(512)}, f32[2400,512]{1,0:T(8,128)S(1)}) fusion(f32[2400,512]{1,0:T(8,128)} %copy-done, f32[2400]{0:T(1024)S(1)} %fusion.64, f32[2400]{0:T(1024)S(1)} %broadcast_multiply_fusion.1, f32[512]{0:T(512)} %bitcast.266, bf16[2400,512]{1,0:T(8,128)(2,1)} %copy-done.11, ...), kind=kOutput, calls=%fused_computation.94 | convolution fusion | flops 1270575744 | bytes 17772032 | tf_op jit(solution)/shard_map/dot_general | solution.py:30
  301.9 212.7 %while.57 = (s32[]{:T(128)}, bf16[2,1200,512]{1,2,0:T(8,128)(2,1)}, bf16[2,1200,512]{1,2,0:T(8,128)(2,1)}, bf16[2,1200,512]{1,2,0:T(8,128)(2,1)}, bf16[2,1200,51...) while((s32[]{:T(128)}, bf16[2,1200,512]{1,2,0:T(8,128)(2,1)}, ...), condition=%wide.region_18.19_spmd, body=%wide.region_14.18_spmd.sunk | while | flops 938880000 | bytes 66559980 | solution.py:258
  310.4 91.9 %while.59 = (s32[]{:T(128)}, bf16[8,1200,64]{1,2,0:T(8,128)(2,1)}, bf16[8,1200,64]{1,2,0:T(8,128)(2,1)}, bf16[8,1200,64]{1,2,0:T(8,128)(2,1)}, bf16[8,1200,64]{1...) while((s32[]{:T(128)}, bf16[8,1200,64]{1,2,0:T(8,128)(2,1)}, ...), condition=%wide.region_17.17_spmd.clone, body=%wide.region_15.16_spmd.clone.sunk | while | flops 938878784 | bytes 46324600 | solution.py:94
  416.8 91.9 %while.59 = (s32[]{:T(128)}, bf16[8,1200,64]{1,2,0:T(8,128)(2,1)}, bf16[8,1200,64]{1,2,0:T(8,128)(2,1)}, bf16[8,1200,64]{1,2,0:T(8,128)(2,1)}, bf16[8,1200,64]{1...) while((s32[]{:T(128)}, bf16[8,1200,64]{1,2,0:T(8,128)(2,1)}, ...), condition=%wide.region_17.17_spmd.clone, body=%wide.region_15.16_spmd.clone.sunk | while | flops 938878784 | bytes 46324600 | solution.py:94
  514.5 5.1 convolution_bitcast_fusion.3
  524.0 5.3 convolution_bitcast_fusion.4
  532.3 4.6 copy.82
  536.9 4.3 copy.80
  546.5 10.4 %all-reduce.11 = (f32[512]{0:T(512)S(1)}, f32[512]{0:T(512)S(1)}, f32[512]{0:T(512)S(1)}, f32[512]{0:T(512)S(1)}, f32[512]{0:T(512)S(1)}, /*index=5*/f32[512]{0:...) all-reduce(f32[512]{0:T(512)S(1)} %get-tuple-element.489, ...), channel_id=3, replica_groups=mesh['dp'=8,'fsdp'=4] {'fsdp'}, use_global_device_ids=true, to_apply=%region_22.23.clone | all-reduce | flops 4608 | bytes 36864
  557.6 22.4 %all-reduce.9 = (f32[128]{0:T(128)}, f32[128]{0:T(128)}, f32[128]{0:T(128)}, f32[128]{0:T(128)}, f32[128]{0:T(128)}, /*index=5*/f32[128]{0:T(128)}, f32[128]{0:T(128)}, f32[128]{0:T(128)}, f32[128]{0:T(128)}) all-reduce(f32[128]{0:T(128)S(1)} %dynamic-slice.1, f32[128]{0:T(128)S(1)} %dynamic-slice.3, ...), channel_id=1, replica_groups=mesh['dp'=8,'fsdp'=4] {'dp'}, use_global_device_ids=true, to_apply=%region_23.24 | all-reduce | flops 1152 | bytes 9216 | tf_op jit(solution)/shard_map/psum | solution.py:318
  580.1 19.8 %reduce-scatter.7.cloned.1.call-done = f32[128,512]{0,1:T(8,128)} async-done(((f32[512,512]{0,1:T(8,128)}), f32[128,512]{0,1:T(8,128)}) %reduce-scatter.7.cloned.1.call-update) | async-done | bytes 262160 | tf_op jit(solution)/shard_map/reduce_scatter | solution.py:285
  608.6 86.7 %all-reduce.14.cloned.1.call-done = (f32[128,512]{0,1:T(8,128)}, f32[128,512]{0,1:T(8,128)}, f32[128,512]{0,1:T(8,128)}, f32[128,512]{1,0:T(8,128)}, f32[128,512]{1,0:T(8,128)}, /*index=5*/f32[128,512]{1,0:T(8,128)}) async-done(((f32[128,512]{0,1:T(8,128)}, f32[128,512]{0,1:T(8,128)}, f32[128,512]{0,1:T(8,128)}, f32[128,512]{1,0:T(8,128)}, f32[128,512]{1,0:T(8,128)}, /*index=5*/f32[128,512]{1,0:T(8,128)}), ...) | async-done | bytes 1572880 | tf_op jit(solution)/shard_map/psum | solution.py:318
  (424 shorter events, 411.2 us)
Async XLA Ops:
  7.2 572.9 %reduce-scatter.15.cloned.1.call-start = ((), (), s32[]{:S(2)}) async-start(), calls=%async_computation.10 | async-start | bytes 1310720 | tf_op jit(solution)/shard_map/reduce_scatter | solution.py:294
  66.7 47.8 %copy-start.16 = (bf16[512,512]{1,0:T(8,128)(2,1)}, bf16[512,512]{1,0:T(8,128)(2,1)S(1)}, u32[]{:S(2)}) copy-start(bf16[512,512]{1,0:T(8,128)(2,1)S(1)} %all_gather.53) | copy-start | bytes 1572868
  74.2 46.0 %copy-start.14 = (bf16[512,512]{1,0:T(8,128)(2,1)}, bf16[512,512]{1,0:T(8,128)(2,1)S(1)}, u32[]{:S(2)}) copy-start(bf16[512,512]{1,0:T(8,128)(2,1)S(1)} %all_gather.55) | copy-start | bytes 1572868
  81.7 30.1 %copy-start.12 = (bf16[512,512]{1,0:T(8,128)(2,1)}, bf16[512,512]{1,0:T(8,128)(2,1)S(1)}, u32[]{:S(2)}) copy-start(bf16[512,512]{1,0:T(8,128)(2,1)S(1)} %all_gather.56) | copy-start | bytes 1572868
  125.9 99.8 %copy-start.19 = (bf16[512,512]{1,0:T(8,128)(2,1)S(1)}, bf16[512,512]{1,0:T(8,128)(2,1)}, u32[]{:S(2)}) copy-start(bf16[512,512]{1,0:T(8,128)(2,1)} %all_gather.58) | copy-start | bytes 1572868
  125.9 99.8 %copy-start.41 = (f32[4,1,128]{2,1,0:T(1,128)S(1)}, f32[4,1,128]{2,1,0:T(1,128)}, u32[]{:S(2)}) copy-start(f32[4,1,128]{2,1,0:T(1,128)} %convert_element_type.196) | copy-start | bytes 6148
  229.9 16.0 %copy-start = (f32[2400,512]{1,0:T(8,128)}, f32[2400,512]{1,0:T(8,128)S(1)}, u32[]{:S(2)}) copy-start(f32[2400,512]{1,0:T(8,128)S(1)} %get-tuple-element.483) | copy-start | bytes 14745604
  232.4 13.5 %copy-start.9 = (bf16[2400,512]{1,0:T(8,128)(2,1)}, bf16[2400,512]{1,0:T(8,128)(2,1)S(1)}, u32[]{:S(2)}) copy-start(bf16[2400,512]{1,0:T(8,128)(2,1)S(1)} %fusion.63) | copy-start | bytes 7372804
  232.4 14.9 %copy-start.20 = (bf16[512,512]{1,0:T(8,128)(2,1)S(1)}, bf16[512,512]{1,0:T(8,128)(2,1)}, u32[]{:S(2)}) copy-start(bf16[512,512]{1,0:T(8,128)(2,1)} %all_gather.64) | copy-start | bytes 1572868
  232.4 14.9 %copy-start.39 = (f32[4,1,128]{2,1,0:T(1,128)S(1)}, f32[4,1,128]{2,1,0:T(1,128)}, u32[]{:S(2)}) copy-start(f32[4,1,128]{2,1,0:T(1,128)} %convert_element_type.200) | copy-start | bytes 6148
  264.6 7.4 %copy-start.10 = (bf16[2400,512]{1,0:T(8,128)(2,1)S(1)}, bf16[2400,512]{1,0:T(8,128)(2,1)}, u32[]{:S(2)}) copy-start(bf16[2400,512]{1,0:T(8,128)(2,1)} %copy-done.9) | copy-start | bytes 7372804
  274.5 305.6 %reduce-scatter.17.cloned.1.call-start = ((), (), s32[]{:S(2)}) async-start(), calls=%async_computation.11 | async-start | bytes 1310720 | tf_op jit(solution)/shard_map/reduce_scatter | solution.py:296
  278.8 9.5 %copy-start.27 = (f32[2400]{0:T(1024)S(1)}, f32[2400]{0:T(1024)}, u32[]{:S(2)}) copy-start(f32[2400]{0:T(1024)} %copy-done.26) | copy-start | bytes 28804
  278.8 9.5 %copy-start.29 = (f32[4,1,128]{2,1,0:T(1,128)S(1)}, f32[4,1,128]{2,1,0:T(1,128)}, u32[]{:S(2)}) copy-start(f32[4,1,128]{2,1,0:T(1,128)} %convert_element_type.197) | copy-start | bytes 6148
  278.8 301.2 %reduce-scatter.13.cloned.1.call-start = ((), (), s32[]{:S(2)}) async-start(), calls=%async_computation.9 | async-start | bytes 1310720 | tf_op jit(solution)/shard_map/reduce_scatter | solution.py:290
  292.6 6.2 copy-start.23
  298.9 281.2 %reduce-scatter.9.cloned.1.call-start = ((), (), s32[]{:S(2)}) async-start(), calls=%async_computation.7 | async-start | bytes 1310720 | tf_op jit(solution)/shard_map/reduce_scatter | solution.py:287
  519.7 60.4 %reduce-scatter.11.cloned.1.call-start = ((), (), s32[]{:S(2)}) async-start(), calls=%async_computation.8 | async-start | bytes 1310720 | tf_op jit(solution)/shard_map/reduce_scatter | solution.py:288
  524.0 75.8 %reduce-scatter.7.cloned.1.call-start = ((), (), s32[]{:S(2)}) async-start(), calls=%async_computation.6 | async-start | bytes 1310720 | tf_op jit(solution)/shard_map/reduce_scatter | solution.py:285
  524.0 5.6 copy-start.8
  529.4 166.0 %all-reduce.14.cloned.1.call-start = ((), (), s32[]{:S(2)}) async-start(), calls=%async_computation.12 | async-start | bytes 3145728 | tf_op jit(solution)/shard_map/psum | solution.py:318
  532.3 9.0 %copy-start.43 = (u32[32]{0:T(128)S(1)}, u32[32]{0:T(128)}, u32[]{:S(2)}) copy-start(u32[32]{0:T(128)} %constant.167) | copy-start | bytes 388
  532.3 10.3 %copy-start.3 = (bf16[2,1200,512]{2,1,0:T(8,128)(2,1)S(1)}, bf16[2,1200,512]{2,1,0:T(8,128)(2,1)}, u32[]{:S(2)}) copy-start(bf16[2,1200,512]{2,1,0:T(8,128)(2,1)} %param.43) | copy-start | bytes 7372804
  541.2 5.2 copy-start.31
  541.2 5.2 copy-start.32
  541.2 5.3 copy-start.33
  541.2 5.3 copy-start.34
  541.2 5.3 copy-start.35
  541.2 5.3 copy-start.38
  541.3 58.6 %copy-start.17 = (bf16[512,512]{1,0:T(8,128)(2,1)S(1)}, bf16[512,512]{1,0:T(8,128)(2,1)}, u32[]{:S(2)}) copy-start(bf16[512,512]{1,0:T(8,128)(2,1)} %copy-done.16) | copy-start | bytes 1572868
  541.3 58.6 %copy-start.24 = (f32[2400]{0:T(1024)S(1)}, f32[2400]{0:T(1024)}, u32[]{:S(2)}) copy-start(f32[2400]{0:T(1024)} %copy-done.23) | copy-start | bytes 28804
  542.9 56.9 %copy-start.6 = (bf16[2,1200,512]{2,1,0:T(8,128)(2,1)S(1)}, bf16[2,1200,512]{2,1,0:T(8,128)(2,1)}, u32[]{:S(2)}) copy-start(bf16[2,1200,512]{2,1,0:T(8,128)(2,1)} %copy.80) | copy-start | bytes 7372804
  (20 other events, 46.9 us)
Sparse Core Ops, SparseCore 0:
  274.6 25.2 reduce-scatter.14
  302.5 24.8 reduce-scatter.16
  330.0 24.8 reduce-scatter.12
  519.8 25.2 reduce-scatter.8
  547.5 24.8 reduce-scatter.10
  574.9 24.8 reduce-scatter.6
  604.0 91.3 all-reduce.13
where the time goes:
time: 718 us; the launch traced here: 713 us
  matrix products  314 us (44%)
  blocking collectives  130 us (18%)
  waiting for transfers between devices  107 us (15%)
  local copies, waits for them, and re-layouts  85.1 us (12%)
  other arithmetic  59.5 us (8%)
  between operations  15.7 us (2%)
    dot_general x54, matrix products, dot_last(): lax.dot_general(left, right, (((1,), (1,)), ((), ())), preferred_element_...  139 us
    dot_general x38, matrix products, dot_plain(): return jnp.dot(left, right, preferred_element_type=jnp.float32)  96.3 us
    psum x1, waiting for transfers between devices, body(): lax.psum((owned_query, owned_query_bias, owned_keys, owned_values, owned_...  86.7 us
    dot_general x38, matrix products, dot_first(): lax.dot_general(left, right, (((0,), (0,)), ((), ())), preferred_element_...  78.9 us
    dynamic_slice x14, local copies, waits for them, and re-layouts, body(): lax.map(attend_cell, (queries.reshape(cell_count, length, width), keys_al...  28.6 us
    psum x1, blocking collectives, body(): lax.psum((owned_query, owned_query_bias, owned_keys, owned_values, owned_...  22.4 us
    reduce_scatter x1, waiting for transfers between devices, body(): lax.psum_scatter(query_proj_grad, 'fsdp', scatter_dimension=0, tiled=True)  19.8 us
    unnamed x106, local copies, waits for them, and re-layouts  18 us
  transfers between devices with their start and end apart: 7, of which 2 were waited for; matrix products, arithmetic and copies ran while one was open for 39% of the time, Pallas kernels for 0%

commit v1 on v0

v1 whole, which is shorter than its diff:
```python
import functools

import jax
import jax.numpy as jnp
from jax import lax
from jax.experimental import pallas as pl
from jax.experimental.pallas import tpu as pltpu
from jax.sharding import PartitionSpec as P

H = 8
HD = 64
SCALE = HD ** (-0.5)
NORM_EPSILON = 1e-05
MASK_FILL = -1e30

CHUNK = 336
ROWS = 480
ONES = 16
LANES = 128

F32 = jnp.float32
BF16 = jnp.bfloat16
MEBI = 1 << 20


def dot(left, right, left_dim=1, right_dim=0):
    return lax.dot_general(
        left, right, (((left_dim,), (right_dim,)), ((), ())), preferred_element_type=F32
    )


def chunk_rows(chunk):
    return pl.ds(pl.multiple_of(chunk * CHUNK, 16), CHUNK)


def pair_rows(pair, offset=0, size=LANES):
    return pl.ds(pl.multiple_of(pair * LANES + offset, HD), size)


def chunk_count(known):
    return (known + CHUNK - 1) // CHUNK


def gather_kernel(known_ref, flags_ref, x_ref, xc_ref, xt_ref, pos_ref):
    known = known_ref[pl.program_id(0)]
    length = x_ref.shape[1]
    flagged = flags_ref[0] > 0
    before = lax.broadcasted_iota(jnp.int32, (length, length), 0)
    after = lax.broadcasted_iota(jnp.int32, (length, length), 1)
    upper = jnp.where(before <= after, 1.0, 0.0).astype(BF16)
    marks = jnp.broadcast_to(jnp.where(flagged, 1.0, 0.0), (16, length)).astype(BF16)
    place = dot(marks, upper)[0:1, :].astype(jnp.int32) - 1
    place = jnp.where(flagged, place, -1)
    pos_ref[0] = place

    def one_chunk(chunk, carry):
        target = chunk * CHUNK + lax.broadcasted_iota(jnp.int32, (CHUNK, length), 0)
        target = jnp.minimum(target, known - 1)
        chosen = jnp.where(place == target, 1.0, 0.0).astype(BF16)
        xc_ref[0, chunk_rows(chunk), :] = dot(chosen, x_ref[0]).astype(BF16)
        return carry

    lax.fori_loop(0, chunk_count(known), one_chunk, 0)
    width = x_ref.shape[2]
    xt_ref[0, 0:width, :] = x_ref[0].T
    xt_ref[0, width:, :] = jnp.ones((ONES, length), BF16)


def gather_known(known, flags, x):
    cells, length, width = x.shape
    padded = -(-length // CHUNK) * CHUNK
    one = lambda *shape: pl.BlockSpec((1,) + shape, lambda i, known: (i, 0, 0))
    return pl.pallas_call(
        gather_kernel,
        out_shape=(
            jax.ShapeDtypeStruct((cells, padded, width), BF16),
            jax.ShapeDtypeStruct((cells, width + ONES, length), BF16),
            jax.ShapeDtypeStruct((cells, 1, length), jnp.int32),
        ),
        grid_spec=pltpu.PrefetchScalarGridSpec(
            num_scalar_prefetch=1,
            grid=(cells,),
            in_specs=[one(1, length), one(length, width)],
            out_specs=[one(padded, width), one(width + ONES, length), one(1, length)],
        ),
        compiler_params=pltpu.CompilerParams(vmem_limit_bytes=60 * MEBI),
        name="gather_known",
    )(known, flags, x)


def attend_kernel(
    known_ref, xt_ref, xc_ref, pos_ref, wq_ref, wk_ref, wv_ref, bq_ref, bv_ref, bv_row_ref,
    qt_ref, kt_ref, vt_ref, kc_ref, vc_ref, ot_ref, o_ref, lse_ref,
    vct, qz, top, acc,
):
    known = known_ref[pl.program_id(0)]
    width, length = qt_ref.shape[1], qt_ref.shape[2]
    pairs = width // LANES
    steps = chunk_count(known)
    hidden = pos_ref[0] < 0

    xt = xt_ref[0, 0:width, :]
    qt_ref[0] = (dot(wq_ref[...], xt, 0, 0) + bq_ref[...]).astype(BF16)
    kt_ref[0] = dot(wk_ref[...], xt, 0, 0).astype(BF16)
    vt_ref[0] = (dot(wv_ref[...], xt, 0, 0) + bv_ref[...]).astype(BF16)

    def project(chunk, carry):
        rows = chunk_rows(chunk)
        xc = xc_ref[0, rows, :]
        keys = dot(xc, wk_ref[...]).astype(BF16)
        values = dot(xc, wv_ref[...]) + bv_row_ref[...]
        for pair in range(pairs):
            cols = slice(pair * LANES, (pair + 1) * LANES)
            kc_ref[0, pair, rows, :] = keys[:, cols]
            vc_ref[0, pair, rows, :] = values[:, cols].astype(BF16)
        row = chunk * CHUNK + lax.broadcasted_iota(jnp.int32, (CHUNK, width), 0)
        held = jnp.where(row < known, values, 0.0).astype(BF16).T
        row = chunk * CHUNK + lax.broadcasted_iota(jnp.int32, (16, CHUNK), 1)
        valid = jnp.where(row < known, 1.0, 0.0).astype(BF16)
        for head in range(width // HD):
            vct[chunk, head, 0:HD, :] = held[head * HD : (head + 1) * HD, :]
            vct[chunk, head, HD:, :] = valid
        return carry

    lax.fori_loop(0, steps, project, 0)

    def one_pair(pair, carry):
        low = lax.broadcasted_iota(jnp.int32, (LANES, length), 0) < HD
        scaled = qt_ref[0, pair_rows(pair), :].astype(F32) * SCALE
        qz[0] = jnp.where(low, scaled, 0.0).astype(BF16)
        qz[1] = jnp.where(low, 0.0, scaled).astype(BF16)
        for side in range(2):
            rows = pair_rows(pair, side * HD, HD)
            own = jnp.sum(
                qt_ref[0, rows, :].astype(F32) * kt_ref[0, rows, :].astype(F32),
                axis=0,
                keepdims=True,
            )
            top[side] = jnp.where(hidden, own * SCALE, MASK_FILL)
            acc[side, 0:HD, :] = jnp.where(hidden, vt_ref[0, rows, :].astype(F32), 0.0)
            acc[side, HD:, :] = jnp.broadcast_to(jnp.where(hidden, 1.0, 0.0), (16, length))

        def one_chunk(chunk, carry):
            keys = kc_ref[0, pair, chunk_rows(chunk), :]
            for side in range(2):
                scores = dot(keys, qz[side])
                peak = jnp.maximum(top[side], jnp.max(scores, axis=0, keepdims=True))
                probs = jnp.exp(scores - peak).astype(BF16)
                fade = jnp.exp(top[side] - peak)
                acc[side] = acc[side] * fade + dot(vct[chunk, 2 * pair + side], probs)
                top[side] = peak
            return carry

        lax.fori_loop(0, steps, one_chunk, 0)
        for side in range(2):
            total = acc[side, HD : HD + 1, :]
            ot_ref[0, pair_rows(pair, side * HD, HD), :] = (acc[side, 0:HD, :] / total).astype(BF16)
            lse_ref[0, 2 * pair + side] = top[side] + jnp.log(total)
        return carry

    lax.fori_loop(0, pairs, one_pair, 0)
    o_ref[0] = ot_ref[0].T


def attend(known, xt, xc, pos, wq, wk, wv, bq, bv, bv_row):
    cells, length = xt.shape[0], xt.shape[2]
    width = xt.shape[1] - ONES
    padded = xc.shape[1]
    pairs = width // LANES
    one = lambda *shape: pl.BlockSpec((1,) + shape, lambda i, known: (i,) + (0,) * len(shape))
    full = lambda *shape: pl.BlockSpec(shape, lambda i, known: (0,) * len(shape))
    turned = jax.ShapeDtypeStruct((cells, width, length), BF16)
    packed = jax.ShapeDtypeStruct((cells, pairs, padded, LANES), BF16)
    return pl.pallas_call(
        attend_kernel,
        out_shape=(
            turned, turned, turned, packed, packed, turned,
            jax.ShapeDtypeStruct((cells, length, width), BF16),
            jax.ShapeDtypeStruct((cells, H, 1, length), F32),
        ),
        grid_spec=pltpu.PrefetchScalarGridSpec(
            num_scalar_prefetch=1,
            grid=(cells,),
            in_specs=[
                one(width + ONES, length), one(padded, width), one(1, length),
                full(width, width), full(width, width), full(width, width),
                full(width, 1), full(width, 1), full(1, width),
            ],
            out_specs=[
                one(width, length), one(width, length), one(width, length),
                one(pairs, padded, LANES), one(pairs, padded, LANES),
                one(width, length), one(length, width), one(H, 1, length),
            ],
            scratch_shapes=[
                pltpu.VMEM((padded // CHUNK, H, HD + 16, CHUNK), BF16),
                pltpu.VMEM((2, LANES, length), BF16),
                pltpu.VMEM((2, 1, length), F32),
                pltpu.VMEM((2, HD + 16, length), F32),
            ],
        ),
        compiler_params=pltpu.CompilerParams(vmem_limit_bytes=60 * MEBI),
        name="attend",
    )(known, xt, xc, pos, wq, wk, wv, bq, bv, bv_row)


def row_mean(rows):
    return jnp.mean(rows, axis=-1, keepdims=True)


def normalize(rows):
    centred = rows - row_mean(rows)
    scale = lax.rsqrt(row_mean(centred * centred) + NORM_EPSILON)
    return centred * scale, scale


def norm_back(grad, normed, scale):
    return scale * (grad - row_mean(grad) - normed * row_mean(grad * normed))


def column_sum(rows):
    return jnp.sum(rows, axis=0, keepdims=True)


def middle_kernel(
    x_ref, o_ref, cot_ref, wo_ref, wu_ref, wd_ref, vec_ref,
    result_ref, dhid_ref, datt_ref, go_ref, gu_ref, gd_ref, gvec_ref,
):
    @pl.when(pl.program_id(0) == 0)
    def _():
        go_ref[...] = jnp.zeros_like(go_ref)
        gu_ref[...] = jnp.zeros_like(gu_ref)
        gd_ref[...] = jnp.zeros_like(gd_ref)
        gvec_ref[...] = jnp.zeros_like(gvec_ref)

    out_bias, gain_one, shift_one = vec_ref[0:1, :], vec_ref[1:2, :], vec_ref[2:3, :]
    up_bias, down_bias = vec_ref[3:4, :], vec_ref[4:5, :]
    gain_two, shift_two = vec_ref[5:6, :], vec_ref[6:7, :]
    attended = o_ref[...]
    first_in = x_ref[...].astype(F32) + (dot(attended, wo_ref[...]) + out_bias)
    norm_one, scale_one = normalize(first_in)
    first_norm = norm_one * gain_one + shift_one
    first_low = first_norm.astype(BF16)
    pre_act = dot(first_low, wu_ref[...]) + up_bias
    below = 0.5 * (1.0 + lax.erf(pre_act * (0.5**0.5)))
    activated = (pre_act * below).astype(BF16)
    slope = below + pre_act * (jnp.exp(-0.5 * pre_act * pre_act) * 0.3989422804014327)
    second_in = first_norm + (dot(activated, wd_ref[...]) + down_bias)
    norm_two, scale_two = normalize(second_in)
    result_ref[...] = (norm_two * gain_two + shift_two).astype(BF16)

    dy = cot_ref[...].astype(F32)
    d_second = norm_back(dy * gain_two, norm_two, scale_two)
    d_ff = d_second.astype(BF16)
    gd_ref[...] += dot(activated, d_ff, 0, 0)
    d_pre = (dot(d_ff, wd_ref[...], 1, 1) * slope).astype(BF16)
    gu_ref[...] += dot(first_low, d_pre, 0, 0)
    d_first = d_second + dot(d_pre, wu_ref[...], 1, 1)
    d_hidden = norm_back(d_first * gain_one, norm_one, scale_one)
    d_attn = d_hidden.astype(BF16)
    go_ref[...] += dot(attended, d_attn, 0, 0)
    dhid_ref[...] = d_attn
    datt_ref[...] = dot(d_attn, wo_ref[...], 1, 1).astype(BF16)
    gvec_ref[0:1, :] += column_sum(d_attn.astype(F32))
    gvec_ref[1:2, :] += column_sum(d_first * norm_one)
    gvec_ref[2:3, :] += column_sum(d_first)
    gvec_ref[3:4, :] += column_sum(d_pre.astype(F32))
    gvec_ref[4:5, :] += column_sum(d_ff.astype(F32))
    gvec_ref[5:6, :] += column_sum(dy * norm_two)
    gvec_ref[6:7, :] += column_sum(dy)


def middle(x, o, cot, wo, wu, wd, vectors):
    rows, width = x.shape
    step = ROWS if rows % ROWS == 0 else rows
    block = pl.BlockSpec((step, width), lambda i: (i, 0))
    full = lambda *shape: pl.BlockSpec(shape, lambda i: (0,) * len(shape))
    low = jax.ShapeDtypeStruct((rows, width), BF16)
    square = jax.ShapeDtypeStruct((width, width), F32)
    return pl.pallas_call(
        middle_kernel,
        out_shape=(low, low, low, square, square, square, jax.ShapeDtypeStruct((8, width), F32)),
        grid=(rows // step,),
        in_specs=[block, block, block] + [full(width, width)] * 3 + [full(8, width)],
        out_specs=[block, block, block] + [full(width, width)] * 3 + [full(8, width)],
        compiler_params=pltpu.CompilerParams(vmem_limit_bytes=60 * MEBI),
        name="middle",
    )(x, o, cot, wo, wu, wd, vectors)


def back_kernel(
    known_ref, pos_ref, xt_ref, qt_ref, kt_ref, vt_ref, kc_ref, vc_ref, ot_ref, lse_ref,
    datt_ref, dhid_ref, wq_ref, wk_ref, wv_ref,
    tg_ref, gq_ref, gk_ref, gv_ref, gvec_ref,
    dot_t, hot, kct, qz, oz, dqa, dkv, delta, dt,
):
    @pl.when(pl.program_id(0) == 0)
    def _():
        gq_ref[...] = jnp.zeros_like(gq_ref)
        gk_ref[...] = jnp.zeros_like(gk_ref)
        gv_ref[...] = jnp.zeros_like(gv_ref)
        gvec_ref[...] = jnp.zeros_like(gvec_ref)

    known = known_ref[pl.program_id(0)]
    width, length = qt_ref.shape[1], qt_ref.shape[2]
    pairs = width // LANES
    steps = chunk_count(known)
    place = pos_ref[0]
    hidden = place < 0
    dot_t[...] = datt_ref[0].T

    def prepare(chunk, carry):
        row = chunk * CHUNK + lax.broadcasted_iota(jnp.int32, (CHUNK, length), 0)
        hot[chunk] = jnp.where(place == row, 1.0, 0.0).astype(BF16)
        row = chunk * CHUNK + lax.broadcasted_iota(jnp.int32, (CHUNK, LANES), 0)
        for pair in range(pairs):
            keys = kc_ref[0, pair, chunk_rows(chunk), :].astype(F32)
            keys = jnp.where(row < known, keys, 0.0).astype(BF16)
            kct[chunk, pair * LANES : (pair + 1) * LANES, :] = keys.T
        return carry

    lax.fori_loop(0, steps, prepare, 0)

    def one_pair(pair, carry):
        low = lax.broadcasted_iota(jnp.int32, (LANES, length), 0) < HD
        scaled = qt_ref[0, pair_rows(pair), :].astype(F32) * SCALE
        qz[0] = jnp.where(low, scaled, 0.0).astype(BF16)
        qz[1] = jnp.where(low, 0.0, scaled).astype(BF16)
        grads = dot_t[pair_rows(pair), :].astype(F32)
        oz[0] = jnp.where(low, grads, 0.0).astype(BF16)
        oz[1] = jnp.where(low, 0.0, grads).astype(BF16)
        for side in range(2):
            rows = pair_rows(pair, side * HD, HD)
            base = side * HD
            query = qt_ref[0, rows, :].astype(F32) * SCALE
            key = kt_ref[0, rows, :].astype(F32)
            grad = dot_t[rows, :].astype(F32)
            delta_row = jnp.sum(grad * ot_ref[0, rows, :].astype(F32), axis=0, keepdims=True)
            delta[side] = delta_row
            own = jnp.sum(query * key, axis=0, keepdims=True)
            prob = jnp.exp(jnp.where(hidden, own, MASK_FILL) - lse_ref[0, 2 * pair + side])
            own_grad = jnp.sum(grad * vt_ref[0, rows, :].astype(F32), axis=0, keepdims=True)
            back = (prob * (own_grad - delta_row)).astype(BF16).astype(F32)
            dqa[base : base + HD, :] = back * key
            dkv[base : base + HD, :] = back * query
            dkv[LANES + base : LANES + base + HD, :] = prob.astype(BF16).astype(F32) * grad

        def one_chunk(chunk, carry):
            rows = chunk_rows(chunk)
            keys = kc_ref[0, pair, rows, :]
            values = vc_ref[0, pair, rows, :]
            d_keys = jnp.zeros((CHUNK, LANES), F32)
            d_values = jnp.zeros((CHUNK, LANES), F32)
            for side in range(2):
                base = side * HD
                probs = jnp.exp(dot(keys, qz[side]) - lse_ref[0, 2 * pair + side])
                d_scores = (probs * (dot(values, oz[side]) - delta[side])).astype(BF16)
                d_values += dot(probs.astype(BF16), oz[side], 1, 1)
                d_keys += dot(d_scores, qz[side], 1, 1)
                head = kct[chunk, pair_rows(pair, base, HD), :]
                dqa[base : base + HD, :] += dot(head, d_scores)
            both = jnp.concatenate([d_keys, d_values], axis=1).astype(BF16)
            dkv[...] += dot(both, hot[chunk], 0, 0)
            return carry

        lax.fori_loop(0, steps, one_chunk, 0)
        dt[pair_rows(pair), :] = (dqa[...] * SCALE).astype(BF16)
        dt[pl.ds(pl.multiple_of(width + pair * LANES, LANES), LANES), :] = dkv[0:LANES, :].astype(BF16)
        dt[pl.ds(pl.multiple_of(2 * width + pair * LANES, LANES), LANES), :] = dkv[LANES:, :].astype(BF16)
        return carry

    lax.fori_loop(0, pairs, one_pair, 0)

    xt = xt_ref[0]
    for which, grad_ref in enumerate((gq_ref, gk_ref, gv_ref)):
        part = dot(xt, dt[which * width : (which + 1) * width, :], 1, 1)
        grad_ref[...] += part[0:width, :]
        if which != 1:
            gvec_ref[which : which + 1, :] += part[width : width + 1, :]
    back = (
        dot(wq_ref[...], dt[0:width, :])
        + dot(wk_ref[...], dt[width : 2 * width, :])
        + dot(wv_ref[...], dt[2 * width :, :])
    )
    tg_ref[0] = (back.T + dhid_ref[0].astype(F32)).astype(BF16)


def attend_back(known, pos, xt, qt, kt, vt, kc, vc, ot, lse, datt, dhid, wq, wk, wv):
    cells, width, length = qt.shape
    pairs, padded = kc.shape[1], kc.shape[2]
    one = lambda *shape: pl.BlockSpec((1,) + shape, lambda i, known: (i,) + (0,) * len(shape))
    full = lambda *shape: pl.BlockSpec(shape, lambda i, known: (0,) * len(shape))
    turned = one(width, length)
    square = jax.ShapeDtypeStruct((width, width), F32)
    return pl.pallas_call(
        back_kernel,
        out_shape=(
            jax.ShapeDtypeStruct((cells, length, width), BF16),
            square, square, square, jax.ShapeDtypeStruct((8, width), F32),
        ),
        grid_spec=pltpu.PrefetchScalarGridSpec(
            num_scalar_prefetch=1,
            grid=(cells,),
            in_specs=[
                one(1, length), one(width + ONES, length), turned, turned, turned,
                one(pairs, padded, LANES), one(pairs, padded, LANES), turned, one(H, 1, length),
                one(length, width), one(length, width),
                full(width, width), full(width, width), full(width, width),
            ],
            out_specs=[one(length, width)] + [full(width, width)] * 3 + [full(8, width)],
            scratch_shapes=[
                pltpu.VMEM((width, length), BF16),
                pltpu.VMEM((padded // CHUNK, CHUNK, length), BF16),
                pltpu.VMEM((padded // CHUNK, width, CHUNK), BF16),
                pltpu.VMEM((2, LANES, length), BF16),
                pltpu.VMEM((2, LANES, length), BF16),
                pltpu.VMEM((LANES, length), F32),
                pltpu.VMEM((2 * LANES, length), F32),
                pltpu.VMEM((2, 1, length), F32),
                pltpu.VMEM((3 * width, length), BF16),
            ],
        ),
        compiler_params=pltpu.CompilerParams(vmem_limit_bytes=60 * MEBI),
        name="attend_back",
    )(known, pos, xt, qt, kt, vt, kc, vc, ot, lse, datt, dhid, wq, wk, wv)


def layer(tokens, known_flags, cotangent, squares, vectors):
    wq, wk, wv, wo, wu, wd = squares
    bq, bv, bo, g1, s1, bu, bd, g2, s2 = [v.astype(F32) for v in vectors]
    cells, length, width = tokens.shape
    known = jnp.sum((known_flags > 0).astype(jnp.int32), axis=1)
    xc, xt, pos = gather_known(known, known_flags.reshape(cells, 1, length), tokens)
    qt, kt, vt, kc, vc, ot, o, lse = attend(
        known, xt, xc, pos, wq, wk, wv, bq.reshape(-1, 1), bv.reshape(-1, 1), bv.reshape(1, -1)
    )
    flat = lambda a: a.reshape(cells * length, width)
    rows = jnp.stack([bo, g1, s1, bu, bd, g2, s2, jnp.zeros_like(bo)])
    result, dhid, datt, go, gu, gd, gmid = middle(
        flat(tokens), flat(o), flat(cotangent), wo, wu, wd, rows
    )
    cube = lambda a: a.reshape(cells, length, width)
    tg, gq, gk, gv, gatt = attend_back(
        known, pos, xt, qt, kt, vt, kc, vc, ot, lse, cube(datt), cube(dhid), wq, wk, wv
    )
    return cube(result), tg, (gq, gk, gv, go, gu, gd), (
        gatt[0], gatt[2], gmid[0], gmid[1], gmid[2], gmid[3], gmid[4], gmid[5], gmid[6]
    )


SQUARES = (2, 4, 5, 7, 11, 13)
VECTORS = (3, 6, 8, 9, 10, 12, 14, 15, 16)


def body(*args):
    squares = [lax.all_gather(args[i], "fsdp", axis=0, tiled=True) for i in SQUARES]
    vectors = [lax.all_gather(args[i], "fsdp", axis=0, tiled=True) for i in VECTORS]
    result, tg, gs, gv = layer(args[0], args[1], args[17], squares, vectors)
    out = {}
    for i, g in list(zip(SQUARES, gs)) + list(zip(VECTORS, gv)):
        out[i] = lax.psum(lax.psum_scatter(g, "fsdp", scatter_dimension=0, tiled=True), "dp")
    return (result, tg) + tuple(out[i] for i in range(2, 17))


def solution(mesh):
    cells = P(("dp", "fsdp"), None, None)
    specs = tuple(P("fsdp", None) if i in SQUARES else P("fsdp") for i in range(2, 17))
    return jax.shard_map(
        body,
        mesh=mesh,
        in_specs=(cells, P(("dp", "fsdp"), None)) + specs + (cells,),
        out_specs=(cells, cells) + specs,
        check_vma=False,
    )
```

time: 718 us -> 530 us (0.74)
  matrix products: 314 us -> 0 us
  Pallas kernels: 0 us -> 145 us
  waiting for transfers between devices: 107 us -> 223 us
  local copies, waits for them, and re-layouts: 85.1 us -> 14.9 us
  other arithmetic: 59.5 us -> 2.08 us
    dot_general x130 -> x0, matrix products: 314 us -> none  [the longest x54 139 us: dot_last(): lax.dot_general(left, right, (((1,), (1,)), ((), ())), preferred_element_...]
    pallas_call x0 -> x4, Pallas kernels: none -> 145 us  [the longest x1 70.6 us: attend_back(): pl.pallas_call(back_kernel, out_shape=(jax.ShapeDtypeStruct((cells, lengt...]
    reduce_scatter x6, waiting for transfers between devices: 19.8 us -> 159 us  [body(): lax.psum_scatter(g, 'fsdp', scatter_dimension=0, tiled=True)]
    reduce_sum x25 -> x1, other arithmetic: 33.8 us -> 1.48 us  [layer(): known = jnp.sum((known_flags > 0).astype(jnp.int32), axis=1)]
    dynamic_slice x30 -> x0, local copies, waits for them, and re-layouts: 29 us -> none  [the longest x14 28.6 us: body(): lax.map(attend_cell, (queries.reshape(cell_count, length, width), keys_al...]
    psum x1, waiting for transfers between devices: 86.7 us -> 60.3 us  [body(): lax.psum(lax.psum_scatter(g, 'fsdp', scatter_dimension=0, tiled=True), 'dp')]
    convert_element_type x26 -> x0, other arithmetic: 20.6 us -> none  [the longest x16 15.1 us: back_one_head(): (attn_prob * (grad_prob - delta_row) * HD ** (-0.5)).astype(jnp.bfloat16)]
    while x6 -> x0, local copies, waits for them, and re-layouts: 19.4 us -> none  [the longest x3 11.6 us: body(): lax.map(back_cell, (queries.reshape(cell_count, length, width), keys_all....]
  transfers between devices with their start and end apart: 7 -> 7, of which waited for: 2 -> 7; matrix products, arithmetic and copies ran while one was open for 39% -> 0% of each run, Pallas kernels for 0% -> 0%
where the time goes in v1:
time: 530 us
  waiting for transfers between devices  223 us (42%)
  Pallas kernels  145 us (27%)
  blocking collectives  130 us (25%)
  between operations  15 us (3%)
  local copies, waits for them, and re-layouts  14.9 us (3%)
    reduce_scatter x6, waiting for transfers between devices, body(): lax.psum_scatter(g, 'fsdp', scatter_dimension=0, tiled=True)  159 us
    all_gather x15, blocking collectives, body(): lax.all_gather(args[i], 'fsdp', axis=0, tiled=True)  96.5 us
    pallas_call x1, Pallas kernels, attend_back(): pl.pallas_call(back_kernel, out_shape=(jax.ShapeDtypeStruct((cells, lengt...  70.6 us
    psum x1, waiting for transfers between devices, body(): lax.psum(lax.psum_scatter(g, 'fsdp', scatter_dimension=0, tiled=True), 'dp')  60.3 us
    pallas_call x1, Pallas kernels, attend(): pl.pallas_call(attend_kernel, out_shape=(turned, turned, turned, packed,...  42.2 us
    pallas_call x1, Pallas kernels, middle(): pl.pallas_call(middle_kernel, out_shape=(low, low, low, square, square, s...  24.7 us
    psum x1, blocking collectives, body(): lax.psum(lax.psum_scatter(g, 'fsdp', scatter_dimension=0, tiled=True), 'dp')  22.8 us
  transfers between devices with their start and end apart: 7, of which 7 were waited for; matrix products, arithmetic and copies ran while one was open for 0% of the time, Pallas kernels for 0%

profile of v1, /device:TPU:0, one launch (start us, length us, event | category | flops | bytes accessed | tf_op | source)
XLA Modules:
  0.0 529.5 jit_solution(4014079586528181822)
XLA Ops:
  10.1 10.2 %all_gather.45.wq_ref = bf16[512,512]{1,0:T(8,128)(2,1)} all-gather(bf16[128,512]{1,0:T(8,128)(2,1)} %param.20), channel_id=1, replica_groups=mesh['dp'=8,'fsdp'=4] {'fsdp'}, dimensions={0}, use_global_device_ids=true | all-gather | bytes 655360 | tf_op jit(solution)/shard_map/all_gather | solution.py:455
  20.3 7.9 %all_gather.46.wk_ref = bf16[512,512]{1,0:T(8,128)(2,1)} all-gather(bf16[128,512]{1,0:T(8,128)(2,1)} %param.22), channel_id=1, replica_groups=mesh['dp'=8,'fsdp'=4] {'fsdp'}, dimensions={0}, use_global_device_ids=true | all-gather | bytes 655360 | tf_op jit(solution)/shard_map/all_gather | solution.py:455
  28.2 9.6 %all_gather.47.wv_ref = bf16[512,512]{1,0:T(8,128)(2,1)} all-gather(bf16[128,512]{1,0:T(8,128)(2,1)} %param.23), channel_id=1, replica_groups=mesh['dp'=8,'fsdp'=4] {'fsdp'}, dimensions={0}, use_global_device_ids=true | all-gather | bytes 655360 | tf_op jit(solution)/shard_map/all_gather | solution.py:455
  37.8 5.2 all-gather.1
  44.4 5.2 all-gather
  50.5 7.7 %all_gather.50.wo_ref = bf16[512,512]{1,0:T(8,128)(2,1)} all-gather(bf16[128,512]{1,0:T(8,128)(2,1)S(1)} %copy-done.1), channel_id=1, replica_groups=mesh['dp'=8,'fsdp'=4] {'fsdp'}, dimensions={0}, use_global_device_ids=true | all-gather | bytes 655360 | tf_op jit(solution)/shard_map/all_gather | solution.py:455
  58.1 7.7 %all_gather.51.wu_ref = bf16[512,512]{1,0:T(8,128)(2,1)} all-gather(bf16[128,512]{1,0:T(8,128)(2,1)S(1)} %copy-done.2), channel_id=1, replica_groups=mesh['dp'=8,'fsdp'=4] {'fsdp'}, dimensions={0}, use_global_device_ids=true | all-gather | bytes 655360 | tf_op jit(solution)/shard_map/all_gather | solution.py:455
  65.9 7.7 %all_gather.52.wd_ref = bf16[512,512]{1,0:T(8,128)(2,1)} all-gather(bf16[128,512]{1,0:T(8,128)(2,1)S(1)} %copy-done.3), channel_id=1, replica_groups=mesh['dp'=8,'fsdp'=4] {'fsdp'}, dimensions={0}, use_global_device_ids=true | all-gather | bytes 655360 | tf_op jit(solution)/shard_map/all_gather | solution.py:455
  73.6 5.0 all-gather.8
  78.6 5.0 all-gather.7
  83.7 5.0 all-gather.6
  88.7 5.0 all-gather.5
  93.7 5.0 all-gather.4
  98.8 5.0 all-gather.3
  103.8 5.2 all-gather.2
  109.0 7.6 %gather_known.1 = (bf16[2,1344,512]{2,1,0:T(8,128)(2,1)}, bf16[2,528,1200]{2,1,0:T(8,128)(2,1)}, s32[2,1,1200]{2,1,0:T(1,128)}) custom-call(s32[2]{0:T(128)} %fusion.known_ref, s32[2,1,1200]{2,1,0:T(1,128)} %reshape.67.flags_ref, bf16[2,1200,512]{2,1,0:T(8,128)(2,1)} %x_ref.1), custom_call_target="tpu_custom_call" | custom-call | tf_op jit(solution)/shard_map/gather_known/pallas_call | solution.py:73
  117.2 42.2 %attend.1 = (bf16[2,512,1200]{2,1,0:T(8,128)(2,1)}, bf16[2,512,1200]{2,1,0:T(8,128)(2,1)}, bf16[2,512,1200]{2,1,0:T(8,128)(2,1)}, bf16[2,4,1344,128]{3,2,1,0:T(8...) custom-call(s32[2]{0:T(128)} %fusion.known_ref, ...), custom_call_target="tpu_custom_call" | custom-call | tf_op jit(solution)/shard_map/attend/pallas_call | solution.py:174
  159.4 24.7 %middle.1 = (bf16[2400,512]{1,0:T(8,128)(2,1)}, bf16[2400,512]{1,0:T(8,128)(2,1)}, bf16[2400,512]{1,0:T(8,128)(2,1)}, f32[512,512]{1,0:T(8,128)}, f32[512,512]{1...) custom-call(bf16[2400,512]{1,0:T(8,128)(2,1)} %bitcast.53, bf16[2400,512]{1,0:T(8,128)(2,1)} %bitcast.55, ...), custom_call_target="tpu_custom_call" | custom-call | tf_op jit(solution)/shard_map/middle/pallas_call | solution.py:279
  184.1 70.6 %attend_back.1 = (bf16[2,1200,512]{2,1,0:T(8,128)(2,1)}, f32[512,512]{1,0:T(8,128)}, f32[512,512]{1,0:T(8,128)}, f32[512,512]{1,0:T(8,128)}, f32[8,512]{1,0:T(8,128)}) custom-call(s32[2]{0:T(128)} %fusion.known_ref, s32[2,1,1200]{2,1,0:T(1,128)} %get-tuple-element.42.pos_ref, bf16[2,528,1200]{2,1,0:T(8,128)(2,1)} %get-tuple-element.40.xt_ref, ...), custom_call_target="tpu_custom_call" | custom-call | tf_op jit(solution)/shard_map/attend_back/pallas_call | solution.py:394
  258.1 22.1 %reduce-scatter.11.cloned.1.call-done = f32[128,512]{1,0:T(8,128)} async-done(((f32[512,512]{1,0:T(8,128)}), f32[128,512]{1,0:T(8,128)}) %reduce-scatter.11.cloned.1.call-update) | async-done | bytes 262160 | tf_op jit(solution)/shard_map/reduce_scatter | solution.py:460
  280.1 27.6 %reduce-scatter.7.cloned.1.call-done = f32[128,512]{1,0:T(8,128)} async-done(((f32[512,512]{1,0:T(8,128)}), f32[128,512]{1,0:T(8,128)}) %reduce-scatter.7.cloned.1.call-update) | async-done | bytes 262160 | tf_op jit(solution)/shard_map/reduce_scatter | solution.py:460
  307.7 27.5 %reduce-scatter.9.cloned.1.call-done = f32[128,512]{1,0:T(8,128)} async-done(((f32[512,512]{1,0:T(8,128)}), f32[128,512]{1,0:T(8,128)}) %reduce-scatter.9.cloned.1.call-update) | async-done | bytes 262160 | tf_op jit(solution)/shard_map/reduce_scatter | solution.py:460
  335.2 27.5 %reduce-scatter.13.cloned.1.call-done = f32[128,512]{1,0:T(8,128)} async-done(((f32[512,512]{1,0:T(8,128)}), f32[128,512]{1,0:T(8,128)}) %reduce-scatter.13.cloned.1.call-update) | async-done | bytes 262160 | tf_op jit(solution)/shard_map/reduce_scatter | solution.py:460
  362.7 27.3 %reduce-scatter.15.cloned.1.call-done = f32[128,512]{1,0:T(8,128)} async-done(((f32[512,512]{1,0:T(8,128)}), f32[128,512]{1,0:T(8,128)}) %reduce-scatter.15.cloned.1.call-update) | async-done | bytes 262160 | tf_op jit(solution)/shard_map/reduce_scatter | solution.py:460
  390.0 27.5 %reduce-scatter.17.cloned.1.call-done = f32[128,512]{1,0:T(8,128)} async-done(((f32[512,512]{1,0:T(8,128)}), f32[128,512]{1,0:T(8,128)}) %reduce-scatter.17.cloned.1.call-update) | async-done | bytes 262160 | tf_op jit(solution)/shard_map/reduce_scatter | solution.py:460
  419.6 10.2 %all-reduce.11 = (f32[512]{0:T(512)S(1)}, f32[512]{0:T(512)S(1)}, f32[512]{0:T(512)S(1)}, f32[512]{0:T(512)S(1)}, f32[512]{0:T(512)S(1)}, /*index=5*/f32[512]{0:...) all-reduce(f32[512]{0:T(512)S(1)} %bitcast.66, ...), channel_id=3, replica_groups=mesh['dp'=8,'fsdp'=4] {'fsdp'}, use_global_device_ids=true, to_apply=%region_3.0.clone | all-reduce | flops 4608 | bytes 36864
  430.5 22.8 %all-reduce.9 = (f32[128]{0:T(128)}, f32[128]{0:T(128)}, f32[128]{0:T(128)}, f32[128]{0:T(128)}, f32[128]{0:T(128)}, /*index=5*/f32[128]{0:T(128)}, f32[128]{0:T(128)}, f32[128]{0:T(128)}, f32[128]{0:T(128)}) all-reduce(f32[128]{0:T(128)S(1)} %dynamic-slice.1, f32[128]{0:T(128)S(1)} %dynamic-slice.3, ...), channel_id=1, replica_groups=mesh['dp'=8,'fsdp'=4] {'dp'}, use_global_device_ids=true, to_apply=%region_4.0 | all-reduce | flops 1152 | bytes 9216 | tf_op jit(solution)/shard_map/psum | solution.py:460
  453.3 60.3 %all-reduce.14.cloned.1.call-done = (f32[128,512]{1,0:T(8,128)}, f32[128,512]{1,0:T(8,128)}, f32[128,512]{1,0:T(8,128)}, f32[128,512]{1,0:T(8,128)}, f32[128,512]{1,0:T(8,128)}, /*index=5*/f32[128,512]{1,0:T(8,128)}) async-done(((f32[128,512]{1,0:T(8,128)}, f32[128,512]{1,0:T(8,128)}, f32[128,512]{1,0:T(8,128)}, f32[128,512]{1,0:T(8,128)}, f32[128,512]{1,0:T(8,128)}, /*index=5*/f32[128,512]{1,0:T(8,128)}), ...) | async-done | bytes 1572880 | tf_op jit(solution)/shard_map/psum | solution.py:460
  513.6 1.7 copy.45
  515.3 1.7 copy.46
  517.0 1.7 copy.47
  518.6 1.7 copy.48
  (69 shorter events, 13.5 us)
Async XLA Ops:
  7.2 43.3 %copy-start.1 = (bf16[128,512]{1,0:T(8,128)(2,1)S(1)}, bf16[128,512]{1,0:T(8,128)(2,1)}, u32[]{:S(2)}) copy-start(bf16[128,512]{1,0:T(8,128)(2,1)} %param.25) | copy-start | bytes 393220
  7.2 50.9 %copy-start.2 = (bf16[128,512]{1,0:T(8,128)(2,1)S(1)}, bf16[128,512]{1,0:T(8,128)(2,1)}, u32[]{:S(2)}) copy-start(bf16[128,512]{1,0:T(8,128)(2,1)} %param.29) | copy-start | bytes 393220
  7.2 58.7 %copy-start.3 = (bf16[128,512]{1,0:T(8,128)(2,1)S(1)}, bf16[128,512]{1,0:T(8,128)(2,1)}, u32[]{:S(2)}) copy-start(bf16[128,512]{1,0:T(8,128)(2,1)} %param.31) | copy-start | bytes 393220
  7.2 66.4 %copy-start.5 = (bf16[128]{0:T(256)(128)(2,1)S(1)}, bf16[128]{0:T(256)(128)(2,1)}, u32[]{:S(2)}) copy-start(bf16[128]{0:T(256)(128)(2,1)} %param.34) | copy-start | bytes 772
  7.2 71.4 %copy-start.6 = (bf16[128]{0:T(256)(128)(2,1)S(1)}, bf16[128]{0:T(256)(128)(2,1)}, u32[]{:S(2)}) copy-start(bf16[128]{0:T(256)(128)(2,1)} %param.33) | copy-start | bytes 772
  7.2 76.4 %copy-start.7 = (bf16[128]{0:T(256)(128)(2,1)S(1)}, bf16[128]{0:T(256)(128)(2,1)}, u32[]{:S(2)}) copy-start(bf16[128]{0:T(256)(128)(2,1)} %param.32) | copy-start | bytes 772
  7.3 81.4 %copy-start.8 = (bf16[128]{0:T(256)(128)(2,1)S(1)}, bf16[128]{0:T(256)(128)(2,1)}, u32[]{:S(2)}) copy-start(bf16[128]{0:T(256)(128)(2,1)} %param.30) | copy-start | bytes 772
  7.3 86.5 %copy-start.9 = (bf16[128]{0:T(256)(128)(2,1)S(1)}, bf16[128]{0:T(256)(128)(2,1)}, u32[]{:S(2)}) copy-start(bf16[128]{0:T(256)(128)(2,1)} %param.28) | copy-start | bytes 772
  7.3 91.5 %copy-start.10 = (bf16[128]{0:T(256)(128)(2,1)S(1)}, bf16[128]{0:T(256)(128)(2,1)}, u32[]{:S(2)}) copy-start(bf16[128]{0:T(256)(128)(2,1)} %param.27) | copy-start | bytes 772
  7.3 96.5 %copy-start.11 = (bf16[128]{0:T(256)(128)(2,1)S(1)}, bf16[128]{0:T(256)(128)(2,1)}, u32[]{:S(2)}) copy-start(bf16[128]{0:T(256)(128)(2,1)} %param.26) | copy-start | bytes 772
  7.3 272.8 %reduce-scatter.11.cloned.1.call-start = ((), (), s32[]{:S(2)}) async-start(), calls=%async_computation.8 | async-start | bytes 1310720 | tf_op jit(solution)/shard_map/reduce_scatter | solution.py:460
  254.8 53.0 %reduce-scatter.7.cloned.1.call-start = ((), (), s32[]{:S(2)}) async-start(), calls=%async_computation.6 | async-start | bytes 1310720 | tf_op jit(solution)/shard_map/reduce_scatter | solution.py:460
  255.5 79.7 %reduce-scatter.9.cloned.1.call-start = ((), (), s32[]{:S(2)}) async-start(), calls=%async_computation.7 | async-start | bytes 1310720 | tf_op jit(solution)/shard_map/reduce_scatter | solution.py:460
  256.2 161.2 %copy-start.12 = (u32[32]{0:T(128)S(1)}, u32[32]{0:T(128)}, u32[]{:S(2)}) copy-start(u32[32]{0:T(128)} %constant.10) | copy-start | bytes 388
  256.3 163.3 %copy-start.4 = (f32[8,512]{1,0:T(8,128)S(1)}, f32[8,512]{1,0:T(8,128)}, u32[]{:S(2)}) copy-start(f32[8,512]{1,0:T(8,128)} %get-tuple-element.60) | copy-start | bytes 49156
  256.3 106.4 %reduce-scatter.13.cloned.1.call-start = ((), (), s32[]{:S(2)}) async-start(), calls=%async_computation.9 | async-start | bytes 1310720 | tf_op jit(solution)/shard_map/reduce_scatter | solution.py:460
  256.8 133.1 %reduce-scatter.15.cloned.1.call-start = ((), (), s32[]{:S(2)}) async-start(), calls=%async_computation.10 | async-start | bytes 1310720 | tf_op jit(solution)/shard_map/reduce_scatter | solution.py:460
  257.4 160.0 %reduce-scatter.17.cloned.1.call-start = ((), (), s32[]{:S(2)}) async-start(), calls=%async_computation.11 | async-start | bytes 1310720 | tf_op jit(solution)/shard_map/reduce_scatter | solution.py:460
  258.0 255.6 %all-reduce.14.cloned.1.call-start = ((), (), s32[]{:S(2)}) async-start(), calls=%async_computation.12 | async-start | bytes 3145728 | tf_op jit(solution)/shard_map/psum | solution.py:460
  513.6 8.4 %copy-start = (f32[128,512]{1,0:T(8,128)S(1)}, f32[128,512]{1,0:T(8,128)}, u32[]{:S(2)}) copy-start(f32[128,512]{1,0:T(8,128)} %get-tuple-element.111) | copy-start | bytes 786436
Sparse Core Ops, SparseCore 0:
  254.9 25.1 reduce-scatter.10
  282.8 24.8 reduce-scatter.6
  310.3 24.8 reduce-scatter.8
  337.7 24.8 reduce-scatter.12
  365.1 24.8 reduce-scatter.14
  392.5 24.8 reduce-scatter.16
  421.6 91.9 all-reduce.13

commit v2 on v1

v2 whole, which is shorter than its diff:
```python
import functools

import jax
import jax.numpy as jnp
from jax import lax
from jax.experimental import pallas as pl
from jax.experimental.pallas import tpu as pltpu
from jax.sharding import PartitionSpec as P

H = 8
HD = 64
SCALE = HD ** (-0.5)
NORM_EPSILON = 1e-05
MASK_FILL = -1e30
SAFE_SCORE = 50.0

CHUNK = 672
ROWS = 480
ONES = 16
EXTRA = 16
LANES = 128
TRIPLE = 3 * LANES
GROUPS = ((0, 2), (2, 2))

F32 = jnp.float32
BF16 = jnp.bfloat16
VMEM_LIMIT = 60 << 20

SQUARES = (2, 4, 5, 7, 11, 13)
VECTORS = (3, 6, 8, 9, 10, 12, 14, 15, 16)
MIDDLE_VECTORS = 7


def dot(left, right, left_dim=1, right_dim=0):
    return lax.dot_general(
        left, right, (((left_dim,), (right_dim,)), ((), ())), preferred_element_type=F32
    )


def params():
    return pltpu.CompilerParams(vmem_limit_bytes=VMEM_LIMIT)


def cost(flops, moved):
    return pl.CostEstimate(flops=int(flops), bytes_accessed=int(moved), transcendentals=0)


def offsets(shards):
    held, mask = [0], shards // 2
    while mask:
        held = held + [offset ^ mask for offset in held]
        mask //= 2
    return held


def gather_kernel(scalars_ref, flags_ref, x_ref, xc_ref, xt_ref, pos_ref):
    known = scalars_ref[pl.program_id(0)]
    length, width = x_ref.shape[1], x_ref.shape[2]
    flagged = flags_ref[0] > 0
    before = lax.broadcasted_iota(jnp.int32, (length, length), 0)
    after = lax.broadcasted_iota(jnp.int32, (length, length), 1)
    upper = jnp.where(before <= after, 1.0, 0.0).astype(BF16)
    marks = jnp.broadcast_to(jnp.where(flagged, 1.0, 0.0), (16, length)).astype(BF16)
    place = dot(marks, upper)[0:1, :].astype(jnp.int32) - 1
    place = jnp.where(flagged, place, -1)
    pos_ref[0] = place

    for chunk in range(xc_ref.shape[1] // CHUNK):

        @pl.when(chunk * CHUNK < known)
        def _():
            target = chunk * CHUNK + lax.broadcasted_iota(jnp.int32, (CHUNK, length), 0)
            target = jnp.minimum(target, known - 1)
            chosen = jnp.where(place == target, 1.0, 0.0).astype(BF16)
            xc_ref[0, chunk * CHUNK : (chunk + 1) * CHUNK, :] = dot(chosen, x_ref[0]).astype(BF16)

    xt_ref[0, 0:width, :] = x_ref[0].T
    xt_ref[0, width:, :] = jnp.ones((ONES, length), BF16)


def gather_known(scalars, flags, x):
    cells, length, width = x.shape
    padded = -(-length // CHUNK) * CHUNK
    one = lambda *shape: pl.BlockSpec((1,) + shape, lambda i, s: (i, 0, 0))
    return pl.pallas_call(
        gather_kernel,
        out_shape=(
            jax.ShapeDtypeStruct((cells, padded, width), BF16),
            jax.ShapeDtypeStruct((cells, width + ONES, length), BF16),
            jax.ShapeDtypeStruct((cells, 1, length), jnp.int32),
        ),
        grid_spec=pltpu.PrefetchScalarGridSpec(
            num_scalar_prefetch=1,
            grid=(cells,),
            in_specs=[one(1, length), one(length, width)],
            out_specs=[one(padded, width), one(width + ONES, length), one(1, length)],
        ),
        compiler_params=params(),
        cost_estimate=cost(cells * 2e9, cells * 6e6),
        name="gather_known",
    )(scalars, flags, x)


def as_column(row):
    return jnp.broadcast_to(row, (LANES, LANES)).T[:, 0:1]


def attend_kernel(*refs, held, cells):
    scalars_ref, refs = refs[0], refs[1:]
    pieces, refs = refs[: len(held)], refs[len(held) :]
    (
        xt_ref, xc_ref, pos_ref,
        w_ref, vec_ref, qkv_ref, kct_ref, vc_ref, e_ref, more_ref, top_ref, ot_ref, o_ref, lse_ref,
        bias, qz, vct, top, acc, fast, spill,
    ) = refs
    cell, pair = pl.program_id(0), pl.program_id(1)
    known = scalars_ref[cell]
    me = scalars_ref[cells]
    width, length = w_ref.shape[0], xt_ref.shape[2]
    pairs = width // LANES
    block = width // len(held)

    @pl.when((cell == 0) & (pair == 0))
    def _():
        for offset, piece in zip(held, pieces):
            owner = me ^ offset
            rows = pl.ds(pl.multiple_of(owner * block, block), block)
            for which in range(3):
                for p in range(pairs):
                    col = p * TRIPLE + which * LANES
                    w_ref[rows, col : col + LANES] = piece[
                        which * block : (which + 1) * block, p * LANES : (p + 1) * LANES
                    ]
            vec_ref[:, rows] = piece[3 * block :, 0:block].astype(F32)
        for p in range(pairs):
            cols = slice(p * LANES, (p + 1) * LANES)
            bias[p, :, 0:1] = as_column(vec_ref[0:1, cols])
            bias[p, :, 1:2] = as_column(vec_ref[1:2, cols])

    weights = w_ref[:, pl.ds(pl.multiple_of(pair * TRIPLE, LANES), TRIPLE)]
    hidden = pos_ref[0] < 0
    turned = dot(weights, xt_ref[0, 0:width, :], 0, 0)
    queries = (turned[0:LANES, :] + bias[pair, :, 0:1]).astype(BF16)
    keys = turned[LANES : 2 * LANES, :].astype(BF16)
    values = (turned[2 * LANES :, :] + bias[pair, :, 1:2]).astype(BF16)
    qkv_ref[0, 0, 0:LANES, :] = queries
    qkv_ref[0, 0, LANES : 2 * LANES, :] = keys
    qkv_ref[0, 0, 2 * LANES :, :] = values
    low = lax.broadcasted_iota(jnp.int32, (LANES, length), 0) < HD
    scaled = queries.astype(F32) * SCALE
    qz[0] = jnp.where(low, scaled, 0.0).astype(BF16)
    qz[1] = jnp.where(low, 0.0, scaled).astype(BF16)
    keys = keys.astype(F32)
    values = values.astype(F32)
    for side in range(2):
        rows = slice(side * HD, (side + 1) * HD)
        q, k = scaled[rows, :], keys[rows, :]
        own = jnp.sum(q * k, axis=0, keepdims=True)
        longest_q = jnp.max(jnp.sum(q * q, axis=0, keepdims=True))
        longest_k = jnp.max(jnp.sum(k * k, axis=0, keepdims=True))
        safe = longest_q * longest_k < SAFE_SCORE * SAFE_SCORE
        fast[side] = safe.astype(jnp.int32)
        top[side] = jnp.where(safe, 0.0, jnp.where(hidden, own, MASK_FILL))
        weight = jnp.exp(jnp.where(safe, own, 0.0))
        weight = jnp.where(hidden, weight, 0.0).astype(BF16).astype(F32)
        acc[side, 0:HD, :] = weight * values[rows, :]
        acc[side, HD:, :] = jnp.broadcast_to(weight, (EXTRA, length))
    both = (fast[0] + fast[1]) == 2
    value_bias = vec_ref[1:2, pl.ds(pl.multiple_of(pair * LANES, LANES), LANES)]

    def one_chunk(chunk, exps):
        rows = pl.ds(pl.multiple_of(chunk * CHUNK, 16), CHUNK)
        packed = dot(xc_ref[0, rows, :], weights[:, LANES:])
        keys = packed[:, 0:LANES]
        values = packed[:, LANES:] + value_bias
        row = chunk * CHUNK + lax.broadcasted_iota(jnp.int32, (CHUNK, LANES), 0)
        valid = row < known
        kct_ref[0, 0, chunk] = jnp.where(valid, keys, 0.0).T.astype(BF16)
        values_t = jnp.where(valid, values, 0.0).T.astype(BF16)
        keys = keys.astype(BF16)
        vc_ref[0, 0, rows, :] = values.astype(BF16)
        row = chunk * CHUNK + lax.broadcasted_iota(jnp.int32, (EXTRA, CHUNK), 1)
        counted = jnp.where(row < known, 1.0, 0.0).astype(BF16)
        for side in range(2):
            vct[side, 0:HD, :] = values_t[side * HD : (side + 1) * HD, :]
            vct[side, HD:, :] = counted

        @pl.when(both)
        def _():
            for side in range(2):
                probs = jnp.exp(dot(keys, qz[side])).astype(BF16)
                exps[side] = probs
                acc[side] += dot(vct[side], probs)
                top_ref[0, 0, chunk, side] = top[side]

        @pl.when(jnp.logical_not(both))
        def _():
            for side in range(2):
                scores = dot(keys, qz[side])
                peak = jnp.maximum(top[side], jnp.max(scores, axis=0, keepdims=True))
                probs = jnp.exp(scores - peak).astype(BF16)
                exps[side] = probs
                acc[side] = acc[side] * jnp.exp(top[side] - peak) + dot(vct[side], probs)
                top[side] = peak
                top_ref[0, 0, chunk, side] = peak

    @pl.when(known > 0)
    def _():
        one_chunk(0, e_ref.at[0, 0])

    def later_chunk(chunk, carry):
        one_chunk(chunk, spill)
        pltpu.sync_copy(spill, more_ref.at[cell, pair, chunk - 1])
        return carry

    lax.fori_loop(1, (known + CHUNK - 1) // CHUNK, later_chunk, 0)

    for side in range(2):
        total = acc[side, HD : HD + 1, :]
        ot_ref[0, side * HD : (side + 1) * HD, :] = (acc[side, 0:HD, :] / total).astype(BF16)
        lse_ref[0, side] = top[side] + jnp.log(total)
    o_ref[0] = ot_ref[0].T


def attend(scalars, held, pieces, xt, xc, pos):
    cells, length = xt.shape[0], xt.shape[2]
    width = xt.shape[1] - ONES
    padded = xc.shape[1]
    pairs = width // LANES
    chunks = padded // CHUNK
    full = lambda *shape: pl.BlockSpec(shape, lambda c, p, s: (0,) * len(shape))
    shape = jax.ShapeDtypeStruct
    return pl.pallas_call(
        functools.partial(attend_kernel, held=held, cells=cells),
        out_shape=(
            shape((width, 3 * width), BF16),
            shape((EXTRA, width), F32),
            shape((cells, pairs, TRIPLE, length), BF16),
            shape((cells, pairs, chunks, LANES, CHUNK), BF16),
            shape((cells, pairs, padded, LANES), BF16),
            shape((cells, pairs, 2, CHUNK, length), BF16),
            shape((cells, pairs, max(chunks - 1, 1), 2, CHUNK, length), BF16),
            shape((cells, pairs, chunks, 2, 1, length), F32),
            shape((cells, width, length), BF16),
            shape((cells, length, width), BF16),
            shape((cells, H, 1, length), F32),
        ),
        grid_spec=pltpu.PrefetchScalarGridSpec(
            num_scalar_prefetch=1,
            grid=(cells, pairs),
            in_specs=[full(*piece.shape) for piece in pieces]
            + [
                pl.BlockSpec((1, width + ONES, length), lambda c, p, s: (c, 0, 0)),
                pl.BlockSpec((1, padded, width), lambda c, p, s: (c, 0, 0)),
                pl.BlockSpec((1, 1, length), lambda c, p, s: (c, 0, 0)),
            ],
            out_specs=[
                full(width, 3 * width),
                full(EXTRA, width),
                pl.BlockSpec((1, 1, TRIPLE, length), lambda c, p, s: (c, p, 0, 0)),
                pl.BlockSpec((1, 1, chunks, LANES, CHUNK), lambda c, p, s: (c, p, 0, 0, 0)),
                pl.BlockSpec((1, 1, padded, LANES), lambda c, p, s: (c, p, 0, 0)),
                pl.BlockSpec((1, 1, 2, CHUNK, length), lambda c, p, s: (c, p, 0, 0, 0)),
                pl.BlockSpec(memory_space=pl.ANY),
                pl.BlockSpec((1, 1, chunks, 2, 1, length), lambda c, p, s: (c, p, 0, 0, 0, 0)),
                pl.BlockSpec((1, LANES, length), lambda c, p, s: (c, p, 0)),
                pl.BlockSpec((1, length, LANES), lambda c, p, s: (c, 0, p)),
                pl.BlockSpec((1, 2, 1, length), lambda c, p, s: (c, p, 0, 0)),
            ],
            scratch_shapes=[
                pltpu.VMEM((pairs, LANES, 8), F32),
                pltpu.VMEM((2, LANES, length), BF16),
                pltpu.VMEM((2, HD + EXTRA, CHUNK), BF16),
                pltpu.VMEM((2, 1, length), F32),
                pltpu.VMEM((2, HD + EXTRA, length), F32),
                pltpu.SMEM((2,), jnp.int32),
                pltpu.VMEM((2, CHUNK, length), BF16),
            ],
        ),
        compiler_params=params(),
        cost_estimate=cost(cells * 1e10, cells * 2.5e7),
        name="attend",
    )(scalars, *pieces, xt, xc, pos)


def row_mean(rows):
    return jnp.mean(rows, axis=-1, keepdims=True)


def normalize(rows):
    centred = rows - row_mean(rows)
    scale = lax.rsqrt(row_mean(centred * centred) + NORM_EPSILON)
    return centred * scale, scale


def norm_back(grad, normed, scale):
    return scale * (grad - row_mean(grad) - normed * row_mean(grad * normed))


def column_sum(rows):
    return jnp.sum(rows, axis=0, keepdims=True)


def middle_kernel(*refs, held, cells):
    scalars_ref, refs = refs[0], refs[1:]
    pieces, refs = refs[: len(held)], refs[len(held) :]
    (
        x_ref, o_ref, cot_ref, vec_ref,
        result_ref, dhid_ref, datt_ref, keep_ref, send_ref,
        w, go, gu, gd, gvec,
    ) = refs
    me = scalars_ref[cells]
    width = x_ref.shape[1]
    block = width // len(held)

    @pl.when(pl.program_id(0) == 0)
    def _():
        for offset, piece in zip(held, pieces):
            rows = pl.ds(pl.multiple_of((me ^ offset) * block, block), block)
            for which in range(3):
                w[which, rows, :] = piece[which * block : (which + 1) * block, :]
        go[...] = jnp.zeros_like(go)
        gu[...] = jnp.zeros_like(gu)
        gd[...] = jnp.zeros_like(gd)
        gvec[...] = jnp.zeros_like(gvec)

    out_bias, gain_one, shift_one, up_bias, down_bias, gain_two, shift_two = (
        vec_ref[2 + i : 3 + i, :] for i in range(MIDDLE_VECTORS)
    )
    attended = o_ref[...]
    first_in = x_ref[...].astype(F32) + (dot(attended, w[0]) + out_bias)
    norm_one, scale_one = normalize(first_in)
    first_norm = norm_one * gain_one + shift_one
    first_low = first_norm.astype(BF16)
    pre_act = dot(first_low, w[1]) + up_bias
    below = 0.5 * (1.0 + lax.erf(pre_act * (0.5**0.5)))
    activated = (pre_act * below).astype(BF16)
    slope = below + pre_act * (jnp.exp(-0.5 * pre_act * pre_act) * 0.3989422804014327)
    second_in = first_norm + (dot(activated, w[2]) + down_bias)
    norm_two, scale_two = normalize(second_in)
    result_ref[...] = (norm_two * gain_two + shift_two).astype(BF16)

    dy = cot_ref[...].astype(F32)
    d_second = norm_back(dy * gain_two, norm_two, scale_two)
    d_ff = d_second.astype(BF16)
    gd[...] += dot(activated, d_ff, 0, 0)
    d_pre = (dot(d_ff, w[2], 1, 1) * slope).astype(BF16)
    gu[...] += dot(first_low, d_pre, 0, 0)
    d_first = d_second + dot(d_pre, w[1], 1, 1)
    d_hidden = norm_back(d_first * gain_one, norm_one, scale_one)
    d_attn = d_hidden.astype(BF16)
    go[...] += dot(attended, d_attn, 0, 0)
    dhid_ref[...] = d_attn
    datt_ref[...] = dot(d_attn, w[0], 1, 1).astype(BF16)
    gvec[0:1, :] += column_sum(d_attn.astype(F32))
    gvec[1:2, :] += column_sum(d_first * norm_one)
    gvec[2:3, :] += column_sum(d_first)
    gvec[3:4, :] += column_sum(d_pre.astype(F32))
    gvec[4:5, :] += column_sum(d_ff.astype(F32))
    gvec[5:6, :] += column_sum(dy * norm_two)
    gvec[6:7, :] += column_sum(dy)

    @pl.when(pl.program_id(0) == pl.num_programs(0) - 1)
    def _():
        for offset in range(len(held)):
            target = (keep_ref, send_ref)[offset % 2].at[offset // 2]
            rows = pl.ds(pl.multiple_of((me ^ offset) * block, block), block)
            for which, grad in enumerate((go, gu, gd)):
                cols = slice(which * width, (which + 1) * width)
                target[0:block, cols] = grad[rows, :].astype(BF16)
            target[block:, :] = jnp.zeros((EXTRA, 3 * width), BF16)
            target[block:, 0:block] = gvec[:, rows].astype(BF16)


def middle(scalars, held, pieces, x, o, cot, vec, cells):
    rows, width = x.shape
    step = ROWS if rows % ROWS == 0 else rows
    block = pl.BlockSpec((step, width), lambda i, s: (i, 0))
    full = lambda *shape: pl.BlockSpec(shape, lambda i, s: (0,) * len(shape))
    low = jax.ShapeDtypeStruct((rows, width), BF16)
    half = (len(held) // 2, width // len(held) + EXTRA, 3 * width)
    return pl.pallas_call(
        functools.partial(middle_kernel, held=held, cells=cells),
        out_shape=(low, low, low, jax.ShapeDtypeStruct(half, BF16), jax.ShapeDtypeStruct(half, BF16)),
        grid_spec=pltpu.PrefetchScalarGridSpec(
            num_scalar_prefetch=1,
            grid=(rows // step,),
            in_specs=[full(*piece.shape) for piece in pieces] + [block, block, block, full(EXTRA, width)],
            out_specs=[block, block, block, full(*half), full(*half)],
            scratch_shapes=[
                pltpu.VMEM((3, width, width), BF16),
                pltpu.VMEM((width, width), F32),
                pltpu.VMEM((width, width), F32),
                pltpu.VMEM((width, width), F32),
                pltpu.VMEM((EXTRA, width), F32),
            ],
        ),
        compiler_params=params(),
        cost_estimate=cost(rows * 5e6, rows * 8e3),
        name="middle",
    )(scalars, *pieces, x, o, cot, vec)


def back_kernel(
    scalars_ref, pos_ref, xt_ref, qkv_ref, kct_ref, vc_ref, e_ref, more_ref, top_ref, ot_ref, lse_ref,
    datt_ref,
    dt_ref, keep_ref, send_ref,
    hot, qz, og, dqa, dkv, delta, grad, spill,
    *, shards, cells, first_pair,
):
    pair, cell = pl.program_id(0), pl.program_id(1)
    known = scalars_ref[cell]
    me = scalars_ref[cells]
    width, length = xt_ref.shape[1] - ONES, xt_ref.shape[2]
    block = width // shards
    steps = (known + CHUNK - 1) // CHUNK
    place = pos_ref[0]
    hidden = place < 0

    @pl.when(pair == 0)
    def _():
        def mark(chunk, carry):
            row = chunk * CHUNK + lax.broadcasted_iota(jnp.int32, (CHUNK, length), 0)
            hot[cell, chunk] = jnp.where(place == row, 1.0, 0.0).astype(BF16)
            return carry

        lax.fori_loop(0, steps, mark, 0)

    low = lax.broadcasted_iota(jnp.int32, (LANES, length), 0) < HD
    queries = qkv_ref[0, 0, 0:LANES, :].astype(F32) * SCALE
    qz[0] = jnp.where(low, queries, 0.0).astype(BF16)
    qz[1] = jnp.where(low, 0.0, queries).astype(BF16)
    turned = datt_ref[0].T
    og[...] = turned
    turned = turned.astype(F32)
    for side in range(2):
        rows = slice(side * HD, (side + 1) * HD)
        query, grads = queries[rows, :], turned[rows, :]
        key = qkv_ref[0, 0, LANES + side * HD : LANES + (side + 1) * HD, :].astype(F32)
        value = qkv_ref[0, 0, 2 * LANES + side * HD : 2 * LANES + (side + 1) * HD, :].astype(F32)
        delta_row = jnp.sum(grads * ot_ref[0, rows, :].astype(F32), axis=0, keepdims=True)
        delta[side] = delta_row
        own = jnp.sum(query * key, axis=0, keepdims=True)
        prob = jnp.exp(jnp.where(hidden, own, MASK_FILL) - lse_ref[0, side])
        own_grad = jnp.sum(grads * value, axis=0, keepdims=True)
        back = (prob * (own_grad - delta_row)).astype(BF16).astype(F32)
        dqa[rows, :] = back * key
        dkv[rows, :] = back * query
        dkv[LANES + side * HD : LANES + (side + 1) * HD, :] = prob.astype(BF16).astype(F32) * grads

    def one_chunk(chunk, exps):
        values = vc_ref[0, 0, pl.ds(pl.multiple_of(chunk * CHUNK, 16), CHUNK), :]
        d_keys = jnp.zeros((CHUNK, LANES), F32)
        d_values = jnp.zeros((CHUNK, LANES), F32)
        for side in range(2):
            rows = slice(side * HD, (side + 1) * HD)
            share = jnp.exp(top_ref[0, 0, chunk, side] - lse_ref[0, side])
            mine = low if side == 0 else jnp.logical_not(low)
            oz = jnp.where(mine, og[...].astype(F32) * share, 0.0).astype(BF16)
            probs = exps[side]
            d_scores = (probs.astype(F32) * (dot(values, oz) - delta[side] * share)).astype(BF16)
            d_values += dot(probs, oz, 1, 1)
            d_keys += dot(d_scores, qz[side], 1, 1)
            dqa[rows, :] += dot(kct_ref[0, 0, chunk, rows, :], d_scores)
        joined = jnp.concatenate([d_keys, d_values], axis=1).astype(BF16)
        dkv[...] += dot(joined, hot[cell, chunk], 0, 0)

    @pl.when(known > 0)
    def _():
        one_chunk(0, e_ref.at[0, 0])

    def later_chunk(chunk, carry):
        pltpu.sync_copy(more_ref.at[cell, first_pair + pair, chunk - 1], spill)
        one_chunk(chunk, spill)
        return carry

    lax.fori_loop(1, steps, later_chunk, 0)

    dt_ref[0, 0, 0:LANES, :] = (dqa[...] * SCALE).astype(BF16)
    dt_ref[0, 0, LANES:, :] = dkv[...].astype(BF16)
    term = dot(xt_ref[0], dt_ref[0, 0], 1, 1)

    @pl.when(cell == 0)
    def _():
        grad[...] = term

    @pl.when(cell > 0)
    def _():
        grad[...] += term

    @pl.when(cell == cells - 1)
    def _():
        for offset in range(shards):
            owner = me ^ offset
            target = (keep_ref, send_ref)[offset % 2].at[0, offset // 2]
            rows = pl.ds(pl.multiple_of(owner * block, block), block)
            target[0:block, :] = grad[rows, :].astype(BF16)
            ours = jnp.where(owner == first_pair + pair, 1.0, 0.0)
            target[block:, :] = (grad[width:, :] * ours).astype(BF16)


def attend_back(group, shards, scalars, pos, xt, qkv, kct, vc, e, more, top, ot, lse, datt):
    first, count = group
    cells, length = xt.shape[0], xt.shape[2]
    width = xt.shape[1] - ONES
    padded = vc.shape[2]
    chunks = padded // CHUNK
    half = (count, shards // 2, width // shards + EXTRA, TRIPLE)
    part = pl.BlockSpec((1,) + half[1:], lambda p, c, s: (p, 0, 0, 0))
    shape = jax.ShapeDtypeStruct
    return pl.pallas_call(
        functools.partial(back_kernel, shards=shards, cells=cells, first_pair=first),
        out_shape=(shape((cells, count, TRIPLE, length), BF16), shape(half, BF16), shape(half, BF16)),
        grid_spec=pltpu.PrefetchScalarGridSpec(
            num_scalar_prefetch=1,
            grid=(count, cells),
            in_specs=[
                pl.BlockSpec((1, 1, length), lambda p, c, s: (c, 0, 0)),
                pl.BlockSpec((1, width + ONES, length), lambda p, c, s: (c, 0, 0)),
                pl.BlockSpec((1, 1, TRIPLE, length), lambda p, c, s: (c, first + p, 0, 0)),
                pl.BlockSpec((1, 1, chunks, LANES, CHUNK), lambda p, c, s: (c, first + p, 0, 0, 0)),
                pl.BlockSpec((1, 1, padded, LANES), lambda p, c, s: (c, first + p, 0, 0)),
                pl.BlockSpec((1, 1, 2, CHUNK, length), lambda p, c, s: (c, first + p, 0, 0, 0)),
                pl.BlockSpec(memory_space=pl.ANY),
                pl.BlockSpec((1, 1, chunks, 2, 1, length), lambda p, c, s: (c, first + p, 0, 0, 0, 0)),
                pl.BlockSpec((1, LANES, length), lambda p, c, s: (c, first + p, 0)),
                pl.BlockSpec((1, 2, 1, length), lambda p, c, s: (c, first + p, 0, 0)),
                pl.BlockSpec((1, length, LANES), lambda p, c, s: (c, 0, first + p)),
            ],
            out_specs=[
                pl.BlockSpec((1, 1, TRIPLE, length), lambda p, c, s: (c, p, 0, 0)),
                part,
                part,
            ],
            scratch_shapes=[
                pltpu.VMEM((cells, chunks, CHUNK, length), BF16),
                pltpu.VMEM((2, LANES, length), BF16),
                pltpu.VMEM((LANES, length), BF16),
                pltpu.VMEM((LANES, length), F32),
                pltpu.VMEM((2 * LANES, length), F32),
                pltpu.VMEM((2, 1, length), F32),
                pltpu.VMEM((width + ONES, TRIPLE), F32),
                pltpu.VMEM((2, CHUNK, length), BF16),
            ],
        ),
        compiler_params=params(),
        cost_estimate=cost(cells * count * 6e9, cells * count * 7e6),
        name="attend_back",
    )(scalars, pos, xt, qkv, kct, vc, e, more, top, ot, lse, datt)


def input_kernel(w_ref, dhid_ref, *refs):
    parts, out_ref = refs[:-1], refs[-1]
    back, col = None, 0
    for part in parts:
        rows = part.shape[1]
        term = dot(w_ref[:, col : col + rows], part[0])
        back = term if back is None else back + term
        col += rows
    out_ref[0] = (back.T + dhid_ref[0].astype(F32)).astype(BF16)


def input_grad(w, dhid, parts):
    cells, length, width = dhid.shape
    parts = [part.reshape(cells, -1, length) for part in parts]
    block = pl.BlockSpec((1, length, width), lambda i: (i, 0, 0))
    return pl.pallas_call(
        input_kernel,
        out_shape=jax.ShapeDtypeStruct(dhid.shape, BF16),
        grid=(cells,),
        in_specs=[pl.BlockSpec(w.shape, lambda i: (0, 0)), block]
        + [pl.BlockSpec((1,) + part.shape[1:], lambda i: (i, 0, 0)) for part in parts],
        out_specs=block,
        compiler_params=params(),
        cost_estimate=cost(cells * 2e9, cells * 8e6),
        name="input_grad",
    )(w, dhid, *parts)


def swap(values, axis, mask):
    size = lax.axis_size(axis)
    return lax.ppermute(values, axis, [(i, i ^ mask) for i in range(size)])


def masks(axis):
    found, mask = [], 1
    while mask < lax.axis_size(axis):
        found.append(mask)
        mask *= 2
    return found


def gather_pieces(own):
    held = [own]
    for mask in reversed(masks("fsdp")):
        held = held + [swap(piece, "fsdp", mask) for piece in held]
    return held


def plus(left, right):
    return left.astype(F32) + right.astype(F32)


def reduce_parts(keep, send, dim):
    for mask in masks("fsdp"):
        if mask > 1:
            keep, send = (lax.slice_in_dim(total, i, total.shape[dim], 2, dim) for i in (0, 1))
        total = plus(keep, swap(send, "fsdp", mask)).astype(BF16)
    total = jnp.squeeze(total, dim)
    for mask in masks("dp"):
        total = plus(total.astype(BF16), swap(total.astype(BF16), "dp", mask))
    return total.astype(F32)


def body(*args):
    tokens, known_flags, cotangent = args[0], args[1], args[17]
    cells, length, width = tokens.shape
    shards = lax.axis_size("fsdp")
    block = width // shards
    held = offsets(shards)

    vectors = jnp.stack([args[i] for i in VECTORS])
    vectors = jnp.pad(vectors, ((0, EXTRA - len(VECTORS)), (0, width - block)))
    early = gather_pieces(jnp.concatenate([args[i] for i in SQUARES[:3]] + [vectors]))
    own = jnp.concatenate([args[i] for i in SQUARES[3:]])
    late = [own] + [swap(own, "fsdp", offset) for offset in held[1:]]

    known = jnp.sum((known_flags > 0).astype(jnp.int32), axis=1)
    scalars = jnp.concatenate([known, lax.axis_index("fsdp").astype(jnp.int32)[None]])
    xc, xt, pos = gather_known(scalars, known_flags.reshape(cells, 1, length), tokens)
    w, vec, qkv, kct, vc, e, more, top, ot, o, lse = attend(scalars, held, early, xt, xc, pos)
    flat = lambda a: a.reshape(cells * length, width)
    result, dhid, datt, keep, send = middle(
        scalars, held, late, flat(tokens), flat(o), flat(cotangent), vec, cells
    )
    middle_grads = reduce_parts(keep, send, 0)
    cube = lambda a: a.reshape(cells, length, width)
    parts, pair_grads = [], []
    for group in GROUPS:
        dt, keep, send = attend_back(
            group, shards, scalars, pos, xt, qkv, kct, vc, e, more, top, ot, lse, cube(datt)
        )
        parts.append(dt)
        pair_grads.append(reduce_parts(keep, send, 1))
    tokens_grad = input_grad(w, cube(dhid), parts)

    pair_grads = jnp.concatenate(pair_grads)
    pick = lambda which: pair_grads[:, :, which * LANES : (which + 1) * LANES]
    out = {}
    for which, i in enumerate(SQUARES[:3]):
        out[i] = pick(which)[:, 0:block].transpose(1, 0, 2).reshape(block, width)
        out[i + 1] = jnp.sum(pick(which)[:, block], axis=0)
    for which, i in enumerate(SQUARES[3:]):
        out[i] = middle_grads[0:block, which * width : (which + 1) * width]
    out[6] = jnp.sum(pick(2)[:, block], axis=0)
    out[4] = pick(1)[:, 0:block].transpose(1, 0, 2).reshape(block, width)
    out[5] = pick(2)[:, 0:block].transpose(1, 0, 2).reshape(block, width)
    for row, i in enumerate(VECTORS[2:]):
        out[i] = middle_grads[block + row, 0:block]
    return (cube(result), tokens_grad) + tuple(out[i] for i in range(2, 17))


def solution(mesh):
    cells = P(("dp", "fsdp"), None, None)
    specs = tuple(P("fsdp", None) if i in SQUARES else P("fsdp") for i in range(2, 17))
    return jax.shard_map(
        body,
        mesh=mesh,
        in_specs=(cells, P(("dp", "fsdp"), None)) + specs + (cells,),
        out_specs=(cells, cells) + specs,
        check_vma=False,
    )
```

time: 530 us -> 246 us (0.46)
  waiting for transfers between devices: 223 us -> 49.8 us
  blocking collectives: 130 us -> 0 us
  starting transfers between devices: 0.27 us -> 43 us
  between operations: 15 us -> 1.27 us
  Pallas kernels: 145 us -> 132 us
    reduce_scatter x6 -> x0, waiting for transfers between devices: 159 us -> none  [body(): lax.psum_scatter(g, 'fsdp', scatter_dimension=0, tiled=True)]
    all_gather x15 -> x0, blocking collectives: 96.5 us -> none  [body(): lax.all_gather(args[i], 'fsdp', axis=0, tiled=True)]
    psum x1 -> x0, waiting for transfers between devices: 60.3 us -> none  [body(): lax.psum(lax.psum_scatter(g, 'fsdp', scatter_dimension=0, tiled=True), 'dp')]
    ppermute x0 -> x21, waiting for transfers between devices: none -> 49.8 us  [swap(): return lax.ppermute(values, axis, [(i, i ^ mask) for i in range(size)])]
    ppermute x0 -> x21, starting transfers between devices: none -> 43 us  [swap(): return lax.ppermute(values, axis, [(i, i ^ mask) for i in range(size)])]
    psum x1 -> x0, blocking collectives: 22.8 us -> none  [body(): lax.psum(lax.psum_scatter(g, 'fsdp', scatter_dimension=0, tiled=True), 'dp')]
    pallas_call x3 -> x5, Pallas kernels: 137 us -> 125 us  [the longest x2 55.8 us: attend_back(): pl.pallas_call(functools.partial(back_kernel, shards=shards, cells=cells,...]
    unnamed x1 -> x0, blocking collectives: 10.2 us -> none
  transfers between devices with their start and end apart: 7 -> 21, of which waited for: 7 -> 7; matrix products, arithmetic and copies ran while one was open for 0% -> 5% of each run, Pallas kernels for 0% -> 32%
where the time goes in v2:
time: 246 us; the launch traced here: 243 us
  Pallas kernels  132 us (54%)
  waiting for transfers between devices  49.8 us (20%)
  starting transfers between devices  43 us (17%)
  local copies, waits for them, and re-layouts  12.9 us (5%)
  other arithmetic  4.43 us (2%)
    pallas_call x2, Pallas kernels, attend_back(): pl.pallas_call(functools.partial(back_kernel, shards=shards, cells=cells,...  55.8 us
    ppermute x21, waiting for transfers between devices, swap(): return lax.ppermute(values, axis, [(i, i ^ mask) for i in range(size)])  49.8 us
    ppermute x21, starting transfers between devices, swap(): return lax.ppermute(values, axis, [(i, i ^ mask) for i in range(size)])  43 us
    pallas_call x1, Pallas kernels, attend(): pl.pallas_call(functools.partial(attend_kernel, held=held, cells=cells),...  33.6 us
    pallas_call x1, Pallas kernels, middle(): pl.pallas_call(functools.partial(middle_kernel, held=held, cells=cells),...  25.9 us
    pallas_call x1, Pallas kernels, input_grad(): pl.pallas_call(input_kernel, out_shape=jax.ShapeDtypeStruct(dhid.shape, B...  9.71 us
    pallas_call x1, Pallas kernels, gather_known(): pl.pallas_call(gather_kernel, out_shape=(jax.ShapeDtypeStruct((cells, pad...  7.19 us
    unnamed x29, local copies, waits for them, and re-layouts  6.25 us
  transfers between devices with their start and end apart: 21, of which 7 were waited for; matrix products, arithmetic and copies ran while one was open for 5% of the time, Pallas kernels for 32%

profile of v2, /device:TPU:0, one launch (start us, length us, event | category | flops | bytes accessed | tf_op | source)
XLA Modules:
  0.0 243.4 jit_solution(13068067578545895040)
XLA Ops:
  0.7 1.5 stack.39
  2.1 1.1 fusion.2.refs_1_
  3.2 3.0 %collective-permute-start.3 = (bf16[400,512]{1,0:T(8,128)(2,1)S(1)}, bf16[400,512]{1,0:T(8,128)(2,1)S(1)}, u32[]{:S(2)}, u32[]{:S(2)}) collective-permute-start(bf16[400,512]{1,0:T(8,128)(2,1)S(1)} %fusion.2.refs_1_), channel_id=1, source_target_pairs={{0,2},{1,3},{2,0},{3,1},{4,6},{5,7},{6,4},{7,5},{8,10},{9,11},{10,... | collective-permute-start | bytes 1228808 | tf_op jit(solution)/shard_map/ppermute | solution.py:582
  6.2 0.9 constant_dynamic-update-slice_fusion.2
  7.1 0.9 constant_dynamic-update-slice_fusion.1
  8.1 0.9 constant_dynamic-update-slice_fusion.refs_1_
  9.6 1.6 collective-permute-start.2
  12.0 4.5 %collective-permute-done.3.refs_2_ = bf16[400,512]{1,0:T(8,128)(2,1)S(1)} collective-permute-done((bf16[400,512]{1,0:T(8,128)(2,1)S(1)}, bf16[400,512]{1,0:T(8,128)(2,1)S(1)}, u32[]{:S(2)}, u32[]{:S(2)}) %collective-permute-start.3) | collective-permute-done | bytes 409632 | tf_op jit(solution)/shard_map/ppermute | solution.py:582
  17.2 1.3 reshape.72.flags_ref
  18.5 7.2 %gather_known.1 = (bf16[2,1344,512]{2,1,0:T(8,128)(2,1)}, bf16[2,528,1200]{2,1,0:T(8,128)(2,1)}, s32[2,1,1200]{2,1,0:T(1,128)}) custom-call(s32[3]{0:T(128)} %pad_add_fusion.scalars_ref.refs_0_, s32[2,1,1200]{2,1,0:T(1,128)} %reshape.72.flags_ref, bf16[2,1200,512]{2,1,0:T(8,128)(2,1)} %x_ref.1), custom_call_target="tpu_custom_call" | custom-call | flops 4000000000 | bytes 12000000 | tf_op jit(solution)/shard_map/gather_known/pallas_call | solution.py:85
  26.6 33.6 %attend.1 = (bf16[512,1536]{1,0:T(8,128)(2,1)}, f32[16,512]{1,0:T(8,128)}, bf16[2,4,384,1200]{3,2,1,0:T(8,128)(2,1)}, bf16[2,4,2,128,672]{4,3,2,1,0:T(8,128)(2,1...) custom-call(s32[3]{0:T(128)} %pad_add_fusion.scalars_ref.refs_0_, ...), custom_call_target="tpu_custom_call" | custom-call | flops 20000000000 | bytes 50000000 | tf_op jit(solution)/shard_map/attend/pallas_call | solution.py:233
  61.2 25.9 %middle.1 = (bf16[2400,512]{1,0:T(8,128)(2,1)}, bf16[2400,512]{1,0:T(8,128)(2,1)}, bf16[2400,512]{1,0:T(8,128)(2,1)}, bf16[2,144,1536]{2,1,0:T(8,128)(2,1)}, bf16[2,144,1536]{2,1,0:T(8,128)(2,1)}) custom-call(s32[3]{0:T(128)} %pad_add_fusion.scalars_ref.refs_0_, bf16[384,512]{1,0:T(8,128)(2,1)} %copy-done.4, bf16[384,512]{1,0:T(8,128)(2,1)} %copy-done.9, ...), custom_call_target="tpu_custom_call" | custom-call | flops 12000000000 | bytes 19200000 | tf_op jit(solution)/shard_map/middle/pallas_call | solution.py:382
  87.1 27.8 %attend_back.3 = (bf16[2,2,384,1200]{3,2,1,0:T(8,128)(2,1)}, bf16[2,2,144,384]{3,2,1,0:T(8,128)(2,1)}, bf16[2,2,144,384]{3,2,1,0:T(8,128)(2,1)}) custom-call(s32[3]{0:T(128)} %pad_add_fusion.scalars_ref.refs_0_, s32[2,1,1200]{2,1,0:T(1,128)} %get-tuple-element.44.refs_7_.pos_ref, bf16[2,528,1200]{2,1,0:T(8,128)(2,1)} %get-tuple-element.42.refs_5_.xt_ref, ...), custom_call_target="tpu_custom_call" | custom-call | flops 24000000000 | bytes 28000000 | tf_op jit(solution)/shard_map/attend_back/pallas_call | solution.py:511
  115.4 28.0 %attend_back.2 = (bf16[2,2,384,1200]{3,2,1,0:T(8,128)(2,1)}, bf16[2,2,144,384]{3,2,1,0:T(8,128)(2,1)}, bf16[2,2,144,384]{3,2,1,0:T(8,128)(2,1)}) custom-call(s32[3]{0:T(128)} %pad_add_fusion.scalars_ref.refs_0_, s32[2,1,1200]{2,1,0:T(1,128)} %get-tuple-element.44.refs_7_.pos_ref, bf16[2,528,1200]{2,1,0:T(8,128)(2,1)} %get-tuple-element.42.refs_5_.xt_ref, ...), custom_call_target="tpu_custom_call" | custom-call | flops 24000000000 | bytes 28000000 | tf_op jit(solution)/shard_map/attend_back/pallas_call | solution.py:511
  143.7 1.1 copy.38
  145.1 9.7 %input_grad.1 = bf16[2,1200,512]{2,1,0:T(8,128)(2,1)} custom-call(bf16[512,1536]{1,0:T(8,128)(2,1)} %get-tuple-element.48.w_ref, bf16[2,1200,512]{2,1,0:T(8,128)(2,1)} %bitcast.64, bf16[2,768,1200]{2,1,0:T(8,128)(2,1)} %bitcast.62, bf16[2,768,1200]{2,1,0:T(8,128)(2,1)} %bitcast.61), custom_call_target="tpu_custom_call" | custom-call | flops 4000000000 | bytes 16000000 | tf_op jit(solution)/shard_map/input_grad/pallas_call | solution.py:567
  155.0 7.2 %collective-permute-start.12 = (bf16[2,1,144,384]{3,2,1,0:T(8,128)(2,1)S(1)}, bf16[2,1,144,384]{3,2,1,0:T(8,128)(2,1)S(1)}, u32[]{:S(2)}, u32[]{:S(2)}) collective-permute-start(bf16[2,1,144,384]{3,2,1,0:T(8,128)(2,1)S(1)} %slice.103), channel_id=1, source_target_pairs={{0,2},{1,3},{2,0},{3,1},{4,6},{5,7},{6,4},{7,5},{8,10},{9,11},{10,... | collective-permute-start | bytes 663560 | tf_op jit(solution)/shard_map/ppermute | solution.py:582
  162.8 2.1 collective-permute-start.17
  164.8 3.6 %collective-permute-done.12 = bf16[2,1,144,384]{3,2,1,0:T(8,128)(2,1)S(1)} collective-permute-done((bf16[2,1,144,384]{3,2,1,0:T(8,128)(2,1)S(1)}, bf16[2,1,144,384]{3,2,1,0:T(8,128)(2,1)S(1)}, u32[]{:S(2)}, u32[]{:S(2)}) %collective-permute-start.12) | collective-permute-done | bytes 221216 | tf_op jit(solution)/shard_map/ppermute | solution.py:582
  168.5 7.5 %collective-permute-start.13 = (bf16[2,144,384]{2,1,0:T(8,128)(2,1)S(1)}, bf16[2,144,384]{2,1,0:T(8,128)(2,1)S(1)}, u32[]{:S(2)}, u32[]{:S(2)}) collective-permute-start(bf16[2,144,384]{2,1,0:T(8,128)(2,1)S(1)} %fusion.10), channel_id=1, source_target_pairs={{0,4},{4,0},{8,12},{12,8},{16,20},{20,16},{24,28},{28,24},{1,5},{5... | collective-permute-start | bytes 663560 | tf_op jit(solution)/shard_map/ppermute | solution.py:582
  176.0 4.7 %collective-permute-start.8 = (bf16[2,144,384]{2,1,0:T(8,128)(2,1)S(1)}, bf16[2,144,384]{2,1,0:T(8,128)(2,1)S(1)}, u32[]{:S(2)}, u32[]{:S(2)}) collective-permute-start(bf16[2,144,384]{2,1,0:T(8,128)(2,1)S(1)} %fusion.9), channel_id=1, source_target_pairs={{0,4},{4,0},{8,12},{12,8},{16,20},{20,16},{24,28},{28,24},{1,5},{5... | collective-permute-start | bytes 663560 | tf_op jit(solution)/shard_map/ppermute | solution.py:582
  180.7 1.7 collective-permute-done.17
  182.5 7.0 %collective-permute-start.18 = (bf16[144,1536]{1,0:T(8,128)(2,1)S(1)}, bf16[144,1536]{1,0:T(8,128)(2,1)S(1)}, u32[]{:S(2)}, u32[]{:S(2)}) collective-permute-start(bf16[144,1536]{1,0:T(8,128)(2,1)S(1)} %fusion.1), channel_id=1, source_target_pairs={{0,4},{4,0},{8,12},{12,8},{16,20},{20,16},{24,28},{28,24},{1,5},{5... | collective-permute-start | bytes 1327112 | tf_op jit(solution)/shard_map/ppermute | solution.py:582
  189.6 1.6 collective-permute-start.14
  191.8 7.4 %collective-permute-done.18 = bf16[144,1536]{1,0:T(8,128)(2,1)S(1)} collective-permute-done((bf16[144,1536]{1,0:T(8,128)(2,1)S(1)}, bf16[144,1536]{1,0:T(8,128)(2,1)S(1)}, u32[]{:S(2)}, u32[]{:S(2)}) %collective-permute-start.18) | collective-permute-done | bytes 442400 | tf_op jit(solution)/shard_map/ppermute | solution.py:582
  199.3 1.9 collective-permute-start.19
  201.3 2.5 %collective-permute-start.15 = (bf16[2,144,384]{2,1,0:T(8,128)(2,1)S(1)}, bf16[2,144,384]{2,1,0:T(8,128)(2,1)S(1)}, u32[]{:S(2)}, u32[]{:S(2)}) collective-permute-start(bf16[2,144,384]{2,1,0:T(8,128)(2,1)S(1)} %add_convert_fusion.6), channel_id=1, source_target_pairs={{0,16},{4,20},{8,24},{12,28},{16,0},{20,4},{24,8},{28,12},{1,17},{... | collective-permute-start | bytes 663560 | tf_op jit(solution)/shard_map/ppermute | solution.py:582
  204.4 15.0 %collective-permute-done.19 = bf16[144,1536]{1,0:T(8,128)(2,1)S(1)} collective-permute-done((bf16[144,1536]{1,0:T(8,128)(2,1)S(1)}, bf16[144,1536]{1,0:T(8,128)(2,1)S(1)}, u32[]{:S(2)}, u32[]{:S(2)}) %collective-permute-start.19) | collective-permute-done | bytes 442400 | tf_op jit(solution)/shard_map/ppermute | solution.py:582
  219.5 1.0 collective-permute-start.20
  220.5 11.9 %collective-permute-done.10 = bf16[2,144,384]{2,1,0:T(8,128)(2,1)S(1)} collective-permute-done((bf16[2,144,384]{2,1,0:T(8,128)(2,1)S(1)}, bf16[2,144,384]{2,1,0:T(8,128)(2,1)S(1)}, u32[]{:S(2)}, u32[]{:S(2)}) %collective-permute-start.10) | collective-permute-done | bytes 221216 | tf_op jit(solution)/shard_map/ppermute | solution.py:582
  236.0 5.6 %collective-permute-done.20 = bf16[144,1536]{1,0:T(8,128)(2,1)S(1)} collective-permute-done((bf16[144,1536]{1,0:T(8,128)(2,1)S(1)}, bf16[144,1536]{1,0:T(8,128)(2,1)S(1)}, u32[]{:S(2)}, u32[]{:S(2)}) %collective-permute-start.20) | collective-permute-done | bytes 442400 | tf_op jit(solution)/shard_map/ppermute | solution.py:582
  241.8 0.9 fusion.15
  (77 shorter events, 11.8 us)
Async XLA Ops:
  3.2 22.5 %copy-start.3 = (bf16[400,512]{1,0:T(8,128)(2,1)}, bf16[400,512]{1,0:T(8,128)(2,1)S(1)}, u32[]{:S(2)}) copy-start(bf16[400,512]{1,0:T(8,128)(2,1)S(1)} %fusion.2.refs_1_) | copy-start | bytes 1228804
  3.2 13.3 %collective-permute-start.3 = (bf16[400,512]{1,0:T(8,128)(2,1)S(1)}, bf16[400,512]{1,0:T(8,128)(2,1)S(1)}, u32[]{:S(2)}, u32[]{:S(2)}) collective-permute-start(bf16[400,512]{1,0:T(8,128)(2,1)S(1)} %fusion.2.refs_1_), channel_id=1, source_target_pairs={{0,2},{1,3},{2,0},{3,1},{4,6},{5,7},{6,4},{7,5},{8,10},{9,11},{10,... | collective-permute-start | bytes 1228808 | tf_op jit(solution)/shard_map/ppermute | solution.py:582
  6.2 19.5 %collective-permute-start.4 = (bf16[400,512]{1,0:T(8,128)(2,1)S(1)}, bf16[400,512]{1,0:T(8,128)(2,1)S(1)}, u32[]{:S(2)}, u32[]{:S(2)}) collective-permute-start(bf16[400,512]{1,0:T(8,128)(2,1)S(1)} %fusion.2.refs_1_), channel_id=1, source_target_pairs={{0,1},{1,0},{2,3},{3,2},{4,5},{5,4},{6,7},{7,6},{8,9},{9,8},{10,11... | collective-permute-start | bytes 1228808 | tf_op jit(solution)/shard_map/ppermute | solution.py:582
  9.0 16.7 %copy-start.4 = (bf16[384,512]{1,0:T(8,128)(2,1)}, bf16[384,512]{1,0:T(8,128)(2,1)S(1)}, u32[]{:S(2)}) copy-start(bf16[384,512]{1,0:T(8,128)(2,1)S(1)} %constant_dynamic-update-slice_fusion.refs_1_) | copy-start | bytes 1179652
  9.0 51.2 %collective-permute-start = (bf16[384,512]{1,0:T(8,128)(2,1)S(1)}, bf16[384,512]{1,0:T(8,128)(2,1)S(1)}, u32[]{:S(2)}, u32[]{:S(2)}) collective-permute-start(bf16[384,512]{1,0:T(8,128)(2,1)S(1)} %constant_dynamic-update-slice_fusion.refs_1_), channel_id=1, source_target_pairs={{0,2},{1,3},{2,0},{3,1},{4,6},{5,7},{6,4},{7,5},{8,10},{9,11},{10,... | collective-permute-start | bytes 1179656 | tf_op jit(solution)/shard_map/ppermute | solution.py:582
  9.2 51.0 %collective-permute-start.1 = (bf16[384,512]{1,0:T(8,128)(2,1)S(1)}, bf16[384,512]{1,0:T(8,128)(2,1)S(1)}, u32[]{:S(2)}, u32[]{:S(2)}) collective-permute-start(bf16[384,512]{1,0:T(8,128)(2,1)S(1)} %constant_dynamic-update-slice_fusion.refs_1_), channel_id=1, source_target_pairs={{0,1},{1,0},{2,3},{3,2},{4,5},{5,4},{6,7},{7,6},{8,9},{9,8},{10,11... | collective-permute-start | bytes 1179656 | tf_op jit(solution)/shard_map/ppermute | solution.py:582
  9.6 50.6 %collective-permute-start.2 = (bf16[384,512]{1,0:T(8,128)(2,1)S(1)}, bf16[384,512]{1,0:T(8,128)(2,1)S(1)}, u32[]{:S(2)}, u32[]{:S(2)}) collective-permute-start(bf16[384,512]{1,0:T(8,128)(2,1)S(1)} %constant_dynamic-update-slice_fusion.refs_1_), channel_id=1, source_target_pairs={{0,3},{1,2},{2,1},{3,0},{4,7},{5,6},{6,5},{7,4},{8,11},{9,10},{10,... | collective-permute-start | bytes 1179656 | tf_op jit(solution)/shard_map/ppermute | solution.py:582
  16.5 9.2 %copy-start.6 = (bf16[400,512]{1,0:T(8,128)(2,1)}, bf16[400,512]{1,0:T(8,128)(2,1)S(1)}, u32[]{:S(2)}) copy-start(bf16[400,512]{1,0:T(8,128)(2,1)S(1)} %collective-permute-done.3.refs_2_) | copy-start | bytes 1228804
  16.5 9.2 %collective-permute-start.5 = (bf16[400,512]{1,0:T(8,128)(2,1)S(1)}, bf16[400,512]{1,0:T(8,128)(2,1)S(1)}, u32[]{:S(2)}, u32[]{:S(2)}) collective-permute-start(bf16[400,512]{1,0:T(8,128)(2,1)S(1)} %collective-permute-done.3.refs_2_), channel_id=1, source_target_pairs={{0,1},{1,0},{2,3},{3,2},{4,5},{5,4},{6,7},{7,6},{8,9},{9,8},{10,11... | collective-permute-start | bytes 1228808 | tf_op jit(solution)/shard_map/ppermute | solution.py:582
  25.7 0.8 copy-start.7
  25.7 0.9 copy-start.8
  60.2 0.9 copy-start.10
  60.2 1.0 copy-start.11
  114.9 28.5 %copy-start.5 = (bf16[2,144,1536]{2,1,0:T(8,128)(2,1)S(1)}, bf16[2,144,1536]{2,1,0:T(8,128)(2,1)}, u32[]{:S(2)}) copy-start(bf16[2,144,1536]{2,1,0:T(8,128)(2,1)} %get-tuple-element.66) | copy-start | bytes 2654212
  114.9 39.9 %collective-permute-start.11 = (bf16[2,2,144,384]{3,2,1,0:T(8,128)(2,1)}, bf16[2,2,144,384]{3,2,1,0:T(8,128)(2,1)S(1)}, u32[]{:S(2)}, u32[]{:S(2)}) collective-permute-start(bf16[2,2,144,384]{3,2,1,0:T(8,128)(2,1)} %get-tuple-element.64), channel_id=1, source_target_pairs={{0,1},{1,0},{2,3},{3,2},{4,5},{5,4},{6,7},{7,6},{8,9},{9,8},{10,11... | collective-permute-start | bytes 1327112 | tf_op jit(solution)/shard_map/ppermute | solution.py:582
  143.4 19.1 %collective-permute-start.16 = (bf16[2,144,1536]{2,1,0:T(8,128)(2,1)S(1)}, bf16[2,144,1536]{2,1,0:T(8,128)(2,1)S(1)}, u32[]{:S(2)}, u32[]{:S(2)}) collective-permute-start(bf16[2,144,1536]{2,1,0:T(8,128)(2,1)S(1)} %copy-done.5), channel_id=1, source_target_pairs={{0,1},{1,0},{2,3},{3,2},{4,5},{5,4},{6,7},{7,6},{8,9},{9,8},{10,11... | collective-permute-start | bytes 2654216 | tf_op jit(solution)/shard_map/ppermute | solution.py:582
  144.8 17.5 %collective-permute-start.6 = (bf16[2,2,144,384]{3,2,0,1:T(8,128)(2,1)S(1)}, bf16[2,2,144,384]{3,2,0,1:T(8,128)(2,1)S(1)}, u32[]{:S(2)}, u32[]{:S(2)}) collective-permute-start(bf16[2,2,144,384]{3,2,0,1:T(8,128)(2,1)S(1)} %copy.38), channel_id=1, source_target_pairs={{0,1},{1,0},{2,3},{3,2},{4,5},{5,4},{6,7},{7,6},{8,9},{9,8},{10,11... | collective-permute-start | bytes 1327112 | tf_op jit(solution)/shard_map/ppermute | solution.py:582
  145.1 9.7 %copy-start.2 = (bf16[2,2,144,384]{3,2,1,0:T(8,128)(2,1)S(1)}, bf16[2,2,144,384]{3,2,1,0:T(8,128)(2,1)}, u32[]{:S(2)}) copy-start(bf16[2,2,144,384]{3,2,1,0:T(8,128)(2,1)} %get-tuple-element.63) | copy-start | bytes 1327108
  145.1 17.1 %copy-start.1 = (bf16[2,2,144,384]{3,2,1,0:T(8,128)(2,1)S(1)}, bf16[2,2,144,384]{3,2,1,0:T(8,128)(2,1)}, u32[]{:S(2)}) copy-start(bf16[2,2,144,384]{3,2,1,0:T(8,128)(2,1)} %get-tuple-element.61) | copy-start | bytes 1327108
  154.8 7.7 %copy-start = (bf16[2,144,1536]{2,1,0:T(8,128)(2,1)S(1)}, bf16[2,144,1536]{2,1,0:T(8,128)(2,1)}, u32[]{:S(2)}) copy-start(bf16[2,144,1536]{2,1,0:T(8,128)(2,1)} %get-tuple-element.65) | copy-start | bytes 2654212
  155.0 13.4 %collective-permute-start.12 = (bf16[2,1,144,384]{3,2,1,0:T(8,128)(2,1)S(1)}, bf16[2,1,144,384]{3,2,1,0:T(8,128)(2,1)S(1)}, u32[]{:S(2)}, u32[]{:S(2)}) collective-permute-start(bf16[2,1,144,384]{3,2,1,0:T(8,128)(2,1)S(1)} %slice.103), channel_id=1, source_target_pairs={{0,2},{1,3},{2,0},{3,1},{4,6},{5,7},{6,4},{7,5},{8,10},{9,11},{10,... | collective-permute-start | bytes 663560 | tf_op jit(solution)/shard_map/ppermute | solution.py:582
  162.4 13.6 %collective-permute-start.7 = (bf16[2,1,144,384]{3,2,0,1:T(8,128)(2,1)S(1)}, bf16[2,1,144,384]{3,2,0,1:T(8,128)(2,1)S(1)}, u32[]{:S(2)}, u32[]{:S(2)}) collective-permute-start(bf16[2,1,144,384]{3,2,0,1:T(8,128)(2,1)S(1)} %slice.101), channel_id=1, source_target_pairs={{0,2},{1,3},{2,0},{3,1},{4,6},{5,7},{6,4},{7,5},{8,10},{9,11},{10,... | collective-permute-start | bytes 663560 | tf_op jit(solution)/shard_map/ppermute | solution.py:582
  162.8 19.6 %collective-permute-start.17 = (bf16[1,144,1536]{2,1,0:T(8,128)(2,1)S(1)}, bf16[1,144,1536]{2,1,0:T(8,128)(2,1)S(1)}, u32[]{:S(2)}, u32[]{:S(2)}) collective-permute-start(bf16[1,144,1536]{2,1,0:T(8,128)(2,1)S(1)} %slice.113), channel_id=1, source_target_pairs={{0,2},{1,3},{2,0},{3,1},{4,6},{5,7},{6,4},{7,5},{8,10},{9,11},{10,... | collective-permute-start | bytes 1327112 | tf_op jit(solution)/shard_map/ppermute | solution.py:582
  168.5 21.0 %collective-permute-start.13 = (bf16[2,144,384]{2,1,0:T(8,128)(2,1)S(1)}, bf16[2,144,384]{2,1,0:T(8,128)(2,1)S(1)}, u32[]{:S(2)}, u32[]{:S(2)}) collective-permute-start(bf16[2,144,384]{2,1,0:T(8,128)(2,1)S(1)} %fusion.10), channel_id=1, source_target_pairs={{0,4},{4,0},{8,12},{12,8},{16,20},{20,16},{24,28},{28,24},{1,5},{5... | collective-permute-start | bytes 663560 | tf_op jit(solution)/shard_map/ppermute | solution.py:582
  176.0 15.2 %collective-permute-start.8 = (bf16[2,144,384]{2,1,0:T(8,128)(2,1)S(1)}, bf16[2,144,384]{2,1,0:T(8,128)(2,1)S(1)}, u32[]{:S(2)}, u32[]{:S(2)}) collective-permute-start(bf16[2,144,384]{2,1,0:T(8,128)(2,1)S(1)} %fusion.9), channel_id=1, source_target_pairs={{0,4},{4,0},{8,12},{12,8},{16,20},{20,16},{24,28},{28,24},{1,5},{5... | collective-permute-start | bytes 663560 | tf_op jit(solution)/shard_map/ppermute | solution.py:582
  182.5 16.7 %collective-permute-start.18 = (bf16[144,1536]{1,0:T(8,128)(2,1)S(1)}, bf16[144,1536]{1,0:T(8,128)(2,1)S(1)}, u32[]{:S(2)}, u32[]{:S(2)}) collective-permute-start(bf16[144,1536]{1,0:T(8,128)(2,1)S(1)} %fusion.1), channel_id=1, source_target_pairs={{0,4},{4,0},{8,12},{12,8},{16,20},{20,16},{24,28},{28,24},{1,5},{5... | collective-permute-start | bytes 1327112 | tf_op jit(solution)/shard_map/ppermute | solution.py:582
  189.6 11.7 %collective-permute-start.14 = (bf16[2,144,384]{2,1,0:T(8,128)(2,1)S(1)}, bf16[2,144,384]{2,1,0:T(8,128)(2,1)S(1)}, u32[]{:S(2)}, u32[]{:S(2)}) collective-permute-start(bf16[2,144,384]{2,1,0:T(8,128)(2,1)S(1)} %add_convert_fusion.7), channel_id=1, source_target_pairs={{0,8},{4,12},{8,0},{12,4},{16,24},{20,28},{24,16},{28,20},{1,9},{5... | collective-permute-start | bytes 663560 | tf_op jit(solution)/shard_map/ppermute | solution.py:582
  191.3 12.5 %collective-permute-start.9 = (bf16[2,144,384]{2,1,0:T(8,128)(2,1)S(1)}, bf16[2,144,384]{2,1,0:T(8,128)(2,1)S(1)}, u32[]{:S(2)}, u32[]{:S(2)}) collective-permute-start(bf16[2,144,384]{2,1,0:T(8,128)(2,1)S(1)} %add_convert_fusion.10), channel_id=1, source_target_pairs={{0,8},{4,12},{8,0},{12,4},{16,24},{20,28},{24,16},{28,20},{1,9},{5... | collective-permute-start | bytes 663560 | tf_op jit(solution)/shard_map/ppermute | solution.py:582
  199.3 20.1 %collective-permute-start.19 = (bf16[144,1536]{1,0:T(8,128)(2,1)S(1)}, bf16[144,1536]{1,0:T(8,128)(2,1)S(1)}, u32[]{:S(2)}, u32[]{:S(2)}) collective-permute-start(bf16[144,1536]{1,0:T(8,128)(2,1)S(1)} %add_convert_fusion.2), channel_id=1, source_target_pairs={{0,8},{4,12},{8,0},{12,4},{16,24},{20,28},{24,16},{28,20},{1,9},{5... | collective-permute-start | bytes 1327112 | tf_op jit(solution)/shard_map/ppermute | solution.py:582
  201.3 19.2 %collective-permute-start.15 = (bf16[2,144,384]{2,1,0:T(8,128)(2,1)S(1)}, bf16[2,144,384]{2,1,0:T(8,128)(2,1)S(1)}, u32[]{:S(2)}, u32[]{:S(2)}) collective-permute-start(bf16[2,144,384]{2,1,0:T(8,128)(2,1)S(1)} %add_convert_fusion.6), channel_id=1, source_target_pairs={{0,16},{4,20},{8,24},{12,28},{16,0},{20,4},{24,8},{28,12},{1,17},{... | collective-permute-start | bytes 663560 | tf_op jit(solution)/shard_map/ppermute | solution.py:582
  203.9 28.6 %collective-permute-start.10 = (bf16[2,144,384]{2,1,0:T(8,128)(2,1)S(1)}, bf16[2,144,384]{2,1,0:T(8,128)(2,1)S(1)}, u32[]{:S(2)}, u32[]{:S(2)}) collective-permute-start(bf16[2,144,384]{2,1,0:T(8,128)(2,1)S(1)} %add_convert_fusion.9), channel_id=1, source_target_pairs={{0,16},{4,20},{8,24},{12,28},{16,0},{20,4},{24,8},{28,12},{1,17},{... | collective-permute-start | bytes 663560 | tf_op jit(solution)/shard_map/ppermute | solution.py:582
  219.5 22.1 %collective-permute-start.20 = (bf16[144,1536]{1,0:T(8,128)(2,1)S(1)}, bf16[144,1536]{1,0:T(8,128)(2,1)S(1)}, u32[]{:S(2)}, u32[]{:S(2)}) collective-permute-start(bf16[144,1536]{1,0:T(8,128)(2,1)S(1)} %add_convert_fusion.1), channel_id=1, source_target_pairs={{0,16},{4,20},{8,24},{12,28},{16,0},{20,4},{24,8},{28,12},{1,17},{... | collective-permute-start | bytes 1327112 | tf_op jit(solution)/shard_map/ppermute | solution.py:582
  (1 other events, 0.7 us)

commit v3 on v2

v3 whole, which is shorter than its diff:
```python
import functools

import jax
import jax.numpy as jnp
from jax import lax
from jax.experimental import pallas as pl
from jax.experimental.pallas import tpu as pltpu
from jax.sharding import PartitionSpec as P

H = 8
HD = 64
SCALE = HD ** (-0.5)
NORM_EPSILON = 1e-05
MASK_FILL = -1e30
SAFE_SCORE = 50.0

CHUNK = 672
ROWS = 480
SPLITS = 1
STAGES = 7
ONES = 16
EXTRA = 16
LANES = 128
CUT = 512
LOG2E = 1.4426950408889634
TRIPLE = 3 * LANES
GROUPS = ((0, 2), (2, 2))

F32 = jnp.float32
BF16 = jnp.bfloat16
VMEM_LIMIT = 60 << 20

SQUARES = (2, 4, 5, 7, 11, 13)
VECTORS = (3, 6, 8, 9, 10, 12, 14, 15, 16)
MIDDLE_VECTORS = 7


def dot(left, right, left_dim=1, right_dim=0):
    return lax.dot_general(
        left, right, (((left_dim,), (right_dim,)), ((), ())), preferred_element_type=F32
    )


def params():
    return pltpu.CompilerParams(vmem_limit_bytes=VMEM_LIMIT)


def cost(flops, moved):
    return pl.CostEstimate(flops=int(flops), bytes_accessed=int(moved), transcendentals=0)


def offsets(shards):
    held, mask = [0], shards // 2
    while mask:
        held = held + [offset ^ mask for offset in held]
        mask //= 2
    return held


def pack_kernel(*refs):
    flags_ref, squares, vectors = refs[0], refs[1:7], refs[7:16]
    early_ref, late_ref, scalars_ref = refs[16:]
    block = squares[0].shape[0]
    for i in range(3):
        early_ref[i * block : (i + 1) * block, :] = squares[i][...]
        late_ref[i * block : (i + 1) * block, :] = squares[3 + i][...]
    rows = [vector[...].astype(F32).reshape(1, -1) for vector in vectors]
    rows = jnp.concatenate(rows + [jnp.zeros((EXTRA - len(rows), block), F32)], axis=0)
    early_ref[3 * block :, :] = jnp.zeros((EXTRA, early_ref.shape[1]), BF16)
    early_ref[3 * block :, 0:block] = rows.astype(BF16)
    flagged = jnp.where(flags_ref[...] > 0, 1.0, 0.0)
    cells = flags_ref.shape[0]
    for cell in range(cells):
        scalars_ref[cell] = jnp.sum(flagged[cell : cell + 1, :]).astype(jnp.int32)
    scalars_ref[cells] = lax.axis_index("fsdp")


def pack(flags, squares, vectors):
    block, width = squares[0].shape
    cells = flags.shape[0]
    vmem = pl.BlockSpec(memory_space=pltpu.VMEM)
    return pl.pallas_call(
        pack_kernel,
        out_shape=(
            jax.ShapeDtypeStruct((3 * block + EXTRA, width), BF16),
            jax.ShapeDtypeStruct((3 * block, width), BF16),
            jax.ShapeDtypeStruct((cells + 1,), jnp.int32),
        ),
        in_specs=[vmem] * 16,
        out_specs=[vmem, vmem, pl.BlockSpec(memory_space=pltpu.SMEM)],
        compiler_params=params(),
        name="pack",
    )(flags, *squares, *vectors)


def gather_kernel(scalars_ref, flags_ref, x_ref, xc_ref, xt_ref, pos_ref):
    known = scalars_ref[pl.program_id(0)]
    length, width = x_ref.shape[1], x_ref.shape[2]
    flagged = flags_ref[pl.ds(pl.program_id(0), 1), :] > 0
    before = lax.broadcasted_iota(jnp.int32, (length, length), 0)
    after = lax.broadcasted_iota(jnp.int32, (length, length), 1)
    upper = jnp.where(before <= after, 1.0, 0.0).astype(BF16)
    marks = jnp.broadcast_to(jnp.where(flagged, 1.0, 0.0), (16, length)).astype(BF16)
    place = dot(marks, upper)[0:1, :].astype(jnp.int32) - 1
    place = jnp.where(flagged, place, -1)
    pos_ref[0] = place

    for chunk in range(xc_ref.shape[1] // CHUNK):

        @pl.when((chunk == 0) | (chunk * CHUNK < known))
        def _():
            target = chunk * CHUNK + lax.broadcasted_iota(jnp.int32, (CHUNK, length), 0)
            target = jnp.where(known > 0, jnp.minimum(target, known - 1), -2)
            chosen = jnp.where(place == target, 1.0, 0.0).astype(BF16)
            xc_ref[0, chunk * CHUNK : (chunk + 1) * CHUNK, :] = dot(chosen, x_ref[0]).astype(BF16)

    xt_ref[0, 0:width, :] = x_ref[0].T
    xt_ref[0, width:, :] = jnp.ones((ONES, length), BF16)


def gather_known(scalars, flags, x):
    cells, length, width = x.shape
    padded = -(-length // CHUNK) * CHUNK
    one = lambda *shape: pl.BlockSpec((1,) + shape, lambda i, s: (i, 0, 0))
    return pl.pallas_call(
        gather_kernel,
        out_shape=(
            jax.ShapeDtypeStruct((cells, padded, width), BF16),
            jax.ShapeDtypeStruct((cells, width + ONES, length), BF16),
            jax.ShapeDtypeStruct((cells, 1, length), jnp.int32),
        ),
        grid_spec=pltpu.PrefetchScalarGridSpec(
            num_scalar_prefetch=1,
            grid=(cells,),
            in_specs=[pl.BlockSpec(flags.shape, lambda i, s: (0, 0)), one(length, width)],
            out_specs=[one(padded, width), one(width + ONES, length), one(1, length)],
        ),
        compiler_params=params(),
        cost_estimate=cost(cells * 2e9, cells * 6e6),
        name="gather_known",
    )(scalars, flags, x)


def as_column(row):
    return jnp.broadcast_to(row, (LANES, LANES)).T[:, 0:1]


def attend_kernel(*refs, held, cells):
    scalars_ref, refs = refs[0], refs[1:]
    pieces, refs = refs[: len(held)], refs[len(held) :]
    (
        xt_ref, xc_ref, pos_ref,
        w_ref, vec_ref, qkv_ref, kct_ref, vc_ref, e_ref, more_ref, top_ref, ot_ref, o_ref, lse_ref, own_ref,
        bias, qz, kc, vct, top, own, acc, spill,
    ) = refs
    cell, pair = pl.program_id(0), pl.program_id(1)
    known = scalars_ref[cell]
    me = scalars_ref[cells]
    width, length = w_ref.shape[0], xt_ref.shape[2]
    pairs = width // LANES
    block = width // len(held)

    @pl.when((cell == 0) & (pair == 0))
    def _():
        for offset, piece in zip(held, pieces):
            owner = me ^ offset
            rows = pl.ds(pl.multiple_of(owner * block, block), block)
            for which in range(3):
                for p in range(pairs):
                    col = p * TRIPLE + which * LANES
                    w_ref[rows, col : col + LANES] = piece[
                        which * block : (which + 1) * block, p * LANES : (p + 1) * LANES
                    ]
            vec_ref[:, rows] = piece[3 * block :, 0:block].astype(F32)
        qz[...] = jnp.zeros_like(qz)
        for p in range(pairs):
            cols = slice(p * LANES, (p + 1) * LANES)
            bias[p, :, 0:1] = as_column(vec_ref[0:1, cols])
            bias[p, :, 1:2] = as_column(vec_ref[1:2, cols])

    col = pl.multiple_of(pair * TRIPLE, LANES)
    part = lambda first, count: w_ref[:, pl.ds(col + first * LANES, count * LANES)]
    hidden = pos_ref[0] < 0
    steps = (known + CHUNK - 1) // CHUNK
    value_bias = vec_ref[1:2, pl.ds(pl.multiple_of(pair * LANES, LANES), LANES)]
    tokens = xt_ref[0, 0:width, :]
    heads = [slice(side * HD, (side + 1) * HD) for side in range(2)]
    cuts = [slice(start, min(start + CUT, length)) for start in range(0, length, CUT)]

    def project(chunk):
        rows = pl.ds(pl.multiple_of(chunk * CHUNK, 16), CHUNK)
        packed = dot(xc_ref[0, rows, :], part(1, 2))
        yield
        row = chunk * CHUNK + lax.broadcasted_iota(jnp.int32, (CHUNK, LANES), 0)
        keys = packed[:, 0:LANES]
        kc[...] = keys.astype(BF16)
        kct_ref[0, 0, chunk] = jnp.where(row < known, keys, 0.0).astype(BF16).T
        yield
        values = packed[:, LANES:] + value_bias
        vc_ref[0, 0, rows, :] = values.astype(BF16)
        values = jnp.where(row < known, values, 0.0).astype(BF16).T
        counted = chunk * CHUNK + lax.broadcasted_iota(jnp.int32, (EXTRA, CHUNK), 1)
        counted = jnp.where(counted < known, 1.0, 0.0).astype(BF16)
        for side in range(2):
            vct[side, 0:HD, :] = values[heads[side], :]
            vct[side, HD:, :] = counted
        yield

    def begin(side, shifted):
        weight = jnp.ones((1, length), F32) if shifted else jnp.exp(own[side])
        weight = jnp.where(hidden, weight, 0.0).astype(BF16).astype(F32)
        top[side] = jnp.where(hidden, own[side], MASK_FILL) if shifted else jnp.zeros((1, length), F32)
        return weight

    def own_values(side):
        return qkv_ref[0, 0, 2 * LANES + side * HD : 2 * LANES + (side + 1) * HD, :].astype(F32)

    def measure(side):
        q = qkv_ref[0, 0, heads[side], :].astype(F32)
        k = qkv_ref[0, 0, LANES + side * HD : LANES + (side + 1) * HD, :].astype(F32)
        own[side] = jnp.sum(q * k, axis=0, keepdims=True) * SCALE
        longest_q = jnp.max(jnp.sum(q * q, axis=0, keepdims=True))
        longest_k = jnp.max(jnp.sum(k * k, axis=0, keepdims=True))
        return longest_q * longest_k < (SAFE_SCORE / SCALE) * (SAFE_SCORE / SCALE)

    def conclude(side):
        total = acc[side, HD : HD + 1, :]
        ot_ref[0, heads[side], :] = (acc[side, 0:HD, :] * (1.0 / total)).astype(BF16)
        lse_ref[0, side] = top[side] + jnp.log(total)
        own_ref[0, side] = own[side]

    first = project(0)
    next(first)
    turned = dot(part(0, 1), tokens, 0, 0)
    next(first)
    queries = (turned + bias[pair, :, 0:1]).astype(BF16)
    turned = dot(part(1, 1), tokens, 0, 0)
    qkv_ref[0, 0, 0:LANES, :] = queries
    for side in range(2):
        qz[side, heads[side], :] = queries[heads[side], :]
    next(first)
    qkv_ref[0, 0, LANES : 2 * LANES, :] = turned.astype(BF16)
    turned = dot(part(2, 1), tokens, 0, 0)
    weights = []
    safe = None
    for side in range(2):
        for cut in cuts:
            scores = dot(kc[...], qz[side, :, cut])
            e_ref[0, 0, side, :, cut] = jnp.exp2(scores * (SCALE * LOG2E)).astype(BF16)
            if side == 0 and cut is cuts[0]:
                qkv_ref[0, 0, 2 * LANES :, :] = (turned + bias[pair, :, 1:2]).astype(BF16)
            if cut is cuts[1]:
                bounded = measure(side)
                safe = bounded if safe is None else safe & bounded
                weights.append(begin(side, False))
        total = dot(vct[side], e_ref[0, 0, side])
        acc[side, 0:HD, :] = total[0:HD, :] + weights[side] * own_values(side)
        acc[side, HD:, :] = total[HD:, :] + weights[side]
    for side in range(2):
        conclude(side)
        top_ref[0, 0, 0, side] = top[side]
    o_ref[0] = ot_ref[0].T

    def weigh(chunk, side, exps, shifted):
        scores = dot(kc[...], qz[side]) * SCALE
        if shifted:
            peak = jnp.maximum(top[side], jnp.max(scores, axis=0, keepdims=True))
            peak = jnp.where(known > 0, peak, top[side])
            scores = jnp.minimum(scores - peak, 0.0)
        probs = jnp.exp(scores).astype(BF16)
        exps[side] = probs
        if shifted:
            acc[side] = acc[side] * jnp.exp(top[side] - peak) + dot(vct[side], probs)
            top[side] = peak
        else:
            acc[side] += dot(vct[side], probs)
        top_ref[0, 0, chunk, side] = top[side]

    @pl.when(jnp.logical_not(safe))
    def _():
        for side in range(2):
            weight = begin(side, True)
            acc[side, 0:HD, :] = weight * own_values(side)
            acc[side, HD:, :] = jnp.broadcast_to(weight, (EXTRA, length))
            weigh(0, side, e_ref.at[0, 0], True)

    def later_chunk(chunk, carry):
        for _ in project(chunk):
            pass

        @pl.when(safe)
        def _():
            for side in range(2):
                weigh(chunk, side, spill, False)

        @pl.when(jnp.logical_not(safe))
        def _():
            for side in range(2):
                weigh(chunk, side, spill, True)

        pltpu.sync_copy(spill, more_ref.at[cell, pair, chunk - 1])
        return carry

    lax.fori_loop(1, steps, later_chunk, 0)

    @pl.when(jnp.logical_not(safe) | (steps > 1))
    def _():
        for side in range(2):
            conclude(side)
        o_ref[0] = ot_ref[0].T


def attend(scalars, held, pieces, xt, xc, pos):
    cells, length = xt.shape[0], xt.shape[2]
    width = xt.shape[1] - ONES
    padded = xc.shape[1]
    pairs = width // LANES
    chunks = padded // CHUNK
    full = lambda *shape: pl.BlockSpec(shape, lambda c, p, s: (0,) * len(shape))
    shape = jax.ShapeDtypeStruct
    return pl.pallas_call(
        functools.partial(attend_kernel, held=held, cells=cells),
        out_shape=(
            shape((width, 3 * width), BF16),
            shape((EXTRA, width), F32),
            shape((cells, pairs, TRIPLE, length), BF16),
            shape((cells, pairs, chunks, LANES, CHUNK), BF16),
            shape((cells, pairs, padded, LANES), BF16),
            shape((cells, pairs, 2, CHUNK, length), BF16),
            shape((cells, pairs, max(chunks - 1, 1), 2, CHUNK, length), BF16),
            shape((cells, pairs, chunks, 2, 1, length), F32),
            shape((cells, width, length), BF16),
            shape((cells, length, width), BF16),
            shape((cells, H, 1, length), F32),
            shape((cells, H, 1, length), F32),
        ),
        grid_spec=pltpu.PrefetchScalarGridSpec(
            num_scalar_prefetch=1,
            grid=(cells, pairs),
            in_specs=[full(*piece.shape) for piece in pieces]
            + [
                pl.BlockSpec((1, width + ONES, length), lambda c, p, s: (c, 0, 0)),
                pl.BlockSpec((1, padded, width), lambda c, p, s: (c, 0, 0)),
                pl.BlockSpec((1, 1, length), lambda c, p, s: (c, 0, 0)),
            ],
            out_specs=[
                full(width, 3 * width),
                full(EXTRA, width),
                pl.BlockSpec((1, 1, TRIPLE, length), lambda c, p, s: (c, p, 0, 0)),
                pl.BlockSpec((1, 1, chunks, LANES, CHUNK), lambda c, p, s: (c, p, 0, 0, 0)),
                pl.BlockSpec((1, 1, padded, LANES), lambda c, p, s: (c, p, 0, 0)),
                pl.BlockSpec((1, 1, 2, CHUNK, length), lambda c, p, s: (c, p, 0, 0, 0)),
                pl.BlockSpec(memory_space=pl.ANY),
                pl.BlockSpec((1, 1, chunks, 2, 1, length), lambda c, p, s: (c, p, 0, 0, 0, 0)),
                pl.BlockSpec((1, LANES, length), lambda c, p, s: (c, p, 0)),
                pl.BlockSpec((1, length, LANES), lambda c, p, s: (c, 0, p)),
                pl.BlockSpec((1, 2, 1, length), lambda c, p, s: (c, p, 0, 0)),
                pl.BlockSpec((1, 2, 1, length), lambda c, p, s: (c, p, 0, 0)),
            ],
            scratch_shapes=[
                pltpu.VMEM((pairs, LANES, 8), F32),
                pltpu.VMEM((2, LANES, length), BF16),
                pltpu.VMEM((CHUNK, LANES), BF16),
                pltpu.VMEM((2, HD + EXTRA, CHUNK), BF16),
                pltpu.VMEM((2, 1, length), F32),
                pltpu.VMEM((2, 1, length), F32),
                pltpu.VMEM((2, HD + EXTRA, length), F32),
                pltpu.VMEM((2, CHUNK, length), BF16),
            ],
        ),
        compiler_params=params(),
        cost_estimate=cost(cells * 1e10, cells * 2.5e7),
        name="attend",
    )(scalars, *pieces, xt, xc, pos)


def row_mean(rows):
    return jnp.mean(rows, axis=-1, keepdims=True)


def normalize(rows):
    centred = rows - row_mean(rows)
    scale = lax.rsqrt(row_mean(centred * centred) + NORM_EPSILON)
    return centred * scale, scale


def norm_back(grad, normed, scale):
    return scale * (grad - row_mean(grad) - normed * row_mean(grad * normed))


def column_sum(rows):
    return jnp.sum(rows, axis=0, keepdims=True)


def middle_kernel(*refs, held, cells):
    scalars_ref, refs = refs[0], refs[1:]
    pieces, refs = refs[: len(held)], refs[len(held) :]
    (
        x_ref, o_ref, cot_ref, vec_ref,
        result_ref, dhid_ref, datt_ref, keep_ref, send_ref,
        w, go, gu, gd, gvec,
    ) = refs
    me = scalars_ref[cells]
    width = x_ref.shape[1]
    block = width // len(held)

    @pl.when(pl.program_id(0) == 0)
    def _():
        for offset, piece in zip(held, pieces):
            rows = pl.ds(pl.multiple_of((me ^ offset) * block, block), block)
            for which in range(3):
                w[which, rows, :] = piece[which * block : (which + 1) * block, :]
        go[...] = jnp.zeros_like(go)
        gu[...] = jnp.zeros_like(gu)
        gd[...] = jnp.zeros_like(gd)
        gvec[...] = jnp.zeros_like(gvec)

    def stages(rows):
        out_bias, gain_one, shift_one, up_bias, down_bias, gain_two, shift_two = (
            vec_ref[2 + i : 3 + i, :] for i in range(MIDDLE_VECTORS)
        )
        attended = o_ref[rows, :]
        product = dot(attended, w[0])
        yield
        norm_one, scale_one = normalize(x_ref[rows, :].astype(F32) + (product + out_bias))
        first_norm = norm_one * gain_one + shift_one
        first_low = first_norm.astype(BF16)
        product = dot(first_low, w[1])
        yield
        pre_act = product + up_bias
        below = 0.5 * (1.0 + lax.erf(pre_act * (0.5**0.5)))
        activated = (pre_act * below).astype(BF16)
        product = dot(activated, w[2])
        slope = below + pre_act * (jnp.exp(-0.5 * pre_act * pre_act) * 0.3989422804014327)
        yield
        norm_two, scale_two = normalize(first_norm + (product + down_bias))
        result_ref[rows, :] = (norm_two * gain_two + shift_two).astype(BF16)
        dy = cot_ref[rows, :].astype(F32)
        d_second = norm_back(dy * gain_two, norm_two, scale_two)
        d_ff = d_second.astype(BF16)
        product = dot(d_ff, w[2], 1, 1)
        gvec[4:5, :] += column_sum(d_ff.astype(F32))
        gvec[5:6, :] += column_sum(dy * norm_two)
        gvec[6:7, :] += column_sum(dy)
        yield
        d_pre = (product * slope).astype(BF16)
        product = dot(d_pre, w[1], 1, 1)
        gd[...] += dot(activated, d_ff, 0, 0)
        gvec[3:4, :] += column_sum(d_pre.astype(F32))
        yield
        d_first = d_second + product
        d_hidden = norm_back(d_first * gain_one, norm_one, scale_one)
        d_attn = d_hidden.astype(BF16)
        dhid_ref[rows, :] = d_attn
        product = dot(d_attn, w[0], 1, 1)
        gu[...] += dot(first_low, d_pre, 0, 0)
        gvec[0:1, :] += column_sum(d_attn.astype(F32))
        gvec[1:2, :] += column_sum(d_first * norm_one)
        gvec[2:3, :] += column_sum(d_first)
        yield
        datt_ref[rows, :] = product.astype(BF16)
        go[...] += dot(attended, d_attn, 0, 0)
        yield

    step = x_ref.shape[0] // SPLITS
    live = [stages(slice(i * step, (i + 1) * step)) for i in range(SPLITS)]
    for turn in range(STAGES + SPLITS - 1):
        for i, part in enumerate(live):
            if 0 <= turn - i < STAGES:
                next(part)

    @pl.when(pl.program_id(0) == pl.num_programs(0) - 1)
    def _():
        for offset in range(len(held)):
            target = (keep_ref, send_ref)[offset % 2].at[offset // 2]
            rows = pl.ds(pl.multiple_of((me ^ offset) * block, block), block)
            for which, grad in enumerate((go, gu, gd)):
                cols = slice(which * width, (which + 1) * width)
                target[0:block, cols] = grad[rows, :].astype(BF16)
            target[block:, :] = jnp.zeros((EXTRA, 3 * width), BF16)
            target[block:, 0:block] = gvec[:, rows].astype(BF16)


def middle(scalars, held, pieces, x, o, cot, vec, cells):
    rows, width = x.shape
    step = ROWS if rows % ROWS == 0 else rows
    block = pl.BlockSpec((step, width), lambda i, s: (i, 0))
    full = lambda *shape: pl.BlockSpec(shape, lambda i, s: (0,) * len(shape))
    low = jax.ShapeDtypeStruct((rows, width), BF16)
    half = (len(held) // 2, width // len(held) + EXTRA, 3 * width)
    return pl.pallas_call(
        functools.partial(middle_kernel, held=held, cells=cells),
        out_shape=(low, low, low, jax.ShapeDtypeStruct(half, BF16), jax.ShapeDtypeStruct(half, BF16)),
        grid_spec=pltpu.PrefetchScalarGridSpec(
            num_scalar_prefetch=1,
            grid=(rows // step,),
            in_specs=[full(*piece.shape) for piece in pieces] + [block, block, block, full(EXTRA, width)],
            out_specs=[block, block, block, full(*half), full(*half)],
            scratch_shapes=[
                pltpu.VMEM((3, width, width), BF16),
                pltpu.VMEM((width, width), F32),
                pltpu.VMEM((width, width), F32),
                pltpu.VMEM((width, width), F32),
                pltpu.VMEM((EXTRA, width), F32),
            ],
        ),
        compiler_params=params(),
        cost_estimate=cost(rows * 5e6, rows * 8e3),
        name="middle",
    )(scalars, *pieces, x, o, cot, vec)


def back_kernel(
    scalars_ref, pos_ref, xt_ref, qkv_ref, kct_ref, vc_ref, e_ref, more_ref, top_ref, ot_ref, lse_ref,
    own_ref, datt_ref,
    dt_ref, keep_ref, send_ref,
    hot, oz, og, ds, joined, dqa, dkv, self_q, self_kv, delta, grad, term, spill,
    *, shards, cells, first_pair,
):
    pair, cell = pl.program_id(0), pl.program_id(1)
    known = scalars_ref[cell]
    me = scalars_ref[cells]
    width, length = xt_ref.shape[1] - ONES, xt_ref.shape[2]
    block = width // shards
    steps = (known + CHUNK - 1) // CHUNK
    place = pos_ref[0]
    hidden = place < 0

    @pl.when(pair == 0)
    def _():
        hot[cell, 0] = jnp.where(
            place == lax.broadcasted_iota(jnp.int32, (CHUNK, length), 0), 1.0, 0.0
        ).astype(BF16)

        def mark(chunk, carry):
            row = chunk * CHUNK + lax.broadcasted_iota(jnp.int32, (CHUNK, length), 0)
            hot[cell, chunk] = jnp.where(place == row, 1.0, 0.0).astype(BF16)
            return carry

        lax.fori_loop(1, steps, mark, 0)

    heads = [slice(side * HD, (side + 1) * HD) for side in range(2)]
    cuts = [slice(start, min(start + CUT, length)) for start in range(0, length, CUT)]
    queries = qkv_ref.at[0, 0, 0:LANES]

    @pl.when((pair == 0) & (cell == 0))
    def _():
        oz[...] = jnp.zeros_like(oz)

    og[...] = datt_ref[0].T

    def share(chunk, side):
        return jnp.exp(top_ref[0, 0, chunk, side] - lse_ref[0, side])

    def outset(side):
        rows = heads[side]
        grads = og[rows, :].astype(F32)
        query = queries[rows, :].astype(F32) * SCALE
        key = qkv_ref[0, 0, LANES + side * HD : LANES + (side + 1) * HD, :].astype(F32)
        value = qkv_ref[0, 0, 2 * LANES + side * HD : 2 * LANES + (side + 1) * HD, :].astype(F32)
        prob = jnp.exp(jnp.where(hidden, own_ref[0, side], MASK_FILL) - lse_ref[0, side])
        own_grad = jnp.sum(grads * value, axis=0, keepdims=True)
        back = (prob * (own_grad - delta[side])).astype(BF16).astype(F32)
        self_q[rows, :] = back * key
        self_kv[rows, :] = back * query
        self_kv[LANES + side * HD : LANES + (side + 1) * HD, :] = prob.astype(BF16).astype(F32) * grads

    def score_grads(chunk, side, exps, values, cut, scaled):
        part = dot(values, oz[side, :, cut]) - scaled[:, cut]
        ds[side, :, cut] = (exps[side, :, cut].astype(F32) * part).astype(BF16)

    def spread(chunk, side, part):
        scaled = share(chunk, side)
        oz[side, heads[side], :] = (og[heads[side], :].astype(F32) * scaled).astype(BF16)
        return delta[side] * scaled

    def close(q_part, kv_part):
        dt_ref[0, 0, 0:LANES, :] = ((q_part + self_q[...]) * SCALE).astype(BF16)
        dt_ref[0, 0, LANES:, :] = (kv_part + self_kv[...]).astype(BF16)
        term[...] = dot(xt_ref[0], dt_ref[0, 0], 1, 1)

    exps = e_ref.at[0, 0]
    values = vc_ref[0, 0, 0:CHUNK, :]
    for side in range(2):
        rows = heads[side]
        delta[side] = jnp.sum(
            og[rows, :].astype(F32) * ot_ref[0, rows, :].astype(F32), axis=0, keepdims=True
        )
    scaled = [spread(0, side, None) for side in range(2)]
    for cut in cuts:
        score_grads(0, 0, exps, values, cut, scaled[0])
    d_values = dot(exps[0], oz[0], 1, 1)
    outset(0)
    for cut in cuts:
        score_grads(0, 1, exps, values, cut, scaled[1])
    d_keys = dot(ds[0], queries[...], 1, 1)
    outset(1)
    d_values += dot(exps[1], oz[1], 1, 1)
    lanes = lax.broadcasted_iota(jnp.int32, (CHUNK, LANES), 1) < HD
    joined[:, LANES:] = d_values.astype(BF16)
    dqa[0:HD, :] = dot(kct_ref[0, 0, 0, 0:HD, :], ds[0])
    d_keys = jnp.where(lanes, d_keys, dot(ds[1], queries[...], 1, 1)) * SCALE
    dqa[HD:, :] = dot(kct_ref[0, 0, 0, HD:, :], ds[1])
    joined[:, 0:LANES] = d_keys.astype(BF16)
    dkv[...] = dot(joined[...], hot[cell, 0], 0, 0)
    close(dqa[...], dkv[...])

    def later_chunk(chunk, carry):
        pltpu.sync_copy(more_ref.at[cell, first_pair + pair, chunk - 1], spill)
        values = vc_ref[0, 0, pl.ds(pl.multiple_of(chunk * CHUNK, 16), CHUNK), :]
        d_values = jnp.zeros((CHUNK, LANES), F32)
        for side in range(2):
            scaled = spread(chunk, side, None)
            for cut in cuts:
                score_grads(chunk, side, spill, values, cut, scaled)
            d_values += dot(spill[side], oz[side], 1, 1)
            dqa[heads[side], :] += dot(kct_ref[0, 0, chunk, heads[side], :], ds[side])
        d_keys = jnp.where(lanes, dot(ds[0], queries[...], 1, 1), dot(ds[1], queries[...], 1, 1)) * SCALE
        joined[:, 0:LANES] = d_keys.astype(BF16)
        joined[:, LANES:] = d_values.astype(BF16)
        dkv[...] += dot(joined[...], hot[cell, chunk], 0, 0)
        return carry

    @pl.when(steps > 1)
    def _():
        lax.fori_loop(1, steps, later_chunk, 0)
        close(dqa[...], dkv[...])

    @pl.when(cell == 0)
    def _():
        grad[...] = term[...]

    @pl.when(cell > 0)
    def _():
        grad[...] += term[...]

    @pl.when(cell == cells - 1)
    def _():
        for offset in range(shards):
            owner = me ^ offset
            target = (keep_ref, send_ref)[offset % 2].at[offset // 2, 0]
            rows = pl.ds(pl.multiple_of(owner * block, block), block)
            target[0:block, :] = grad[rows, :].astype(BF16)
            ours = jnp.where(owner == first_pair + pair, 1.0, 0.0)
            target[block:, :] = (grad[width:, :] * ours).astype(BF16)


def attend_back(group, shards, scalars, pos, xt, qkv, kct, vc, e, more, top, ot, lse, own, datt):
    first, count = group
    cells, length = xt.shape[0], xt.shape[2]
    width = xt.shape[1] - ONES
    padded = vc.shape[2]
    chunks = padded // CHUNK
    half = (shards // 2, count, width // shards + EXTRA, TRIPLE)
    part = pl.BlockSpec((shards // 2, 1) + half[2:], lambda p, c, s: (0, p, 0, 0))
    shape = jax.ShapeDtypeStruct
    return pl.pallas_call(
        functools.partial(back_kernel, shards=shards, cells=cells, first_pair=first),
        out_shape=(shape((cells, count, TRIPLE, length), BF16), shape(half, BF16), shape(half, BF16)),
        grid_spec=pltpu.PrefetchScalarGridSpec(
            num_scalar_prefetch=1,
            grid=(count, cells),
            in_specs=[
                pl.BlockSpec((1, 1, length), lambda p, c, s: (c, 0, 0)),
                pl.BlockSpec((1, width + ONES, length), lambda p, c, s: (c, 0, 0)),
                pl.BlockSpec((1, 1, TRIPLE, length), lambda p, c, s: (c, first + p, 0, 0)),
                pl.BlockSpec((1, 1, chunks, LANES, CHUNK), lambda p, c, s: (c, first + p, 0, 0, 0)),
                pl.BlockSpec((1, 1, padded, LANES), lambda p, c, s: (c, first + p, 0, 0)),
                pl.BlockSpec((1, 1, 2, CHUNK, length), lambda p, c, s: (c, first + p, 0, 0, 0)),
                pl.BlockSpec(memory_space=pl.ANY),
                pl.BlockSpec((1, 1, chunks, 2, 1, length), lambda p, c, s: (c, first + p, 0, 0, 0, 0)),
                pl.BlockSpec((1, LANES, length), lambda p, c, s: (c, first + p, 0)),
                pl.BlockSpec((1, 2, 1, length), lambda p, c, s: (c, first + p, 0, 0)),
                pl.BlockSpec((1, 2, 1, length), lambda p, c, s: (c, first + p, 0, 0)),
                pl.BlockSpec((1, length, LANES), lambda p, c, s: (c, 0, first + p)),
            ],
            out_specs=[
                pl.BlockSpec((1, 1, TRIPLE, length), lambda p, c, s: (c, p, 0, 0)),
                part,
                part,
            ],
            scratch_shapes=[
                pltpu.VMEM((cells, chunks, CHUNK, length), BF16),
                pltpu.VMEM((2, LANES, length), BF16),
                pltpu.VMEM((LANES, length), BF16),
                pltpu.VMEM((2, CHUNK, length), BF16),
                pltpu.VMEM((CHUNK, 2 * LANES), BF16),
                pltpu.VMEM((LANES, length), F32),
                pltpu.VMEM((2 * LANES, length), F32),
                pltpu.VMEM((LANES, length), F32),
                pltpu.VMEM((2 * LANES, length), F32),
                pltpu.VMEM((2, 1, length), F32),
                pltpu.VMEM((width + ONES, TRIPLE), F32),
                pltpu.VMEM((width + ONES, TRIPLE), F32),
                pltpu.VMEM((2, CHUNK, length), BF16),
            ],
        ),
        compiler_params=params(),
        cost_estimate=cost(cells * count * 6e9, cells * count * 7e6),
        name="attend_back",
    )(scalars, pos, xt, qkv, kct, vc, e, more, top, ot, lse, own, datt)


def input_kernel(w_ref, dhid_ref, *refs):
    parts, out_ref = refs[:-1], refs[-1]
    back, col = None, 0
    for part in parts:
        rows = part.shape[1]
        term = dot(w_ref[:, col : col + rows], part[0])
        back = term if back is None else back + term
        col += rows
    out_ref[0] = (back.T + dhid_ref[0].astype(F32)).astype(BF16)


def input_grad(w, dhid, parts):
    cells, length, width = dhid.shape
    parts = [part.reshape(cells, -1, length) for part in parts]
    block = pl.BlockSpec((1, length, width), lambda i: (i, 0, 0))
    return pl.pallas_call(
        input_kernel,
        out_shape=jax.ShapeDtypeStruct(dhid.shape, BF16),
        grid=(cells,),
        in_specs=[pl.BlockSpec(w.shape, lambda i: (0, 0)), block]
        + [pl.BlockSpec((1,) + part.shape[1:], lambda i: (i, 0, 0)) for part in parts],
        out_specs=block,
        compiler_params=params(),
        cost_estimate=cost(cells * 2e9, cells * 8e6),
        name="input_grad",
    )(w, dhid, *parts)


def finish_kernel(*refs):
    terms, halves, outs = refs[:2], refs[2:-15], refs[-15:]
    block, width = outs[0].shape
    for which in range(3):
        cols = slice(which * width, (which + 1) * width)
        outs[3 + which][...] = terms[0][0:block, cols].astype(F32) + terms[1][0:block, cols].astype(F32)
    rows = terms[0][block:, 0:block].astype(F32) + terms[1][block:, 0:block].astype(F32)
    for row in range(MIDDLE_VECTORS):
        outs[8 + row][...] = rows[row : row + 1, :].reshape(block)

    def write(order):
        biases = [jnp.zeros((1, LANES), F32), jnp.zeros((1, LANES), F32)]
        pair = 0
        for group in range(0, len(halves), 2):
            for part in [halves[group + i] for i in order]:
                for p in range(part.shape[0]):
                    for which in range(3):
                        cols = slice(which * LANES, (which + 1) * LANES)
                        outs[which][:, pair * LANES : (pair + 1) * LANES] = part[p, 0:block, cols].astype(F32)
                    biases[0] += part[p, block : block + 1, 0:LANES].astype(F32)
                    biases[1] += part[p, block : block + 1, 2 * LANES :].astype(F32)
                    pair += 1
        outs[6][...] = biases[0].reshape(block)
        outs[7][...] = biases[1].reshape(block)

    low = lax.axis_index("dp") % 2 == 0

    @pl.when(low)
    def _():
        write((0, 1))

    @pl.when(jnp.logical_not(low))
    def _():
        write((1, 0))


def finish(parts, block, width):
    vmem = pl.BlockSpec(memory_space=pltpu.VMEM)
    return pl.pallas_call(
        finish_kernel,
        out_shape=(jax.ShapeDtypeStruct((block, width), F32),) * 6 + (jax.ShapeDtypeStruct((block,), F32),) * 9,
        in_specs=[vmem] * len(parts),
        out_specs=[vmem] * 15,
        compiler_params=params(),
        name="finish",
    )(*parts)


def swap(values, axis, mask):
    size = lax.axis_size(axis)
    return lax.ppermute(values, axis, [(i, i ^ mask) for i in range(size)])


def masks(axis):
    found, mask = [], 1
    while mask < lax.axis_size(axis):
        found.append(mask)
        mask *= 2
    return found


def after(value, *others):
    return lax.optimization_barrier((value,) + others)[0]


def gather_pieces(own, beside):
    held = [own]
    for mask in reversed(masks("fsdp")):
        held = held + [swap(piece, "fsdp", mask) for piece in held]
        held = held[:1] + [after(piece, beside) for piece in held[1:]]
    return held


def plus(left, right):
    return left.astype(F32) + right.astype(F32)


class Reduction:
    def __init__(self, keep, send, half_dim=None):
        self.keep, self.send = keep, send
        self.half_dim = half_dim
        order = masks("dp") if half_dim is not None else reversed(masks("dp"))
        self.plan = [("fsdp", mask) for mask in masks("fsdp")] + [("dp", mask) for mask in order]
        self.low = (lax.axis_index("dp") % 2) == 0

    def pair(self):
        return self.keep, self.send

    def start(self, pair=None):
        if self.plan:
            self.keep, self.send = pair or self.pair()
            self.arrived = swap(self.send, *self.plan[0])

    def arrive(self):
        self.plan = self.plan[1:]
        if not self.plan:
            return
        total = plus(self.keep, self.arrived).astype(BF16)
        axis, mask = self.plan[0]
        if axis == "fsdp":
            self.keep, self.send = total[0::2], total[1::2]
        elif mask == 1 and self.half_dim is not None:
            first, second = jnp.split(total, 2, self.half_dim)
            self.keep = jnp.where(self.low, first, second)
            self.send = jnp.where(self.low, second, first)
        else:
            self.keep = self.send = total

    def finish(self):
        while self.plan:
            self.start()
            self.arrive()
        if self.half_dim is None:
            return self.keep[0], self.arrived[0]
        mine = plus(self.keep, self.arrived).astype(BF16)[0]
        if lax.axis_size("dp") == 1:
            return jnp.split(mine, 2, self.half_dim - 1)
        return mine, swap(mine, "dp", 1)


def body(*args):
    tokens, known_flags, cotangent = args[0], args[1], args[17]
    cells, length, width = tokens.shape
    shards = lax.axis_size("fsdp")
    block = width // shards
    held = offsets(shards)

    early, late, scalars = pack(known_flags, [args[i] for i in SQUARES], [args[i] for i in VECTORS])
    xc, xt, pos = gather_known(scalars, known_flags, tokens)
    early = gather_pieces(early, xt)
    late = after(late, *early[:2])
    late = [late] + [swap(late, "fsdp", offset) for offset in held[1:]]
    w, vec, qkv, kct, vc, e, more, top, ot, o, lse, own = attend(scalars, held, early, xt, xc, pos)
    flat = lambda a: a.reshape(cells * length, width)
    result, dhid, datt, keep, send = middle(
        scalars, held, late, flat(tokens), flat(o), flat(cotangent), vec, cells
    )
    cube = lambda a: a.reshape(cells, length, width)
    chains = [Reduction(keep, send)]

    def boundary(value):
        for chain in chains[:-1]:
            chain.arrive()
        newest = chains[-1]
        pairs = lax.optimization_barrier([chain.pair() for chain in chains])
        for chain, (chain.keep, chain.send) in zip(chains, pairs):
            pass
        newest.start()
        newest.arrive()
        value, pairs = lax.optimization_barrier((value, [chain.pair() for chain in chains]))
        for chain, pair in zip(chains, pairs):
            chain.start(pair)
        return value

    parts = []
    for group in GROUPS:
        dt, keep, send = attend_back(
            group, shards, boundary(scalars), pos, xt, qkv, kct, vc, e, more, top, ot, lse, own, cube(datt)
        )
        parts.append(dt)
        chains.append(Reduction(keep, send, 1))
    tokens_grad = input_grad(boundary(w), cube(dhid), parts)
    tokens_grad, arrived = lax.optimization_barrier((tokens_grad, [chain.arrived for chain in chains]))
    for chain, chain.arrived in zip(chains, arrived):
        chain.arrive()
    newest = chains[-1]
    newest.start()
    newest.arrive()
    chains[0].send = after(chains[0].send, newest.send)
    halves = [half for chain in chains for half in chain.finish()]
    summed = finish(halves, block, width)
    out = dict(zip(SQUARES + VECTORS, summed))
    return (cube(result), tokens_grad) + tuple(out[i] for i in range(2, 17))


def solution(mesh):
    cells = P(("dp", "fsdp"), None, None)
    specs = tuple(P("fsdp", None) if i in SQUARES else P("fsdp") for i in range(2, 17))
    return jax.shard_map(
        body,
        mesh=mesh,
        in_specs=(cells, P(("dp", "fsdp"), None)) + specs + (cells,),
        out_specs=(cells, cells) + specs,
        check_vma=False,
    )
```

time: 246 us -> 211 us (0.86)
  waiting for transfers between devices: 49.8 us -> 24.3 us
  Pallas kernels: 132 us -> 155 us
  starting transfers between devices: 43 us -> 21.5 us
  local copies, waits for them, and re-layouts: 12.9 us -> 2.82 us
    ppermute x21 -> x23, waiting for transfers between devices: 49.8 us -> 24.3 us  [swap(): return lax.ppermute(values, axis, [(i, i ^ mask) for i in range(size)])]
    pallas_call x1, Pallas kernels: 33.6 us -> 57.2 us  [attend(): pl.pallas_call(functools.partial(attend_kernel, held=held, cells=cells),...]
    ppermute x21 -> x23, starting transfers between devices: 43 us -> 21.5 us  [swap(): return lax.ppermute(values, axis, [(i, i ^ mask) for i in range(size)])]
    pallas_call x0 -> x2, Pallas kernels: none -> 4.9 us  [the longest x1 2.62 us: finish(): pl.pallas_call(finish_kernel, out_shape=(jax.ShapeDtypeStruct((block, wid...]
    pallas_call x2, Pallas kernels: 55.8 us -> 51.5 us  [attend_back(): pl.pallas_call(functools.partial(back_kernel, shards=shards, cells=cells,...]
    unnamed x29 -> x28, local copies, waits for them, and re-layouts: 6.25 us -> 2.67 us
  transfers between devices with their start and end apart: 21 -> 23, of which waited for: 7 -> 10; matrix products, arithmetic and copies ran while one was open for 5% -> 0% of each run, Pallas kernels for 32% -> 60%
where the time goes in v3:
time: 211 us; the launch traced here: 208 us
  Pallas kernels  155 us (73%)
  waiting for transfers between devices  24.3 us (12%)
  starting transfers between devices  21.5 us (10%)
  other arithmetic  3.3 us (2%)
  local copies, waits for them, and re-layouts  2.82 us (1%)
    pallas_call x1, Pallas kernels, attend(): pl.pallas_call(functools.partial(attend_kernel, held=held, cells=cells),...  57.2 us
    pallas_call x2, Pallas kernels, attend_back(): pl.pallas_call(functools.partial(back_kernel, shards=shards, cells=cells,...  51.5 us
    pallas_call x1, Pallas kernels, middle(): pl.pallas_call(functools.partial(middle_kernel, held=held, cells=cells),...  25.4 us
    ppermute x23, waiting for transfers between devices, swap(): return lax.ppermute(values, axis, [(i, i ^ mask) for i in range(size)])  24.3 us
    ppermute x23, starting transfers between devices, swap(): return lax.ppermute(values, axis, [(i, i ^ mask) for i in range(size)])  21.5 us
    pallas_call x1, Pallas kernels, input_grad(): pl.pallas_call(input_kernel, out_shape=jax.ShapeDtypeStruct(dhid.shape, B...  9.4 us
    pallas_call x1, Pallas kernels, gather_known(): pl.pallas_call(gather_kernel, out_shape=(jax.ShapeDtypeStruct((cells, pad...  6.95 us
  transfers between devices with their start and end apart: 23, of which 10 were waited for; matrix products, arithmetic and copies ran while one was open for 0% of the time, Pallas kernels for 60%

profile of v3, /device:TPU:0, one launch (start us, length us, event | category | flops | bytes accessed | tf_op | source)
XLA Modules:
  0.0 208.4 jit_solution(8192236214175831887)
XLA Ops:
  0.7 2.3 %pack.1 = (bf16[400,512]{1,0:T(8,128)(2,1)}, bf16[384,512]{1,0:T(8,128)(2,1)}, s32[3]{0:T(128)}) custom-call(s32[2,1200]{1,0:T(2,128)} %flags_ref.1, bf16[128,512]{1,0:T(8,128)(2,1)} %refs_1_.1, bf16[128,512]{1,0:T(8,128)(2,1)} %refs_2_.1, bf16[128,512]{1,0:T(8,128)(2,1)} %refs_3_.1, bf16[128,512]{1,0:T(8,128)(2,1)} %refs_4_.1, bf16[128,512]{1,0:T(8,128)(2,1)} %refs_5_.1, ...), custom_call_target="tpu_custom_call" | custom-call | tf_op jit(solution)/shard_map/pack/pallas_call | solution.py:82
  2.9 3.0 %collective-permute-start = (bf16[400,512]{1,0:T(8,128)(2,1)}, bf16[400,512]{1,0:T(8,128)(2,1)S(1)}, u32[]{:S(2)}, u32[]{:S(2)}) collective-permute-start(bf16[400,512]{1,0:T(8,128)(2,1)} %get-tuple-element.100.refs_1_), channel_id=1, source_target_pairs={{0,2},{1,3},{2,0},{3,1},{4,6},{5,7},{6,4},{7,5},{8,10},{9,11},{10,... | collective-permute-start | bytes 1228808 | tf_op jit(solution)/shard_map/ppermute | solution.py:782
  6.0 7.0 %gather_known.1 = (bf16[2,1344,512]{2,1,0:T(8,128)(2,1)}, bf16[2,528,1200]{2,1,0:T(8,128)(2,1)}, s32[2,1,1200]{2,1,0:T(1,128)}) custom-call(s32[3]{0:T(128)} %get-tuple-element.140.scalars_ref.refs_0_, s32[2,1200]{1,0:T(2,128)} %flags_ref.1, bf16[2,1200,512]{2,1,0:T(8,128)(2,1)} %x_ref.1), custom_call_target="tpu_custom_call" | custom-call | flops 4000000000 | bytes 12000000 | tf_op jit(solution)/shard_map/gather_known/pallas_call | solution.py:125
  12.9 2.7 %collective-permute-done.refs_2_ = bf16[400,512]{1,0:T(8,128)(2,1)S(1)} collective-permute-done((bf16[400,512]{1,0:T(8,128)(2,1)}, bf16[400,512]{1,0:T(8,128)(2,1)S(1)}, u32[]{:S(2)}, u32[]{:S(2)}) %collective-permute-start) | collective-permute-done | bytes 409632 | tf_op jit(solution)/shard_map/ppermute | solution.py:782
  15.7 1.8 collective-permute-start.1
  17.9 0.7 copy-done.8
  18.8 57.2 %attend.1 = (bf16[512,1536]{1,0:T(8,128)(2,1)}, f32[16,512]{1,0:T(8,128)}, bf16[2,4,384,1200]{3,2,1,0:T(8,128)(2,1)}, bf16[2,4,2,128,672]{4,3,2,1,0:T(8,128)(2,1...) custom-call(s32[3]{0:T(128)} %get-tuple-element.140.scalars_ref.refs, ...), custom_call_target="tpu_custom_call" | custom-call | flops 20000000000 | bytes 50000000 | tf_op jit(solution)/shard_map/attend/pallas_call | solution.py:321
  76.0 0.7 copy-done.11
  77.0 25.4 %middle.1 = (bf16[2400,512]{1,0:T(8,128)(2,1)}, bf16[2400,512]{1,0:T(8,128)(2,1)}, bf16[2400,512]{1,0:T(8,128)(2,1)}, bf16[2,144,1536]{2,1,0:T(8,128)(2,1)}, bf16[2,144,1536]{2,1,0:T(8,128)(2,1)}) custom-call(s32[3]{0:T(128)} %get-tuple-element.140.scalars_ref.refs_0_, bf16[384,512]{1,0:T(8,128)(2,1)} %get-tuple-element.104.refs_1_, ...), custom_call_target="tpu_custom_call" | custom-call | flops 12000000000 | bytes 19200000 | tf_op jit(solution)/shard_map/middle/pallas_call | solution.py:491
  102.5 2.6 %collective-permute-done.6 = bf16[2,144,1536]{2,1,0:T(8,128)(2,1)S(1)} collective-permute-done((bf16[2,144,1536]{2,1,0:T(8,128)(2,1)}, bf16[2,144,1536]{2,1,0:T(8,128)(2,1)S(1)}, u32[]{:S(2)}, u32[]{:S(2)}) %collective-permute-start.6) | collective-permute-done | bytes 884768 | tf_op jit(solution)/shard_map/ppermute | solution.py:782
  105.1 1.4 add_convert_fusion
  106.6 25.6 %attend_back.2 = (bf16[2,2,384,1200]{3,2,1,0:T(8,128)(2,1)}, bf16[2,2,144,384]{3,2,1,0:T(8,128)(2,1)}, bf16[2,2,144,384]{3,2,1,0:T(8,128)(2,1)}) custom-call(s32[3]{0:T(128)} %get-tuple-element.140.scalars_ref.refs_0_, s32[2,1,1200]{2,1,0:T(1,128)} %get-tuple-element.108.refs_7_.pos_ref, bf16[2,528,1200]{2,1,0:T(8,128)(2,1)} %get-tuple-element.101.refs_5_.xt_ref, ...), custom_call_target="tpu_custom_call" | custom-call | flops 24000000000 | bytes 28000000 | tf_op jit(solution)/shard_map/attend_back/pallas_call | solution.py:657
  132.6 1.9 collective-permute-done.8
  134.4 1.1 add_convert_fusion.4
  135.6 4.4 %collective-permute-start.9 = (bf16[1,144,1536]{2,1,0:T(8,128)(2,1)S(1)}, bf16[1,144,1536]{2,1,0:T(8,128)(2,1)S(1)}, u32[]{:S(2)}, u32[]{:S(2)}) collective-permute-start(bf16[1,144,1536]{2,1,0:T(8,128)(2,1)S(1)} %add_convert_fusion.5), channel_id=1, source_target_pairs={{0,16},{4,20},{8,24},{12,28},{16,0},{20,4},{24,8},{28,12},{1,17},{... | collective-permute-start | bytes 1327112 | tf_op jit(solution)/shard_map/ppermute | solution.py:782
  140.0 25.8 %attend_back.3 = (bf16[2,2,384,1200]{3,2,1,0:T(8,128)(2,1)}, bf16[2,2,144,384]{3,2,1,0:T(8,128)(2,1)}, bf16[2,2,144,384]{3,2,1,0:T(8,128)(2,1)}) custom-call(s32[3]{0:T(128)} %get-tuple-element.140.scalars_ref.refs_0_, s32[2,1,1200]{2,1,0:T(1,128)} %get-tuple-element.108.refs_7_.pos_ref, bf16[2,528,1200]{2,1,0:T(8,128)(2,1)} %get-tuple-element.101.refs_5_.xt_ref, ...), custom_call_target="tpu_custom_call" | custom-call | flops 24000000000 | bytes 28000000 | tf_op jit(solution)/shard_map/attend_back/pallas_call | solution.py:657
  166.2 2.0 collective-permute-done.11
  168.3 1.5 collective-permute-start.12
  169.8 2.2 %collective-permute-start.13 = (bf16[1,1,144,384]{3,2,1,0:T(8,128)(2,1)S(1)}, bf16[1,1,144,384]{3,2,1,0:T(8,128)(2,1)S(1)}, u32[]{:S(2)}, u32[]{:S(2)}) collective-permute-start(bf16[1,1,144,384]{3,2,1,0:T(8,128)(2,1)S(1)} %get-tuple-element.154), channel_id=1, source_target_pairs={{0,4},{4,0},{8,12},{12,8},{16,20},{20,16},{24,28},{28,24},{1,5},{5... | collective-permute-start | bytes 331784 | tf_op jit(solution)/shard_map/ppermute | solution.py:782
  172.0 9.4 %input_grad.1 = bf16[2,1200,512]{2,1,0:T(8,128)(2,1)} custom-call(bf16[512,1536]{1,0:T(8,128)(2,1)} %get-tuple-element.149.w_ref, bf16[2,1200,512]{2,1,0:T(8,128)(2,1)} %bitcast.21, bf16[2,768,1200]{2,1,0:T(8,128)(2,1)} %bitcast.18, bf16[2,768,1200]{2,1,0:T(8,128)(2,1)} %bitcast.19), custom_call_target="tpu_custom_call" | custom-call | flops 4000000000 | bytes 16000000 | tf_op jit(solution)/shard_map/input_grad/pallas_call | solution.py:719
  181.5 1.9 collective-permute-start.15
  183.4 1.0 collective-permute-start.17
  184.5 1.8 collective-permute-done.15
  186.4 0.8 collective-permute-start.20
  187.2 2.0 collective-permute-start.16
  189.8 2.0 collective-permute-done.20
  192.3 6.4 %collective-permute-done.18 = bf16[1,1,144,384]{3,2,1,0:T(8,128)(2,1)S(1)} collective-permute-done((bf16[1,1,144,384]{3,2,1,0:T(8,128)(2,1)S(1)}, bf16[1,1,144,384]{3,2,1,0:T(8,128)(2,1)S(1)}, u32[]{:S(2)}, u32[]{:S(2)}) %collective-permute-start.18) | collective-permute-done | bytes 110624 | tf_op jit(solution)/shard_map/ppermute | solution.py:782
  198.9 1.1 collective-permute-done.21
  200.0 1.0 collective-permute-start.22
  201.0 2.6 %collective-permute-done.19.refs_3_ = bf16[1,144,384]{2,1,0:T(8,128)(2,1)S(1)} collective-permute-done((bf16[1,144,384]{2,1,0:T(8,128)(2,1)S(1)}, bf16[1,144,384]{2,1,0:T(8,128)(2,1)S(1)}, u32[]{:S(2)}, u32[]{:S(2)}) %collective-permute-start.19) | collective-permute-done | bytes 110624 | tf_op jit(solution)/shard_map/ppermute | solution.py:782
  203.6 1.2 collective-permute-done.22.refs_5_
  205.6 2.6 %finish.1 = (f32[128,512]{1,0:T(8,128)}, f32[128,512]{1,0:T(8,128)}, f32[128,512]{1,0:T(8,128)}, f32[128,512]{1,0:T(8,128)}, f32[128,512]{1,0:T(8,128)}, /*index...) custom-call(bf16[144,1536]{1,0:T(8,128)(2,1)} %bitcast.14, ...), custom_call_target="tpu_custom_call" | custom-call | tf_op jit(solution)/shard_map/finish/pallas_call | solution.py:770
  (69 shorter events, 4.2 us)
Async XLA Ops:
  2.9 12.7 %collective-permute-start = (bf16[400,512]{1,0:T(8,128)(2,1)}, bf16[400,512]{1,0:T(8,128)(2,1)S(1)}, u32[]{:S(2)}, u32[]{:S(2)}) collective-permute-start(bf16[400,512]{1,0:T(8,128)(2,1)} %get-tuple-element.100.refs_1_), channel_id=1, source_target_pairs={{0,2},{1,3},{2,0},{3,1},{4,6},{5,7},{6,4},{7,5},{8,10},{9,11},{10,... | collective-permute-start | bytes 1228808 | tf_op jit(solution)/shard_map/ppermute | solution.py:782
  6.0 11.9 %collective-permute-start.4 = (bf16[400,512]{1,0:T(8,128)(2,1)}, bf16[400,512]{1,0:T(8,128)(2,1)S(1)}, u32[]{:S(2)}, u32[]{:S(2)}) collective-permute-start(bf16[400,512]{1,0:T(8,128)(2,1)} %get-tuple-element.100.refs_1_), channel_id=1, source_target_pairs={{0,1},{1,0},{2,3},{3,2},{4,5},{5,4},{6,7},{7,6},{8,9},{9,8},{10,11... | collective-permute-start | bytes 1228808 | tf_op jit(solution)/shard_map/ppermute | solution.py:782
  6.0 9.7 %copy-start.10 = (bf16[384,512]{1,0:T(8,128)(2,1)S(1)}, bf16[384,512]{1,0:T(8,128)(2,1)}, u32[]{:S(2)}) copy-start(bf16[384,512]{1,0:T(8,128)(2,1)} %get-tuple-element.104.refs_1_) | copy-start | bytes 1179652
  15.7 2.2 %copy-start.7 = (bf16[400,512]{1,0:T(8,128)(2,1)}, bf16[400,512]{1,0:T(8,128)(2,1)S(1)}, u32[]{:S(2)}) copy-start(bf16[400,512]{1,0:T(8,128)(2,1)S(1)} %collective-permute-done.refs_2_) | copy-start | bytes 1228804
  15.7 2.2 %collective-permute-start.5 = (bf16[400,512]{1,0:T(8,128)(2,1)S(1)}, bf16[400,512]{1,0:T(8,128)(2,1)S(1)}, u32[]{:S(2)}, u32[]{:S(2)}) collective-permute-start(bf16[400,512]{1,0:T(8,128)(2,1)S(1)} %collective-permute-done.refs_2_), channel_id=1, source_target_pairs={{0,1},{1,0},{2,3},{3,2},{4,5},{5,4},{6,7},{7,6},{8,9},{9,8},{10,11... | collective-permute-start | bytes 1228808 | tf_op jit(solution)/shard_map/ppermute | solution.py:782
  15.7 60.3 %collective-permute-start.1 = (bf16[384,512]{1,0:T(8,128)(2,1)S(1)}, bf16[384,512]{1,0:T(8,128)(2,1)S(1)}, u32[]{:S(2)}, u32[]{:S(2)}) collective-permute-start(bf16[384,512]{1,0:T(8,128)(2,1)S(1)} %copy-done.10), channel_id=1, source_target_pairs={{0,2},{1,3},{2,0},{3,1},{4,6},{5,7},{6,4},{7,5},{8,10},{9,11},{10,... | collective-permute-start | bytes 1179656 | tf_op jit(solution)/shard_map/ppermute | solution.py:782
  17.5 58.5 %collective-permute-start.2 = (bf16[384,512]{1,0:T(8,128)(2,1)S(1)}, bf16[384,512]{1,0:T(8,128)(2,1)S(1)}, u32[]{:S(2)}, u32[]{:S(2)}) collective-permute-start(bf16[384,512]{1,0:T(8,128)(2,1)S(1)} %copy-done.10), channel_id=1, source_target_pairs={{0,1},{1,0},{2,3},{3,2},{4,5},{5,4},{6,7},{7,6},{8,9},{9,8},{10,11... | collective-permute-start | bytes 1179656 | tf_op jit(solution)/shard_map/ppermute | solution.py:782
  17.6 58.4 %collective-permute-start.3 = (bf16[384,512]{1,0:T(8,128)(2,1)S(1)}, bf16[384,512]{1,0:T(8,128)(2,1)S(1)}, u32[]{:S(2)}, u32[]{:S(2)}) collective-permute-start(bf16[384,512]{1,0:T(8,128)(2,1)S(1)} %copy-done.10), channel_id=1, source_target_pairs={{0,3},{1,2},{2,1},{3,0},{4,7},{5,6},{6,5},{7,4},{8,11},{9,10},{10,... | collective-permute-start | bytes 1179656 | tf_op jit(solution)/shard_map/ppermute | solution.py:782
  17.9 0.9 copy-start.9
  76.0 1.0 copy-start.13
  102.4 2.7 %collective-permute-start.6 = (bf16[2,144,1536]{2,1,0:T(8,128)(2,1)}, bf16[2,144,1536]{2,1,0:T(8,128)(2,1)S(1)}, u32[]{:S(2)}, u32[]{:S(2)}) collective-permute-start(bf16[2,144,1536]{2,1,0:T(8,128)(2,1)} %get-tuple-element.116), channel_id=1, source_target_pairs={{0,1},{1,0},{2,3},{3,2},{4,5},{5,4},{6,7},{7,6},{8,9},{9,8},{10,11... | collective-permute-start | bytes 2654216 | tf_op jit(solution)/shard_map/ppermute | solution.py:782
  106.5 25.7 %collective-permute-start.7 = (bf16[1,144,1536]{2,1,0:T(8,128)(2,1)S(1)}, bf16[1,144,1536]{2,1,0:T(8,128)(2,1)S(1)}, u32[]{:S(2)}, u32[]{:S(2)}) collective-permute-start(bf16[1,144,1536]{2,1,0:T(8,128)(2,1)S(1)} %get-tuple-element.118), channel_id=1, source_target_pairs={{0,2},{1,3},{2,0},{3,1},{4,6},{5,7},{6,4},{7,5},{8,10},{9,11},{10,... | collective-permute-start | bytes 1327112 | tf_op jit(solution)/shard_map/ppermute | solution.py:782
  132.4 2.1 collective-permute-start.8
  135.6 30.4 %collective-permute-start.9 = (bf16[1,144,1536]{2,1,0:T(8,128)(2,1)S(1)}, bf16[1,144,1536]{2,1,0:T(8,128)(2,1)S(1)}, u32[]{:S(2)}, u32[]{:S(2)}) collective-permute-start(bf16[1,144,1536]{2,1,0:T(8,128)(2,1)S(1)} %add_convert_fusion.5), channel_id=1, source_target_pairs={{0,16},{4,20},{8,24},{12,28},{16,0},{20,4},{24,8},{28,12},{1,17},{... | collective-permute-start | bytes 1327112 | tf_op jit(solution)/shard_map/ppermute | solution.py:782
  140.0 25.9 %collective-permute-start.10 = (bf16[1,2,144,384]{3,2,1,0:T(8,128)(2,1)S(1)}, bf16[1,2,144,384]{3,2,1,0:T(8,128)(2,1)S(1)}, u32[]{:S(2)}, u32[]{:S(2)}) collective-permute-start(bf16[1,2,144,384]{3,2,1,0:T(8,128)(2,1)S(1)} %get-tuple-element.139), channel_id=1, source_target_pairs={{0,2},{1,3},{2,0},{3,1},{4,6},{5,7},{6,4},{7,5},{8,10},{9,11},{10,... | collective-permute-start | bytes 663560 | tf_op jit(solution)/shard_map/ppermute | solution.py:782
  165.8 2.3 %copy-start.2 = (bf16[2,2,144,384]{3,2,1,0:T(8,128)(2,1)S(1)}, bf16[2,2,144,384]{3,2,1,0:T(8,128)(2,1)}, u32[]{:S(2)}) copy-start(bf16[2,2,144,384]{3,2,1,0:T(8,128)(2,1)} %get-tuple-element.147) | copy-start | bytes 1327108
  166.1 2.1 collective-permute-start.11
  168.3 13.1 %collective-permute-start.12 = (bf16[1,144,1536]{2,1,0:T(8,128)(2,1)S(1)}, bf16[1,144,1536]{2,1,0:T(8,128)(2,1)S(1)}, u32[]{:S(2)}, u32[]{:S(2)}) collective-permute-start(bf16[1,144,1536]{2,1,0:T(8,128)(2,1)S(1)} %add_convert_fusion.3), channel_id=1, source_target_pairs={{0,8},{4,12},{8,0},{12,4},{16,24},{20,28},{24,16},{28,20},{1,9},{5... | collective-permute-start | bytes 1327112 | tf_op jit(solution)/shard_map/ppermute | solution.py:782
  169.8 11.6 %collective-permute-start.13 = (bf16[1,1,144,384]{3,2,1,0:T(8,128)(2,1)S(1)}, bf16[1,1,144,384]{3,2,1,0:T(8,128)(2,1)S(1)}, u32[]{:S(2)}, u32[]{:S(2)}) collective-permute-start(bf16[1,1,144,384]{3,2,1,0:T(8,128)(2,1)S(1)} %get-tuple-element.154), channel_id=1, source_target_pairs={{0,4},{4,0},{8,12},{12,8},{16,20},{20,16},{24,28},{28,24},{1,5},{5... | collective-permute-start | bytes 331784 | tf_op jit(solution)/shard_map/ppermute | solution.py:782
  171.9 9.4 %collective-permute-start.14 = (bf16[1,2,144,384]{3,2,1,0:T(8,128)(2,1)S(1)}, bf16[1,2,144,384]{3,2,1,0:T(8,128)(2,1)S(1)}, u32[]{:S(2)}, u32[]{:S(2)}) collective-permute-start(bf16[1,2,144,384]{3,2,1,0:T(8,128)(2,1)S(1)} %get-tuple-element.155), channel_id=1, source_target_pairs={{0,2},{1,3},{2,0},{3,1},{4,6},{5,7},{6,4},{7,5},{8,10},{9,11},{10,... | collective-permute-start | bytes 663560 | tf_op jit(solution)/shard_map/ppermute | solution.py:782
  181.5 4.8 %collective-permute-start.15 = (bf16[1,1,144,384]{3,2,1,0:T(8,128)(2,1)S(1)}, bf16[1,1,144,384]{3,2,1,0:T(8,128)(2,1)S(1)}, u32[]{:S(2)}, u32[]{:S(2)}) collective-permute-start(bf16[1,1,144,384]{3,2,1,0:T(8,128)(2,1)S(1)} %broadcast_select_fusion), channel_id=1, source_target_pairs={{0,4},{4,0},{8,12},{12,8},{16,20},{20,16},{24,28},{28,24},{1,5},{5... | collective-permute-start | bytes 331784 | tf_op jit(solution)/shard_map/ppermute | solution.py:782
  183.4 5.8 %collective-permute-start.17 = (bf16[1,1,144,384]{3,2,1,0:T(8,128)(2,1)S(1)}, bf16[1,1,144,384]{3,2,1,0:T(8,128)(2,1)S(1)}, u32[]{:S(2)}, u32[]{:S(2)}) collective-permute-start(bf16[1,1,144,384]{3,2,1,0:T(8,128)(2,1)S(1)} %add_convert_fusion.12), channel_id=1, source_target_pairs={{0,8},{4,12},{8,0},{12,4},{16,24},{20,28},{24,16},{28,20},{1,9},{5... | collective-permute-start | bytes 331784 | tf_op jit(solution)/shard_map/ppermute | solution.py:782
  184.5 20.3 %copy-start = (bf16[1,144,1536]{2,1,0:T(8,128)(2,1)}, bf16[1,144,1536]{2,1,0:T(8,128)(2,1)S(1)}, u32[]{:S(2)}) copy-start(bf16[1,144,1536]{2,1,0:T(8,128)(2,1)S(1)} %add_convert_fusion.1) | copy-start | bytes 1327108
  186.4 5.5 %collective-permute-start.20 = (bf16[1,1,144,384]{3,2,1,0:T(8,128)(2,1)S(1)}, bf16[1,1,144,384]{3,2,1,0:T(8,128)(2,1)S(1)}, u32[]{:S(2)}, u32[]{:S(2)}) collective-permute-start(bf16[1,1,144,384]{3,2,1,0:T(8,128)(2,1)S(1)} %add_convert_fusion.13), channel_id=1, source_target_pairs={{0,8},{4,12},{8,0},{12,4},{16,24},{20,28},{24,16},{28,20},{1,9},{5... | collective-permute-start | bytes 331784 | tf_op jit(solution)/shard_map/ppermute | solution.py:782
  187.2 17.6 %collective-permute-start.16 = (bf16[1,144,1536]{2,1,0:T(8,128)(2,1)S(1)}, bf16[1,144,1536]{2,1,0:T(8,128)(2,1)S(1)}, u32[]{:S(2)}, u32[]{:S(2)}) collective-permute-start(bf16[1,144,1536]{2,1,0:T(8,128)(2,1)S(1)} %add_convert_fusion.1), channel_id=1, source_target_pairs={{0,4},{4,0},{8,12},{12,8},{16,20},{20,16},{24,28},{28,24},{1,5},{5... | collective-permute-start | bytes 1327112 | tf_op jit(solution)/shard_map/ppermute | solution.py:782
  189.2 9.5 %collective-permute-start.18 = (bf16[1,1,144,384]{3,2,1,0:T(8,128)(2,1)S(1)}, bf16[1,1,144,384]{3,2,1,0:T(8,128)(2,1)S(1)}, u32[]{:S(2)}, u32[]{:S(2)}) collective-permute-start(bf16[1,1,144,384]{3,2,1,0:T(8,128)(2,1)S(1)} %add_convert_fusion.11), channel_id=1, source_target_pairs={{0,16},{4,20},{8,24},{12,28},{16,0},{20,4},{24,8},{28,12},{1,17},{... | collective-permute-start | bytes 331784 | tf_op jit(solution)/shard_map/ppermute | solution.py:782
  191.9 8.1 %collective-permute-start.21 = (bf16[1,1,144,384]{3,2,1,0:T(8,128)(2,1)S(1)}, bf16[1,1,144,384]{3,2,1,0:T(8,128)(2,1)S(1)}, u32[]{:S(2)}, u32[]{:S(2)}) collective-permute-start(bf16[1,1,144,384]{3,2,1,0:T(8,128)(2,1)S(1)} %add_convert_fusion.9), channel_id=1, source_target_pairs={{0,16},{4,20},{8,24},{12,28},{16,0},{20,4},{24,8},{28,12},{1,17},{... | collective-permute-start | bytes 331784 | tf_op jit(solution)/shard_map/ppermute | solution.py:782
  198.8 6.0 %copy-start.3 = (bf16[1,144,384]{2,1,0:T(8,128)(2,1)}, bf16[1,144,384]{2,1,0:T(8,128)(2,1)S(1)}, u32[]{:S(2)}) copy-start(bf16[1,144,384]{2,1,0:T(8,128)(2,1)S(1)} %fusion.refs_2_) | copy-start | bytes 331780
  198.8 4.8 %collective-permute-start.19 = (bf16[1,144,384]{2,1,0:T(8,128)(2,1)S(1)}, bf16[1,144,384]{2,1,0:T(8,128)(2,1)S(1)}, u32[]{:S(2)}, u32[]{:S(2)}) collective-permute-start(bf16[1,144,384]{2,1,0:T(8,128)(2,1)S(1)} %fusion.refs_2_), channel_id=1, source_target_pairs={{0,4},{4,0},{8,12},{12,8},{16,20},{20,16},{24,28},{28,24},{1,5},{5... | collective-permute-start | bytes 331784 | tf_op jit(solution)/shard_map/ppermute | solution.py:782
  200.0 4.8 %copy-start.4 = (bf16[1,144,384]{2,1,0:T(8,128)(2,1)}, bf16[1,144,384]{2,1,0:T(8,128)(2,1)S(1)}, u32[]{:S(2)}) copy-start(bf16[1,144,384]{2,1,0:T(8,128)(2,1)S(1)} %fusion.1.refs_4_) | copy-start | bytes 331780
  200.0 4.8 %collective-permute-start.22 = (bf16[1,144,384]{2,1,0:T(8,128)(2,1)S(1)}, bf16[1,144,384]{2,1,0:T(8,128)(2,1)S(1)}, u32[]{:S(2)}, u32[]{:S(2)}) collective-permute-start(bf16[1,144,384]{2,1,0:T(8,128)(2,1)S(1)} %fusion.1.refs_4_), channel_id=1, source_target_pairs={{0,4},{4,0},{8,12},{12,8},{16,20},{20,16},{24,28},{28,24},{1,5},{5... | collective-permute-start | bytes 331784 | tf_op jit(solution)/shard_map/ppermute | solution.py:782
  203.6 1.2 copy-start.5
  (5 other events, 3.8 us)

commit v4 on v3

--- a/solution.py
+++ b/solution.py
@@ -28,7 +28,6 @@
 
 F32 = jnp.float32
 BF16 = jnp.bfloat16
-VMEM_LIMIT = 60 << 20
 
 SQUARES = (2, 4, 5, 7, 11, 13)
 VECTORS = (3, 6, 8, 9, 10, 12, 14, 15, 16)
@@ -41,8 +40,8 @@
     )
 
 
-def params():
-    return pltpu.CompilerParams(vmem_limit_bytes=VMEM_LIMIT)
+def params(mebibytes):
+    return pltpu.CompilerParams(vmem_limit_bytes=mebibytes << 20)
 
 
 def cost(flops, moved):
@@ -88,7 +87,7 @@
         ),
         in_specs=[vmem] * 16,
         out_specs=[vmem, vmem, pl.BlockSpec(memory_space=pltpu.SMEM)],
-        compiler_params=params(),
+        compiler_params=params(60),
         name="pack",
     )(flags, *squares, *vectors)
 
@@ -135,7 +134,7 @@
             in_specs=[pl.BlockSpec(flags.shape, lambda i, s: (0, 0)), one(length, width)],
             out_specs=[one(padded, width), one(width + ONES, length), one(1, length)],
         ),
-        compiler_params=params(),
+        compiler_params=params(60),
         cost_estimate=cost(cells * 2e9, cells * 6e6),
         name="gather_known",
     )(scalars, flags, x)
@@ -368,7 +367,7 @@
                 pltpu.VMEM((2, CHUNK, length), BF16),
             ],
         ),
-        compiler_params=params(),
+        compiler_params=params(52),
         cost_estimate=cost(cells * 1e10, cells * 2.5e7),
         name="attend",
     )(scalars, *pieces, xt, xc, pos)
@@ -504,7 +503,7 @@
                 pltpu.VMEM((EXTRA, width), F32),
             ],
         ),
-        compiler_params=params(),
+        compiler_params=params(50),
         cost_estimate=cost(rows * 5e6, rows * 8e3),
         name="middle",
     )(scalars, *pieces, x, o, cot, vec)
@@ -695,7 +694,7 @@
                 pltpu.VMEM((2, CHUNK, length), BF16),
             ],
         ),
-        compiler_params=params(),
+        compiler_params=params(51),
         cost_estimate=cost(cells * count * 6e9, cells * count * 7e6),
         name="attend_back",
     )(scalars, pos, xt, qkv, kct, vc, e, more, top, ot, lse, own, datt)
@@ -723,7 +722,7 @@
         in_specs=[pl.BlockSpec(w.shape, lambda i: (0, 0)), block]
         + [pl.BlockSpec((1,) + part.shape[1:], lambda i: (i, 0, 0)) for part in parts],
         out_specs=block,
-        compiler_params=params(),
+        compiler_params=params(28),
         cost_estimate=cost(cells * 2e9, cells * 8e6),
         name="input_grad",
     )(w, dhid, *parts)
@@ -772,7 +771,7 @@
         out_shape=(jax.ShapeDtypeStruct((block, width), F32),) * 6 + (jax.ShapeDtypeStruct((block,), F32),) * 9,
         in_specs=[vmem] * len(parts),
         out_specs=[vmem] * 15,
-        compiler_params=params(),
+        compiler_params=params(16),
         name="finish",
     )(*parts)
 

time: 211 us -> 203 us (0.962)
  Pallas kernels: 155 us -> 120 us
  starting transfers between devices: 21.5 us -> 52.2 us
  other arithmetic: 3.3 us -> 1.18 us
    ppermute x23, starting transfers between devices: 21.5 us -> 52.2 us  [swap(): return lax.ppermute(values, axis, [(i, i ^ mask) for i in range(size)])]
    pallas_call x1, Pallas kernels: 57.2 us -> 27.9 us  [attend(): pl.pallas_call(functools.partial(attend_kernel, held=held, cells=cells),...]
    pallas_call x1, Pallas kernels: 9.4 us -> 5.86 us  [input_grad(): pl.pallas_call(input_kernel, out_shape=jax.ShapeDtypeStruct(dhid.shape, B...]
    convert_element_type x12, other arithmetic: 3.19 us -> 1.07 us  [arrive(): total = plus(self.keep, self.arrived).astype(BF16)]
  transfers between devices with their start and end apart: 23 -> 23, of which waited for: 10 -> 11; matrix products, arithmetic and copies ran while one was open for 0% -> 0% of each run, Pallas kernels for 60% -> 46%
where the time goes in v4:
time: 203 us; the launch traced here: 200 us
  Pallas kernels  120 us (59%)
  starting transfers between devices  52.2 us (26%)
  waiting for transfers between devices  22.7 us (11%)
  local copies, waits for them, and re-layouts  2.99 us (1%)
    ppermute x23, starting transfers between devices, swap(): return lax.ppermute(values, axis, [(i, i ^ mask) for i in range(size)])  52.2 us
    pallas_call x2, Pallas kernels, attend_back(): pl.pallas_call(functools.partial(back_kernel, shards=shards, cells=cells,...  51.3 us
    pallas_call x1, Pallas kernels, attend(): pl.pallas_call(functools.partial(attend_kernel, held=held, cells=cells),...  27.9 us
    pallas_call x1, Pallas kernels, middle(): pl.pallas_call(functools.partial(middle_kernel, held=held, cells=cells),...  23.9 us
    ppermute x23, waiting for transfers between devices, swap(): return lax.ppermute(values, axis, [(i, i ^ mask) for i in range(size)])  22.7 us
    pallas_call x1, Pallas kernels, gather_known(): pl.pallas_call(gather_kernel, out_shape=(jax.ShapeDtypeStruct((cells, pad...  6.97 us
    pallas_call x1, Pallas kernels, input_grad(): pl.pallas_call(input_kernel, out_shape=jax.ShapeDtypeStruct(dhid.shape, B...  5.86 us
  transfers between devices with their start and end apart: 23, of which 11 were waited for; matrix products, arithmetic and copies ran while one was open for 0% of the time, Pallas kernels for 46%

profile of v4, /device:TPU:0, one launch (start us, length us, event | category | flops | bytes accessed | tf_op | source)
XLA Modules:
  0.0 199.7 jit_solution(9894714591445352150)
XLA Ops:
  0.7 2.2 %pack.1 = (bf16[400,512]{1,0:T(8,128)(2,1)}, bf16[384,512]{1,0:T(8,128)(2,1)}, s32[3]{0:T(128)}) custom-call(s32[2,1200]{1,0:T(2,128)} %flags_ref.1, bf16[128,512]{1,0:T(8,128)(2,1)} %refs_1_.1, bf16[128,512]{1,0:T(8,128)(2,1)} %refs_2_.1, bf16[128,512]{1,0:T(8,128)(2,1)} %refs_3_.1, bf16[128,512]{1,0:T(8,128)(2,1)} %refs_4_.1, bf16[128,512]{1,0:T(8,128)(2,1)} %refs_5_.1, ...), custom_call_target="tpu_custom_call" | custom-call | tf_op jit(solution)/shard_map/pack/pallas_call | solution.py:81
  2.9 3.0 %collective-permute-start = (bf16[400,512]{1,0:T(8,128)(2,1)}, bf16[400,512]{1,0:T(8,128)(2,1)S(1)}, u32[]{:S(2)}, u32[]{:S(2)}) collective-permute-start(bf16[400,512]{1,0:T(8,128)(2,1)} %get-tuple-element.100.refs_1_), channel_id=1, source_target_pairs={{0,2},{1,3},{2,0},{3,1},{4,6},{5,7},{6,4},{7,5},{8,10},{9,11},{10,... | collective-permute-start | bytes 1228808 | tf_op jit(solution)/shard_map/ppermute | solution.py:781
  5.9 7.0 %gather_known.1 = (bf16[2,1344,512]{2,1,0:T(8,128)(2,1)}, bf16[2,528,1200]{2,1,0:T(8,128)(2,1)}, s32[2,1,1200]{2,1,0:T(1,128)}) custom-call(s32[3]{0:T(128)} %get-tuple-element.140.scalars_ref.refs_0_, s32[2,1200]{1,0:T(2,128)} %flags_ref.1, bf16[2,1200,512]{2,1,0:T(8,128)(2,1)} %x_ref.1), custom_call_target="tpu_custom_call" | custom-call | flops 4000000000 | bytes 12000000 | tf_op jit(solution)/shard_map/gather_known/pallas_call | solution.py:124
  12.9 2.7 %collective-permute-done.refs_2_ = bf16[400,512]{1,0:T(8,128)(2,1)S(1)} collective-permute-done((bf16[400,512]{1,0:T(8,128)(2,1)}, bf16[400,512]{1,0:T(8,128)(2,1)S(1)}, u32[]{:S(2)}, u32[]{:S(2)}) %collective-permute-start) | collective-permute-done | bytes 409632 | tf_op jit(solution)/shard_map/ppermute | solution.py:781
  15.6 1.7 collective-permute-start.1
  18.5 27.9 %attend.1 = (bf16[512,1536]{1,0:T(8,128)(2,1)}, f32[16,512]{1,0:T(8,128)S(1)}, bf16[2,4,384,1200]{3,2,1,0:T(8,128)(2,1)}, bf16[2,4,2,128,672]{4,3,2,1,0:T(8,128)...) custom-call(s32[3]{0:T(128)S(1)} %copy-done.2, ...), custom_call_target="tpu_custom_call" | custom-call | flops 20000000000 | bytes 50000000 | tf_op jit(solution)/shard_map/attend/pallas_call | solution.py:320
  46.4 23.9 %middle.1 = (bf16[2400,512]{1,0:T(8,128)(2,1)}, bf16[2400,512]{1,0:T(8,128)(2,1)}, bf16[2400,512]{1,0:T(8,128)(2,1)}, bf16[2,144,1536]{2,1,0:T(8,128)(2,1)S(1)}, bf16[2,144,1536]{2,1,0:T(8,128)(2,1)S(1)}) custom-call(s32[3]{0:T(128)S(1)} %copy-done.2, bf16[384,512]{1,0:T(8,128)(2,1)S(1)} %copy-done.1, bf16[384,512]{1,0:T(8,128)(2,1)S(1)} %collective-permute-done.1.refs_2_, ...), custom_call_target="tpu_custom_call" | custom-call | flops 12000000000 | bytes 19200000 | tf_op jit(solution)/shard_map/middle/pallas_call | solution.py:490
  70.4 7.7 %collective-permute-start.6 = (bf16[2,144,1536]{2,1,0:T(8,128)(2,1)S(1)}, bf16[2,144,1536]{2,1,0:T(8,128)(2,1)S(1)}, u32[]{:S(2)}, u32[]{:S(2)}) collective-permute-start(bf16[2,144,1536]{2,1,0:T(8,128)(2,1)S(1)} %get-tuple-element.116), channel_id=1, source_target_pairs={{0,1},{1,0},{2,3},{3,2},{4,5},{5,4},{6,7},{7,6},{8,9},{9,8},{10,11... | collective-permute-start | bytes 2654216 | tf_op jit(solution)/shard_map/ppermute | solution.py:781
  78.1 2.1 %collective-permute-done.6 = bf16[2,144,1536]{2,1,0:T(8,128)(2,1)S(1)} collective-permute-done((bf16[2,144,1536]{2,1,0:T(8,128)(2,1)S(1)}, bf16[2,144,1536]{2,1,0:T(8,128)(2,1)S(1)}, u32[]{:S(2)}, u32[]{:S(2)}) %collective-permute-start.6) | collective-permute-done | bytes 884768 | tf_op jit(solution)/shard_map/ppermute | solution.py:781
  80.5 25.4 %attend_back.2 = (bf16[2,2,384,1200]{3,2,1,0:T(8,128)(2,1)}, bf16[2,2,144,384]{3,2,1,0:T(8,128)(2,1)S(1)}, bf16[2,2,144,384]{3,2,1,0:T(8,128)(2,1)S(1)}) custom-call(s32[3]{0:T(128)S(1)} %copy-done.2, s32[2,1,1200]{2,1,0:T(1,128)S(1)} %copy-done.7, bf16[2,528,1200]{2,1,0:T(8,128)(2,1)} %get-tuple-element.101.refs_5_.xt_ref, ...), custom_call_target="tpu_custom_call" | custom-call | flops 24000000000 | bytes 28000000 | tf_op jit(solution)/shard_map/attend_back/pallas_call | solution.py:656
  106.5 1.4 collective-permute-done.8
  108.1 25.7 %collective-permute-start.9 = (bf16[1,144,1536]{2,1,0:T(8,128)(2,1)S(1)}, bf16[1,144,1536]{2,1,0:T(8,128)(2,1)S(1)}, u32[]{:S(2)}, u32[]{:S(2)}) collective-permute-start(bf16[1,144,1536]{2,1,0:T(8,128)(2,1)S(1)} %add_convert_fusion.5), channel_id=1, source_target_pairs={{0,16},{4,20},{8,24},{12,28},{16,0},{20,4},{24,8},{28,12},{1,17},{... | collective-permute-start | bytes 1327112 | tf_op jit(solution)/shard_map/ppermute | solution.py:781
  133.7 25.9 %attend_back.3 = (bf16[2,2,384,1200]{3,2,1,0:T(8,128)(2,1)}, bf16[2,2,144,384]{3,2,1,0:T(8,128)(2,1)S(1)}, bf16[2,2,144,384]{3,2,1,0:T(8,128)(2,1)S(1)}) custom-call(s32[3]{0:T(128)S(1)} %copy-done.2, s32[2,1,1200]{2,1,0:T(1,128)S(1)} %copy-done.8, bf16[2,528,1200]{2,1,0:T(8,128)(2,1)} %get-tuple-element.101.refs_5_.xt_ref, ...), custom_call_target="tpu_custom_call" | custom-call | flops 24000000000 | bytes 28000000 | tf_op jit(solution)/shard_map/attend_back/pallas_call | solution.py:656
  160.0 1.8 collective-permute-done.11
  161.9 2.0 collective-permute-start.12
  163.9 1.5 collective-permute-start.13
  165.5 2.1 %copy-done.4 = bf16[2,2,384,1200]{3,2,1,0:T(8,128)(2,1)S(1)} copy-done((bf16[2,2,384,1200]{3,2,1,0:T(8,128)(2,1)S(1)}, bf16[2,2,384,1200]{3,2,1,0:T(8,128)(2,1)}, u32[]{:S(2)}) %copy-start.4) | copy-done | bytes 3686424
  167.6 5.9 %input_grad.1 = bf16[2,1200,512]{2,1,0:T(8,128)(2,1)} custom-call(bf16[512,1536]{1,0:T(8,128)(2,1)S(1)} %copy-done.6, bf16[2,1200,512]{2,1,0:T(8,128)(2,1)S(1)} %bitcast.18, bf16[2,768,1200]{2,1,0:T(8,128)(2,1)S(1)} %bitcast.16, bf16[2,768,1200]{2,1,0:T(8,128)(2,1)S(1)} %bitcast.17), custom_call_target="tpu_custom_call" | custom-call | flops 4000000000 | bytes 16000000 | tf_op jit(solution)/shard_map/input_grad/pallas_call | solution.py:718
  173.4 1.0 collective-permute-done.12
  174.5 1.6 collective-permute-start.15
  176.1 1.8 collective-permute-start.17
  178.0 1.3 collective-permute-done.15
  179.3 1.8 collective-permute-start.20
  181.1 1.5 collective-permute-start.16
  182.8 1.5 collective-permute-done.20
  184.3 1.4 collective-permute-start.21
  185.8 6.4 %collective-permute-done.18 = bf16[1,1,144,384]{3,2,1,0:T(8,128)(2,1)S(1)} collective-permute-done((bf16[1,1,144,384]{3,2,1,0:T(8,128)(2,1)S(1)}, bf16[1,1,144,384]{3,2,1,0:T(8,128)(2,1)S(1)}, u32[]{:S(2)}, u32[]{:S(2)}) %collective-permute-start.18) | collective-permute-done | bytes 110624 | tf_op jit(solution)/shard_map/ppermute | solution.py:781
  192.2 1.1 collective-permute-done.21
  193.3 1.3 collective-permute-start.22
  194.6 2.3 %collective-permute-done.19.refs_3_ = bf16[1,144,384]{2,1,0:T(8,128)(2,1)S(1)} collective-permute-done((bf16[1,144,384]{2,1,0:T(8,128)(2,1)S(1)}, bf16[1,144,384]{2,1,0:T(8,128)(2,1)S(1)}, u32[]{:S(2)}, u32[]{:S(2)}) %collective-permute-start.19) | collective-permute-done | bytes 110624 | tf_op jit(solution)/shard_map/ppermute | solution.py:781
  197.0 1.2 collective-permute-done.22.refs_5_
  198.2 1.3 finish.1
  (59 shorter events, 3.3 us)
Async XLA Ops:
  2.9 12.7 %collective-permute-start = (bf16[400,512]{1,0:T(8,128)(2,1)}, bf16[400,512]{1,0:T(8,128)(2,1)S(1)}, u32[]{:S(2)}, u32[]{:S(2)}) collective-permute-start(bf16[400,512]{1,0:T(8,128)(2,1)} %get-tuple-element.100.refs_1_), channel_id=1, source_target_pairs={{0,2},{1,3},{2,0},{3,1},{4,6},{5,7},{6,4},{7,5},{8,10},{9,11},{10,... | collective-permute-start | bytes 1228808 | tf_op jit(solution)/shard_map/ppermute | solution.py:781
  5.9 11.8 %collective-permute-start.4 = (bf16[400,512]{1,0:T(8,128)(2,1)}, bf16[400,512]{1,0:T(8,128)(2,1)S(1)}, u32[]{:S(2)}, u32[]{:S(2)}) collective-permute-start(bf16[400,512]{1,0:T(8,128)(2,1)} %get-tuple-element.100.refs_1_), channel_id=1, source_target_pairs={{0,1},{1,0},{2,3},{3,2},{4,5},{5,4},{6,7},{7,6},{8,9},{9,8},{10,11... | collective-permute-start | bytes 1228808 | tf_op jit(solution)/shard_map/ppermute | solution.py:781
  5.9 9.7 %copy-start.1 = (bf16[384,512]{1,0:T(8,128)(2,1)S(1)}, bf16[384,512]{1,0:T(8,128)(2,1)}, u32[]{:S(2)}) copy-start(bf16[384,512]{1,0:T(8,128)(2,1)} %get-tuple-element.104.refs_1_) | copy-start | bytes 1179652
  5.9 11.8 %copy-start = (bf16[400,512]{1,0:T(8,128)(2,1)S(1)}, bf16[400,512]{1,0:T(8,128)(2,1)}, u32[]{:S(2)}) copy-start(bf16[400,512]{1,0:T(8,128)(2,1)} %get-tuple-element.100.refs_1_) | copy-start | bytes 1228804
  5.9 11.8 %copy-start.2 = (s32[3]{0:T(128)S(1)}, s32[3]{0:T(128)}, u32[]{:S(2)}) copy-start(s32[3]{0:T(128)} %get-tuple-element.140.scalars_ref.refs_0_) | copy-start | bytes 40
  15.6 2.2 %collective-permute-start.5 = (bf16[400,512]{1,0:T(8,128)(2,1)S(1)}, bf16[400,512]{1,0:T(8,128)(2,1)S(1)}, u32[]{:S(2)}, u32[]{:S(2)}) collective-permute-start(bf16[400,512]{1,0:T(8,128)(2,1)S(1)} %collective-permute-done.refs_2_), channel_id=1, source_target_pairs={{0,1},{1,0},{2,3},{3,2},{4,5},{5,4},{6,7},{7,6},{8,9},{9,8},{10,11... | collective-permute-start | bytes 1228808 | tf_op jit(solution)/shard_map/ppermute | solution.py:781
  15.6 30.8 %collective-permute-start.1 = (bf16[384,512]{1,0:T(8,128)(2,1)S(1)}, bf16[384,512]{1,0:T(8,128)(2,1)S(1)}, u32[]{:S(2)}, u32[]{:S(2)}) collective-permute-start(bf16[384,512]{1,0:T(8,128)(2,1)S(1)} %copy-done.1), channel_id=1, source_target_pairs={{0,2},{1,3},{2,0},{3,1},{4,6},{5,7},{6,4},{7,5},{8,10},{9,11},{10,... | collective-permute-start | bytes 1179656 | tf_op jit(solution)/shard_map/ppermute | solution.py:781
  17.4 29.1 %collective-permute-start.2 = (bf16[384,512]{1,0:T(8,128)(2,1)S(1)}, bf16[384,512]{1,0:T(8,128)(2,1)S(1)}, u32[]{:S(2)}, u32[]{:S(2)}) collective-permute-start(bf16[384,512]{1,0:T(8,128)(2,1)S(1)} %copy-done.1), channel_id=1, source_target_pairs={{0,1},{1,0},{2,3},{3,2},{4,5},{5,4},{6,7},{7,6},{8,9},{9,8},{10,11... | collective-permute-start | bytes 1179656 | tf_op jit(solution)/shard_map/ppermute | solution.py:781
  17.6 28.8 %collective-permute-start.3 = (bf16[384,512]{1,0:T(8,128)(2,1)S(1)}, bf16[384,512]{1,0:T(8,128)(2,1)S(1)}, u32[]{:S(2)}, u32[]{:S(2)}) collective-permute-start(bf16[384,512]{1,0:T(8,128)(2,1)S(1)} %copy-done.1), channel_id=1, source_target_pairs={{0,3},{1,2},{2,1},{3,0},{4,7},{5,6},{6,5},{7,4},{8,11},{9,10},{10,... | collective-permute-start | bytes 1179656 | tf_op jit(solution)/shard_map/ppermute | solution.py:781
  17.8 0.7 copy-start.7
  70.4 9.7 %collective-permute-start.6 = (bf16[2,144,1536]{2,1,0:T(8,128)(2,1)S(1)}, bf16[2,144,1536]{2,1,0:T(8,128)(2,1)S(1)}, u32[]{:S(2)}, u32[]{:S(2)}) collective-permute-start(bf16[2,144,1536]{2,1,0:T(8,128)(2,1)S(1)} %get-tuple-element.116), channel_id=1, source_target_pairs={{0,1},{1,0},{2,3},{3,2},{4,5},{5,4},{6,7},{7,6},{8,9},{9,8},{10,11... | collective-permute-start | bytes 2654216 | tf_op jit(solution)/shard_map/ppermute | solution.py:781
  80.4 25.5 %collective-permute-start.7 = (bf16[1,144,1536]{2,1,0:T(8,128)(2,1)S(1)}, bf16[1,144,1536]{2,1,0:T(8,128)(2,1)S(1)}, u32[]{:S(2)}, u32[]{:S(2)}) collective-permute-start(bf16[1,144,1536]{2,1,0:T(8,128)(2,1)S(1)} %get-tuple-element.118), channel_id=1, source_target_pairs={{0,2},{1,3},{2,0},{3,1},{4,6},{5,7},{6,4},{7,5},{8,10},{9,11},{10,... | collective-permute-start | bytes 1327112 | tf_op jit(solution)/shard_map/ppermute | solution.py:781
  105.9 27.8 %copy-start.8 = (s32[2,1,1200]{2,1,0:T(1,128)S(1)}, s32[2,1,1200]{2,1,0:T(1,128)}, u32[]{:S(2)}) copy-start(s32[2,1,1200]{2,1,0:T(1,128)} %get-tuple-element.108.refs_7_.pos_ref) | copy-start | bytes 28804
  106.0 1.9 collective-permute-start.8
  108.1 51.7 %collective-permute-start.9 = (bf16[1,144,1536]{2,1,0:T(8,128)(2,1)S(1)}, bf16[1,144,1536]{2,1,0:T(8,128)(2,1)S(1)}, u32[]{:S(2)}, u32[]{:S(2)}) collective-permute-start(bf16[1,144,1536]{2,1,0:T(8,128)(2,1)S(1)} %add_convert_fusion.5), channel_id=1, source_target_pairs={{0,16},{4,20},{8,24},{12,28},{16,0},{20,4},{24,8},{28,12},{1,17},{... | collective-permute-start | bytes 1327112 | tf_op jit(solution)/shard_map/ppermute | solution.py:781
  133.7 26.0 %collective-permute-start.10 = (bf16[1,2,144,384]{3,2,1,0:T(8,128)(2,1)S(1)}, bf16[1,2,144,384]{3,2,1,0:T(8,128)(2,1)S(1)}, u32[]{:S(2)}, u32[]{:S(2)}) collective-permute-start(bf16[1,2,144,384]{3,2,1,0:T(8,128)(2,1)S(1)} %get-tuple-element.139), channel_id=1, source_target_pairs={{0,2},{1,3},{2,0},{3,1},{4,6},{5,7},{6,4},{7,5},{8,10},{9,11},{10,... | collective-permute-start | bytes 663560 | tf_op jit(solution)/shard_map/ppermute | solution.py:781
  133.7 31.7 %copy-start.5 = (bf16[2400,512]{1,0:T(8,128)(2,1)S(1)}, bf16[2400,512]{1,0:T(8,128)(2,1)}, u32[]{:S(2)}) copy-start(bf16[2400,512]{1,0:T(8,128)(2,1)} %get-tuple-element.150) | copy-start | bytes 7372804
  133.7 31.7 %copy-start.6 = (bf16[512,1536]{1,0:T(8,128)(2,1)S(1)}, bf16[512,1536]{1,0:T(8,128)(2,1)}, u32[]{:S(2)}) copy-start(bf16[512,1536]{1,0:T(8,128)(2,1)} %get-tuple-element.149.w_ref) | copy-start | bytes 4718596
  159.7 5.8 %copy-start.3 = (bf16[2,2,384,1200]{3,2,1,0:T(8,128)(2,1)S(1)}, bf16[2,2,384,1200]{3,2,1,0:T(8,128)(2,1)}, u32[]{:S(2)}) copy-start(bf16[2,2,384,1200]{3,2,1,0:T(8,128)(2,1)} %get-tuple-element.151) | copy-start | bytes 11059204
  159.9 1.9 collective-permute-start.11
  161.9 12.4 %collective-permute-start.12 = (bf16[1,144,1536]{2,1,0:T(8,128)(2,1)S(1)}, bf16[1,144,1536]{2,1,0:T(8,128)(2,1)S(1)}, u32[]{:S(2)}, u32[]{:S(2)}) collective-permute-start(bf16[1,144,1536]{2,1,0:T(8,128)(2,1)S(1)} %add_convert_fusion.3), channel_id=1, source_target_pairs={{0,8},{4,12},{8,0},{12,4},{16,24},{20,28},{24,16},{28,20},{1,9},{5... | collective-permute-start | bytes 1327112 | tf_op jit(solution)/shard_map/ppermute | solution.py:781
  163.9 9.5 %collective-permute-start.13 = (bf16[1,1,144,384]{3,2,1,0:T(8,128)(2,1)S(1)}, bf16[1,1,144,384]{3,2,1,0:T(8,128)(2,1)S(1)}, u32[]{:S(2)}, u32[]{:S(2)}) collective-permute-start(bf16[1,1,144,384]{3,2,1,0:T(8,128)(2,1)S(1)} %get-tuple-element.154), channel_id=1, source_target_pairs={{0,4},{4,0},{8,12},{12,8},{16,20},{20,16},{24,28},{28,24},{1,5},{5... | collective-permute-start | bytes 331784 | tf_op jit(solution)/shard_map/ppermute | solution.py:781
  165.4 8.0 %collective-permute-start.14 = (bf16[1,2,144,384]{3,2,1,0:T(8,128)(2,1)S(1)}, bf16[1,2,144,384]{3,2,1,0:T(8,128)(2,1)S(1)}, u32[]{:S(2)}, u32[]{:S(2)}) collective-permute-start(bf16[1,2,144,384]{3,2,1,0:T(8,128)(2,1)S(1)} %get-tuple-element.155), channel_id=1, source_target_pairs={{0,2},{1,3},{2,0},{3,1},{4,6},{5,7},{6,4},{7,5},{8,10},{9,11},{10,... | collective-permute-start | bytes 663560 | tf_op jit(solution)/shard_map/ppermute | solution.py:781
  165.4 2.1 %copy-start.4 = (bf16[2,2,384,1200]{3,2,1,0:T(8,128)(2,1)S(1)}, bf16[2,2,384,1200]{3,2,1,0:T(8,128)(2,1)}, u32[]{:S(2)}) copy-start(bf16[2,2,384,1200]{3,2,1,0:T(8,128)(2,1)} %get-tuple-element.152) | copy-start | bytes 11059204
  174.5 4.8 %collective-permute-start.15 = (bf16[1,1,144,384]{3,2,1,0:T(8,128)(2,1)S(1)}, bf16[1,1,144,384]{3,2,1,0:T(8,128)(2,1)S(1)}, u32[]{:S(2)}, u32[]{:S(2)}) collective-permute-start(bf16[1,1,144,384]{3,2,1,0:T(8,128)(2,1)S(1)} %broadcast_select_fusion), channel_id=1, source_target_pairs={{0,4},{4,0},{8,12},{12,8},{16,20},{20,16},{24,28},{28,24},{1,5},{5... | collective-permute-start | bytes 331784 | tf_op jit(solution)/shard_map/ppermute | solution.py:781
  176.1 6.6 %collective-permute-start.17 = (bf16[1,1,144,384]{3,2,1,0:T(8,128)(2,1)S(1)}, bf16[1,1,144,384]{3,2,1,0:T(8,128)(2,1)S(1)}, u32[]{:S(2)}, u32[]{:S(2)}) collective-permute-start(bf16[1,1,144,384]{3,2,1,0:T(8,128)(2,1)S(1)} %add_convert_fusion.12), channel_id=1, source_target_pairs={{0,8},{4,12},{8,0},{12,4},{16,24},{20,28},{24,16},{28,20},{1,9},{5... | collective-permute-start | bytes 331784 | tf_op jit(solution)/shard_map/ppermute | solution.py:781
  179.3 5.0 %collective-permute-start.20 = (bf16[1,1,144,384]{3,2,1,0:T(8,128)(2,1)S(1)}, bf16[1,1,144,384]{3,2,1,0:T(8,128)(2,1)S(1)}, u32[]{:S(2)}, u32[]{:S(2)}) collective-permute-start(bf16[1,1,144,384]{3,2,1,0:T(8,128)(2,1)S(1)} %add_convert_fusion.13), channel_id=1, source_target_pairs={{0,8},{4,12},{8,0},{12,4},{16,24},{20,28},{24,16},{28,20},{1,9},{5... | collective-permute-start | bytes 331784 | tf_op jit(solution)/shard_map/ppermute | solution.py:781
  181.1 17.0 %collective-permute-start.16 = (bf16[1,144,1536]{2,1,0:T(8,128)(2,1)S(1)}, bf16[1,144,1536]{2,1,0:T(8,128)(2,1)S(1)}, u32[]{:S(2)}, u32[]{:S(2)}) collective-permute-start(bf16[1,144,1536]{2,1,0:T(8,128)(2,1)S(1)} %add_convert_fusion.1), channel_id=1, source_target_pairs={{0,4},{4,0},{8,12},{12,8},{16,20},{20,16},{24,28},{28,24},{1,5},{5... | collective-permute-start | bytes 1327112 | tf_op jit(solution)/shard_map/ppermute | solution.py:781
  182.7 9.5 %collective-permute-start.18 = (bf16[1,1,144,384]{3,2,1,0:T(8,128)(2,1)S(1)}, bf16[1,1,144,384]{3,2,1,0:T(8,128)(2,1)S(1)}, u32[]{:S(2)}, u32[]{:S(2)}) collective-permute-start(bf16[1,1,144,384]{3,2,1,0:T(8,128)(2,1)S(1)} %add_convert_fusion.11), channel_id=1, source_target_pairs={{0,16},{4,20},{8,24},{12,28},{16,0},{20,4},{24,8},{28,12},{1,17},{... | collective-permute-start | bytes 331784 | tf_op jit(solution)/shard_map/ppermute | solution.py:781
  184.3 9.0 %collective-permute-start.21 = (bf16[1,1,144,384]{3,2,1,0:T(8,128)(2,1)S(1)}, bf16[1,1,144,384]{3,2,1,0:T(8,128)(2,1)S(1)}, u32[]{:S(2)}, u32[]{:S(2)}) collective-permute-start(bf16[1,1,144,384]{3,2,1,0:T(8,128)(2,1)S(1)} %add_convert_fusion.9), channel_id=1, source_target_pairs={{0,16},{4,20},{8,24},{12,28},{16,0},{20,4},{24,8},{28,12},{1,17},{... | collective-permute-start | bytes 331784 | tf_op jit(solution)/shard_map/ppermute | solution.py:781
  192.2 4.8 %collective-permute-start.19 = (bf16[1,144,384]{2,1,0:T(8,128)(2,1)S(1)}, bf16[1,144,384]{2,1,0:T(8,128)(2,1)S(1)}, u32[]{:S(2)}, u32[]{:S(2)}) collective-permute-start(bf16[1,144,384]{2,1,0:T(8,128)(2,1)S(1)} %fusion.refs_2_), channel_id=1, source_target_pairs={{0,4},{4,0},{8,12},{12,8},{16,20},{20,16},{24,28},{28,24},{1,5},{5... | collective-permute-start | bytes 331784 | tf_op jit(solution)/shard_map/ppermute | solution.py:781
  193.3 4.8 %collective-permute-start.22 = (bf16[1,144,384]{2,1,0:T(8,128)(2,1)S(1)}, bf16[1,144,384]{2,1,0:T(8,128)(2,1)S(1)}, u32[]{:S(2)}, u32[]{:S(2)}) collective-permute-start(bf16[1,144,384]{2,1,0:T(8,128)(2,1)S(1)} %fusion.1.refs_4_), channel_id=1, source_target_pairs={{0,4},{4,0},{8,12},{12,8},{16,20},{20,16},{24,28},{28,24},{1,5},{5... | collective-permute-start | bytes 331784 | tf_op jit(solution)/shard_map/ppermute | solution.py:781

commit v5 on v4

--- a/solution.py
+++ b/solution.py
@@ -149,7 +149,7 @@
     pieces, refs = refs[: len(held)], refs[len(held) :]
     (
         xt_ref, xc_ref, pos_ref,
-        w_ref, vec_ref, qkv_ref, kct_ref, vc_ref, e_ref, more_ref, top_ref, ot_ref, o_ref, lse_ref, own_ref,
+        w_ref, vec_ref, qkv_ref, kvt_ref, e_ref, more_ref, stats_ref, o_ref,
         bias, qz, kc, vct, top, own, acc, spill,
     ) = refs
     cell, pair = pl.program_id(0), pl.program_id(1)
@@ -193,11 +193,11 @@
         row = chunk * CHUNK + lax.broadcasted_iota(jnp.int32, (CHUNK, LANES), 0)
         keys = packed[:, 0:LANES]
         kc[...] = keys.astype(BF16)
-        kct_ref[0, 0, chunk] = jnp.where(row < known, keys, 0.0).astype(BF16).T
+        kvt_ref[0, 0, chunk, 0:LANES, :] = jnp.where(row < known, keys, 0.0).astype(BF16).T
         yield
         values = packed[:, LANES:] + value_bias
-        vc_ref[0, 0, rows, :] = values.astype(BF16)
         values = jnp.where(row < known, values, 0.0).astype(BF16).T
+        kvt_ref[0, 0, chunk, LANES:, :] = values
         counted = chunk * CHUNK + lax.broadcasted_iota(jnp.int32, (EXTRA, CHUNK), 1)
         counted = jnp.where(counted < known, 1.0, 0.0).astype(BF16)
         for side in range(2):
@@ -224,22 +224,22 @@
 
     def conclude(side):
         total = acc[side, HD : HD + 1, :]
-        ot_ref[0, heads[side], :] = (acc[side, 0:HD, :] * (1.0 / total)).astype(BF16)
-        lse_ref[0, side] = top[side] + jnp.log(total)
-        own_ref[0, side] = own[side]
+        rows = slice(TRIPLE + side * HD, TRIPLE + (side + 1) * HD)
+        qkv_ref[0, 0, rows, :] = (acc[side, 0:HD, :] * (1.0 / total)).astype(BF16)
+        stats_ref[0, 0, side] = top[side] + jnp.log(total)
+        stats_ref[0, 0, 2 + side] = own[side]
 
     first = project(0)
     next(first)
     turned = dot(part(0, 1), tokens, 0, 0)
     next(first)
     queries = (turned + bias[pair, :, 0:1]).astype(BF16)
-    turned = dot(part(1, 1), tokens, 0, 0)
+    turned = dot(part(1, 2), tokens, 0, 0)
     qkv_ref[0, 0, 0:LANES, :] = queries
     for side in range(2):
         qz[side, heads[side], :] = queries[heads[side], :]
     next(first)
-    qkv_ref[0, 0, LANES : 2 * LANES, :] = turned.astype(BF16)
-    turned = dot(part(2, 1), tokens, 0, 0)
+    qkv_ref[0, 0, LANES : 2 * LANES, :] = turned[0:LANES, :].astype(BF16)
     weights = []
     safe = None
     for side in range(2):
@@ -247,7 +247,7 @@
             scores = dot(kc[...], qz[side, :, cut])
             e_ref[0, 0, side, :, cut] = jnp.exp2(scores * (SCALE * LOG2E)).astype(BF16)
             if side == 0 and cut is cuts[0]:
-                qkv_ref[0, 0, 2 * LANES :, :] = (turned + bias[pair, :, 1:2]).astype(BF16)
+                qkv_ref[0, 0, 2 * LANES : TRIPLE, :] = (turned[LANES:, :] + bias[pair, :, 1:2]).astype(BF16)
             if cut is cuts[1]:
                 bounded = measure(side)
                 safe = bounded if safe is None else safe & bounded
@@ -257,8 +257,8 @@
         acc[side, HD:, :] = total[HD:, :] + weights[side]
     for side in range(2):
         conclude(side)
-        top_ref[0, 0, 0, side] = top[side]
-    o_ref[0] = ot_ref[0].T
+        stats_ref[0, 0, 4 + side] = top[side]
+    o_ref[0] = qkv_ref[0, 0, TRIPLE:, :].T
 
     def weigh(chunk, side, exps, shifted):
         scores = dot(kc[...], qz[side]) * SCALE
@@ -273,7 +273,7 @@
             top[side] = peak
         else:
             acc[side] += dot(vct[side], probs)
-        top_ref[0, 0, chunk, side] = top[side]
+        stats_ref[0, 0, 4 + 2 * chunk + side] = top[side]
 
     @pl.when(jnp.logical_not(safe))
     def _():
@@ -306,7 +306,7 @@
     def _():
         for side in range(2):
             conclude(side)
-        o_ref[0] = ot_ref[0].T
+        o_ref[0] = qkv_ref[0, 0, TRIPLE:, :].T
 
 
 def attend(scalars, held, pieces, xt, xc, pos):
@@ -322,16 +322,12 @@
         out_shape=(
             shape((width, 3 * width), BF16),
             shape((EXTRA, width), F32),
-            shape((cells, pairs, TRIPLE, length), BF16),
-            shape((cells, pairs, chunks, LANES, CHUNK), BF16),
-            shape((cells, pairs, padded, LANES), BF16),
+            shape((cells, pairs, 4 * LANES, length), BF16),
+            shape((cells, pairs, chunks, 2 * LANES, CHUNK), BF16),
             shape((cells, pairs, 2, CHUNK, length), BF16),
             shape((cells, pairs, max(chunks - 1, 1), 2, CHUNK, length), BF16),
-            shape((cells, pairs, chunks, 2, 1, length), F32),
-            shape((cells, width, length), BF16),
+            shape((cells, pairs, 4 + 2 * chunks, 1, length), F32),
             shape((cells, length, width), BF16),
-            shape((cells, H, 1, length), F32),
-            shape((cells, H, 1, length), F32),
         ),
         grid_spec=pltpu.PrefetchScalarGridSpec(
             num_scalar_prefetch=1,
@@ -345,16 +341,12 @@
             out_specs=[
                 full(width, 3 * width),
                 full(EXTRA, width),
-                pl.BlockSpec((1, 1, TRIPLE, length), lambda c, p, s: (c, p, 0, 0)),
-                pl.BlockSpec((1, 1, chunks, LANES, CHUNK), lambda c, p, s: (c, p, 0, 0, 0)),
-                pl.BlockSpec((1, 1, padded, LANES), lambda c, p, s: (c, p, 0, 0)),
+                pl.BlockSpec((1, 1, 4 * LANES, length), lambda c, p, s: (c, p, 0, 0)),
+                pl.BlockSpec((1, 1, chunks, 2 * LANES, CHUNK), lambda c, p, s: (c, p, 0, 0, 0)),
                 pl.BlockSpec((1, 1, 2, CHUNK, length), lambda c, p, s: (c, p, 0, 0, 0)),
                 pl.BlockSpec(memory_space=pl.ANY),
-                pl.BlockSpec((1, 1, chunks, 2, 1, length), lambda c, p, s: (c, p, 0, 0, 0, 0)),
-                pl.BlockSpec((1, LANES, length), lambda c, p, s: (c, p, 0)),
+                pl.BlockSpec((1, 1, 4 + 2 * chunks, 1, length), lambda c, p, s: (c, p, 0, 0, 0)),
                 pl.BlockSpec((1, length, LANES), lambda c, p, s: (c, 0, p)),
-                pl.BlockSpec((1, 2, 1, length), lambda c, p, s: (c, p, 0, 0)),
-                pl.BlockSpec((1, 2, 1, length), lambda c, p, s: (c, p, 0, 0)),
             ],
             scratch_shapes=[
                 pltpu.VMEM((pairs, LANES, 8), F32),
@@ -510,8 +502,7 @@
 
 
 def back_kernel(
-    scalars_ref, pos_ref, xt_ref, qkv_ref, kct_ref, vc_ref, e_ref, more_ref, top_ref, ot_ref, lse_ref,
-    own_ref, datt_ref,
+    scalars_ref, pos_ref, xt_ref, qkv_ref, kvt_ref, e_ref, more_ref, stats_ref, datt_ref,
     dt_ref, keep_ref, send_ref,
     hot, oz, og, ds, joined, dqa, dkv, self_q, self_kv, delta, grad, term, spill,
     *, shards, cells, first_pair,
@@ -549,7 +540,7 @@
     og[...] = datt_ref[0].T
 
     def share(chunk, side):
-        return jnp.exp(top_ref[0, 0, chunk, side] - lse_ref[0, side])
+        return jnp.exp(stats_ref[0, 0, 4 + 2 * chunk + side] - stats_ref[0, 0, side])
 
     def outset(side):
         rows = heads[side]
@@ -557,7 +548,7 @@
         query = queries[rows, :].astype(F32) * SCALE
         key = qkv_ref[0, 0, LANES + side * HD : LANES + (side + 1) * HD, :].astype(F32)
         value = qkv_ref[0, 0, 2 * LANES + side * HD : 2 * LANES + (side + 1) * HD, :].astype(F32)
-        prob = jnp.exp(jnp.where(hidden, own_ref[0, side], MASK_FILL) - lse_ref[0, side])
+        prob = jnp.exp(jnp.where(hidden, stats_ref[0, 0, 2 + side], MASK_FILL) - stats_ref[0, 0, side])
         own_grad = jnp.sum(grads * value, axis=0, keepdims=True)
         back = (prob * (own_grad - delta[side])).astype(BF16).astype(F32)
         self_q[rows, :] = back * key
@@ -579,11 +570,14 @@
         term[...] = dot(xt_ref[0], dt_ref[0, 0], 1, 1)
 
     exps = e_ref.at[0, 0]
-    values = vc_ref[0, 0, 0:CHUNK, :]
+    values = kvt_ref[0, 0, 0, LANES:, :].T
     for side in range(2):
         rows = heads[side]
         delta[side] = jnp.sum(
-            og[rows, :].astype(F32) * ot_ref[0, rows, :].astype(F32), axis=0, keepdims=True
+            og[rows, :].astype(F32)
+            * qkv_ref[0, 0, TRIPLE + side * HD : TRIPLE + (side + 1) * HD, :].astype(F32),
+            axis=0,
+            keepdims=True,
         )
     scaled = [spread(0, side, None) for side in range(2)]
     for cut in cuts:
@@ -597,23 +591,23 @@
     d_values += dot(exps[1], oz[1], 1, 1)
     lanes = lax.broadcasted_iota(jnp.int32, (CHUNK, LANES), 1) < HD
     joined[:, LANES:] = d_values.astype(BF16)
-    dqa[0:HD, :] = dot(kct_ref[0, 0, 0, 0:HD, :], ds[0])
+    dqa[0:HD, :] = dot(kvt_ref[0, 0, 0, 0:HD, :], ds[0])
     d_keys = jnp.where(lanes, d_keys, dot(ds[1], queries[...], 1, 1)) * SCALE
-    dqa[HD:, :] = dot(kct_ref[0, 0, 0, HD:, :], ds[1])
+    dqa[HD:, :] = dot(kvt_ref[0, 0, 0, HD:LANES, :], ds[1])
     joined[:, 0:LANES] = d_keys.astype(BF16)
     dkv[...] = dot(joined[...], hot[cell, 0], 0, 0)
     close(dqa[...], dkv[...])
 
     def later_chunk(chunk, carry):
         pltpu.sync_copy(more_ref.at[cell, first_pair + pair, chunk - 1], spill)
-        values = vc_ref[0, 0, pl.ds(pl.multiple_of(chunk * CHUNK, 16), CHUNK), :]
+        values = kvt_ref[0, 0, chunk, LANES:, :].T
         d_values = jnp.zeros((CHUNK, LANES), F32)
         for side in range(2):
             scaled = spread(chunk, side, None)
             for cut in cuts:
                 score_grads(chunk, side, spill, values, cut, scaled)
             d_values += dot(spill[side], oz[side], 1, 1)
-            dqa[heads[side], :] += dot(kct_ref[0, 0, chunk, heads[side], :], ds[side])
+            dqa[heads[side], :] += dot(kvt_ref[0, 0, chunk, heads[side], :], ds[side])
         d_keys = jnp.where(lanes, dot(ds[0], queries[...], 1, 1), dot(ds[1], queries[...], 1, 1)) * SCALE
         joined[:, 0:LANES] = d_keys.astype(BF16)
         joined[:, LANES:] = d_values.astype(BF16)
@@ -644,12 +638,11 @@
             target[block:, :] = (grad[width:, :] * ours).astype(BF16)
 
 
-def attend_back(group, shards, scalars, pos, xt, qkv, kct, vc, e, more, top, ot, lse, own, datt):
+def attend_back(group, shards, scalars, pos, xt, qkv, kvt, e, more, stats, datt):
     first, count = group
     cells, length = xt.shape[0], xt.shape[2]
     width = xt.shape[1] - ONES
-    padded = vc.shape[2]
-    chunks = padded // CHUNK
+    chunks = kvt.shape[2]
     half = (shards // 2, count, width // shards + EXTRA, TRIPLE)
     part = pl.BlockSpec((shards // 2, 1) + half[2:], lambda p, c, s: (0, p, 0, 0))
     shape = jax.ShapeDtypeStruct
@@ -662,15 +655,11 @@
             in_specs=[
                 pl.BlockSpec((1, 1, length), lambda p, c, s: (c, 0, 0)),
                 pl.BlockSpec((1, width + ONES, length), lambda p, c, s: (c, 0, 0)),
-                pl.BlockSpec((1, 1, TRIPLE, length), lambda p, c, s: (c, first + p, 0, 0)),
-                pl.BlockSpec((1, 1, chunks, LANES, CHUNK), lambda p, c, s: (c, first + p, 0, 0, 0)),
-                pl.BlockSpec((1, 1, padded, LANES), lambda p, c, s: (c, first + p, 0, 0)),
+                pl.BlockSpec((1, 1, 4 * LANES, length), lambda p, c, s: (c, first + p, 0, 0)),
+                pl.BlockSpec((1, 1, chunks, 2 * LANES, CHUNK), lambda p, c, s: (c, first + p, 0, 0, 0)),
                 pl.BlockSpec((1, 1, 2, CHUNK, length), lambda p, c, s: (c, first + p, 0, 0, 0)),
                 pl.BlockSpec(memory_space=pl.ANY),
-                pl.BlockSpec((1, 1, chunks, 2, 1, length), lambda p, c, s: (c, first + p, 0, 0, 0, 0)),
-                pl.BlockSpec((1, LANES, length), lambda p, c, s: (c, first + p, 0)),
-                pl.BlockSpec((1, 2, 1, length), lambda p, c, s: (c, first + p, 0, 0)),
-                pl.BlockSpec((1, 2, 1, length), lambda p, c, s: (c, first + p, 0, 0)),
+                pl.BlockSpec((1, 1, 4 + 2 * chunks, 1, length), lambda p, c, s: (c, first + p, 0, 0, 0)),
                 pl.BlockSpec((1, length, LANES), lambda p, c, s: (c, 0, first + p)),
             ],
             out_specs=[
@@ -697,7 +686,7 @@
         compiler_params=params(51),
         cost_estimate=cost(cells * count * 6e9, cells * count * 7e6),
         name="attend_back",
-    )(scalars, pos, xt, qkv, kct, vc, e, more, top, ot, lse, own, datt)
+    )(scalars, pos, xt, qkv, kvt, e, more, stats, datt)
 
 
 def input_kernel(w_ref, dhid_ref, *refs):
@@ -860,7 +849,7 @@
     early = gather_pieces(early, xt)
     late = after(late, *early[:2])
     late = [late] + [swap(late, "fsdp", offset) for offset in held[1:]]
-    w, vec, qkv, kct, vc, e, more, top, ot, o, lse, own = attend(scalars, held, early, xt, xc, pos)
+    w, vec, qkv, kvt, e, more, stats, o = attend(scalars, held, early, xt, xc, pos)
     flat = lambda a: a.reshape(cells * length, width)
     result, dhid, datt, keep, send = middle(
         scalars, held, late, flat(tokens), flat(o), flat(cotangent), vec, cells
@@ -869,23 +858,25 @@
     chains = [Reduction(keep, send)]
 
     def boundary(value):
-        for chain in chains[:-1]:
+        older, newest = chains[:-1], chains[-1]
+        arrived = lax.optimization_barrier([chain.arrived for chain in older])
+        for chain, chain.arrived in zip(older, arrived):
             chain.arrive()
-        newest = chains[-1]
         pairs = lax.optimization_barrier([chain.pair() for chain in chains])
         for chain, (chain.keep, chain.send) in zip(chains, pairs):
             pass
         newest.start()
+        for chain in older:
+            chain.start()
         newest.arrive()
-        value, pairs = lax.optimization_barrier((value, [chain.pair() for chain in chains]))
-        for chain, pair in zip(chains, pairs):
-            chain.start(pair)
+        value, pair = lax.optimization_barrier((value, newest.pair()))
+        newest.start(pair)
         return value
 
     parts = []
     for group in GROUPS:
         dt, keep, send = attend_back(
-            group, shards, boundary(scalars), pos, xt, qkv, kct, vc, e, more, top, ot, lse, own, cube(datt)
+            group, shards, boundary(scalars), pos, xt, qkv, kvt, e, more, stats, cube(datt)
         )
         parts.append(dt)
         chains.append(Reduction(keep, send, 1))

time: 203 us -> 199 us (0.980)
  waiting for transfers between devices: 22.7 us -> 18.7 us
    ppermute x23, waiting for transfers between devices: 22.7 us -> 18.7 us  [swap(): return lax.ppermute(values, axis, [(i, i ^ mask) for i in range(size)])]
  transfers between devices with their start and end apart: 23 -> 23, of which waited for: 11 -> 9; matrix products, arithmetic and copies ran while one was open for 0% -> 0% of each run, Pallas kernels for 46% -> 47%
where the time goes in v5:
time: 199 us; the launch traced here: 196 us
  Pallas kernels  119 us (60%)
  starting transfers between devices  53.2 us (27%)
  waiting for transfers between devices  18.7 us (9%)
  local copies, waits for them, and re-layouts  2.99 us (2%)
    ppermute x23, starting transfers between devices, swap(): return lax.ppermute(values, axis, [(i, i ^ mask) for i in range(size)])  53.2 us
    pallas_call x2, Pallas kernels, attend_back(): pl.pallas_call(functools.partial(back_kernel, shards=shards, cells=cells,...  51.6 us
    pallas_call x1, Pallas kernels, attend(): pl.pallas_call(functools.partial(attend_kernel, held=held, cells=cells),...  27.2 us
    pallas_call x1, Pallas kernels, middle(): pl.pallas_call(functools.partial(middle_kernel, held=held, cells=cells),...  24 us
    ppermute x23, waiting for transfers between devices, swap(): return lax.ppermute(values, axis, [(i, i ^ mask) for i in range(size)])  18.7 us
    pallas_call x1, Pallas kernels, gather_known(): pl.pallas_call(gather_kernel, out_shape=(jax.ShapeDtypeStruct((cells, pad...  6.93 us
    pallas_call x1, Pallas kernels, input_grad(): pl.pallas_call(input_kernel, out_shape=jax.ShapeDtypeStruct(dhid.shape, B...  5.86 us
  transfers between devices with their start and end apart: 23, of which 9 were waited for; matrix products, arithmetic and copies ran while one was open for 0% of the time, Pallas kernels for 47%

profile of v5, /device:TPU:0, one launch (start us, length us, event | category | flops | bytes accessed | tf_op | source)
XLA Modules:
  0.0 196.3 jit_solution(4126571629014580270)
XLA Ops:
  0.7 2.2 %pack.1 = (bf16[400,512]{1,0:T(8,128)(2,1)}, bf16[384,512]{1,0:T(8,128)(2,1)}, s32[3]{0:T(128)}) custom-call(s32[2,1200]{1,0:T(2,128)} %flags_ref.1, bf16[128,512]{1,0:T(8,128)(2,1)} %refs_1_.1, bf16[128,512]{1,0:T(8,128)(2,1)} %refs_2_.1, bf16[128,512]{1,0:T(8,128)(2,1)} %refs_3_.1, bf16[128,512]{1,0:T(8,128)(2,1)} %refs_4_.1, bf16[128,512]{1,0:T(8,128)(2,1)} %refs_5_.1, ...), custom_call_target="tpu_custom_call" | custom-call | tf_op jit(solution)/shard_map/pack/pallas_call | solution.py:81
  2.9 3.0 %collective-permute-start = (bf16[400,512]{1,0:T(8,128)(2,1)}, bf16[400,512]{1,0:T(8,128)(2,1)S(1)}, u32[]{:S(2)}, u32[]{:S(2)}) collective-permute-start(bf16[400,512]{1,0:T(8,128)(2,1)} %get-tuple-element.92.refs_1_), channel_id=1, source_target_pairs={{0,2},{1,3},{2,0},{3,1},{4,6},{5,7},{6,4},{7,5},{8,10},{9,11},{10,... | collective-permute-start | bytes 1228808 | tf_op jit(solution)/shard_map/ppermute | solution.py:770
  5.9 6.9 %gather_known.1 = (bf16[2,1344,512]{2,1,0:T(8,128)(2,1)}, bf16[2,528,1200]{2,1,0:T(8,128)(2,1)}, s32[2,1,1200]{2,1,0:T(1,128)}) custom-call(s32[3]{0:T(128)} %get-tuple-element.128.scalars_ref.refs_0_, s32[2,1200]{1,0:T(2,128)} %flags_ref.1, bf16[2,1200,512]{2,1,0:T(8,128)(2,1)} %x_ref.1), custom_call_target="tpu_custom_call" | custom-call | flops 4000000000 | bytes 12000000 | tf_op jit(solution)/shard_map/gather_known/pallas_call | solution.py:124
  12.9 2.7 %collective-permute-done.refs_2_ = bf16[400,512]{1,0:T(8,128)(2,1)S(1)} collective-permute-done((bf16[400,512]{1,0:T(8,128)(2,1)}, bf16[400,512]{1,0:T(8,128)(2,1)S(1)}, u32[]{:S(2)}, u32[]{:S(2)}) %collective-permute-start) | collective-permute-done | bytes 409632 | tf_op jit(solution)/shard_map/ppermute | solution.py:770
  15.6 1.7 collective-permute-start.1
  17.8 0.7 copy-done.7
  18.5 27.2 %attend.1 = (bf16[512,1536]{1,0:T(8,128)(2,1)}, f32[16,512]{1,0:T(8,128)S(1)}, bf16[2,4,512,1200]{3,2,1,0:T(8,128)(2,1)}, bf16[2,4,2,256,672]{4,3,2,1,0:T(8,128)...) custom-call(s32[3]{0:T(128)S(1)} %copy-done.2, ...), custom_call_target="tpu_custom_call" | custom-call | flops 20000000000 | bytes 50000000 | tf_op jit(solution)/shard_map/attend/pallas_call | solution.py:320
  45.8 24.0 %middle.1 = (bf16[2400,512]{1,0:T(8,128)(2,1)}, bf16[2400,512]{1,0:T(8,128)(2,1)}, bf16[2400,512]{1,0:T(8,128)(2,1)}, bf16[2,144,1536]{2,1,0:T(8,128)(2,1)S(1)}, bf16[2,144,1536]{2,1,0:T(8,128)(2,1)S(1)}) custom-call(s32[3]{0:T(128)S(1)} %copy-done.2, bf16[384,512]{1,0:T(8,128)(2,1)S(1)} %copy-done.1, bf16[384,512]{1,0:T(8,128)(2,1)S(1)} %collective-permute-done.1.refs_2_, ...), custom_call_target="tpu_custom_call" | custom-call | flops 12000000000 | bytes 19200000 | tf_op jit(solution)/shard_map/middle/pallas_call | solution.py:482
  69.7 28.8 %collective-permute-start.6 = (bf16[2,144,1536]{2,1,0:T(8,128)(2,1)S(1)}, bf16[2,144,1536]{2,1,0:T(8,128)(2,1)S(1)}, u32[]{:S(2)}, u32[]{:S(2)}) collective-permute-start(bf16[2,144,1536]{2,1,0:T(8,128)(2,1)S(1)} %get-tuple-element.108), channel_id=1, source_target_pairs={{0,1},{1,0},{2,3},{3,2},{4,5},{5,4},{6,7},{7,6},{8,9},{9,8},{10,11... | collective-permute-start | bytes 2654216 | tf_op jit(solution)/shard_map/ppermute | solution.py:770
  98.5 2.1 %collective-permute-done.6 = bf16[2,144,1536]{2,1,0:T(8,128)(2,1)S(1)} collective-permute-done((bf16[2,144,1536]{2,1,0:T(8,128)(2,1)S(1)}, bf16[2,144,1536]{2,1,0:T(8,128)(2,1)S(1)}, u32[]{:S(2)}, u32[]{:S(2)}) %collective-permute-start.6) | collective-permute-done | bytes 884768 | tf_op jit(solution)/shard_map/ppermute | solution.py:770
  100.9 25.5 %attend_back.2 = (bf16[2,2,384,1200]{3,2,1,0:T(8,128)(2,1)}, bf16[2,2,144,384]{3,2,1,0:T(8,128)(2,1)S(1)}, bf16[2,2,144,384]{3,2,1,0:T(8,128)(2,1)S(1)}) custom-call(s32[3]{0:T(128)S(1)} %copy-done.2, s32[2,1,1200]{2,1,0:T(1,128)S(1)} %copy-done.7, bf16[2,528,1200]{2,1,0:T(8,128)(2,1)} %get-tuple-element.93.refs_5_.xt_ref, ...), custom_call_target="tpu_custom_call" | custom-call | flops 24000000000 | bytes 28000000 | tf_op jit(solution)/shard_map/attend_back/pallas_call | solution.py:649
  127.0 1.4 collective-permute-done.9
  128.6 2.1 %collective-permute-start.10 = (bf16[1,2,144,384]{3,2,1,0:T(8,128)(2,1)S(1)}, bf16[1,2,144,384]{3,2,1,0:T(8,128)(2,1)S(1)}, u32[]{:S(2)}, u32[]{:S(2)}) collective-permute-start(bf16[1,2,144,384]{3,2,1,0:T(8,128)(2,1)S(1)} %get-tuple-element.124), channel_id=1, source_target_pairs={{0,2},{1,3},{2,0},{3,1},{4,6},{5,7},{6,4},{7,5},{8,10},{9,11},{10,... | collective-permute-start | bytes 663560 | tf_op jit(solution)/shard_map/ppermute | solution.py:770
  130.7 26.1 %attend_back.3 = (bf16[2,2,384,1200]{3,2,1,0:T(8,128)(2,1)}, bf16[2,2,144,384]{3,2,1,0:T(8,128)(2,1)S(1)}, bf16[2,2,144,384]{3,2,1,0:T(8,128)(2,1)S(1)}) custom-call(s32[3]{0:T(128)S(1)} %copy-done.2, s32[2,1,1200]{2,1,0:T(1,128)S(1)} %copy-done.8, bf16[2,528,1200]{2,1,0:T(8,128)(2,1)} %get-tuple-element.93.refs_5_.xt_ref, ...), custom_call_target="tpu_custom_call" | custom-call | flops 24000000000 | bytes 28000000 | tf_op jit(solution)/shard_map/attend_back/pallas_call | solution.py:649
  157.1 2.8 %collective-permute-start.12 = (bf16[1,144,1536]{2,1,0:T(8,128)(2,1)S(1)}, bf16[1,144,1536]{2,1,0:T(8,128)(2,1)S(1)}, u32[]{:S(2)}, u32[]{:S(2)}) collective-permute-start(bf16[1,144,1536]{2,1,0:T(8,128)(2,1)S(1)} %add_convert_fusion.3), channel_id=1, source_target_pairs={{0,8},{4,12},{8,0},{12,4},{16,24},{20,28},{24,16},{28,20},{1,9},{5... | collective-permute-start | bytes 1327112 | tf_op jit(solution)/shard_map/ppermute | solution.py:770
  159.9 1.5 collective-permute-start.13
  161.5 1.7 collective-permute-start.14
  163.3 2.1 %copy-done.4 = bf16[2,2,384,1200]{3,2,1,0:T(8,128)(2,1)S(1)} copy-done((bf16[2,2,384,1200]{3,2,1,0:T(8,128)(2,1)S(1)}, bf16[2,2,384,1200]{3,2,1,0:T(8,128)(2,1)}, u32[]{:S(2)}) %copy-start.4) | copy-done | bytes 3686424
  165.4 5.9 %input_grad.1 = bf16[2,1200,512]{2,1,0:T(8,128)(2,1)} custom-call(bf16[512,1536]{1,0:T(8,128)(2,1)S(1)} %copy-done.6, bf16[2,1200,512]{2,1,0:T(8,128)(2,1)S(1)} %bitcast.18, bf16[2,768,1200]{2,1,0:T(8,128)(2,1)S(1)} %bitcast.16, bf16[2,768,1200]{2,1,0:T(8,128)(2,1)S(1)} %bitcast.17), custom_call_target="tpu_custom_call" | custom-call | flops 4000000000 | bytes 16000000 | tf_op jit(solution)/shard_map/input_grad/pallas_call | solution.py:707
  171.3 0.9 collective-permute-start.15
  172.3 1.8 collective-permute-start.17
  174.2 1.9 collective-permute-done.15
  176.2 1.2 collective-permute-start.20
  177.4 1.5 collective-permute-start.16
  178.9 1.8 collective-permute-start.18
  181.1 2.3 %collective-permute-start.21 = (bf16[1,1,144,384]{3,2,1,0:T(8,128)(2,1)S(1)}, bf16[1,1,144,384]{3,2,1,0:T(8,128)(2,1)S(1)}, u32[]{:S(2)}, u32[]{:S(2)}) collective-permute-start(bf16[1,1,144,384]{3,2,1,0:T(8,128)(2,1)S(1)} %add_convert_fusion.9), channel_id=1, source_target_pairs={{0,16},{4,20},{8,24},{12,28},{16,0},{20,4},{24,8},{28,12},{1,17},{... | collective-permute-start | bytes 331784 | tf_op jit(solution)/shard_map/ppermute | solution.py:770
  183.4 5.3 %collective-permute-done.18 = bf16[1,1,144,384]{3,2,1,0:T(8,128)(2,1)S(1)} collective-permute-done((bf16[1,1,144,384]{3,2,1,0:T(8,128)(2,1)S(1)}, bf16[1,1,144,384]{3,2,1,0:T(8,128)(2,1)S(1)}, u32[]{:S(2)}, u32[]{:S(2)}) %collective-permute-start.18) | collective-permute-done | bytes 110624 | tf_op jit(solution)/shard_map/ppermute | solution.py:770
  188.8 1.1 collective-permute-done.21
  189.9 1.0 collective-permute-start.22
  190.9 2.7 %collective-permute-done.19.refs_3_ = bf16[1,144,384]{2,1,0:T(8,128)(2,1)S(1)} collective-permute-done((bf16[1,144,384]{2,1,0:T(8,128)(2,1)S(1)}, bf16[1,144,384]{2,1,0:T(8,128)(2,1)S(1)}, u32[]{:S(2)}, u32[]{:S(2)}) %collective-permute-start.19) | collective-permute-done | bytes 110624 | tf_op jit(solution)/shard_map/ppermute | solution.py:770
  193.6 1.2 collective-permute-done.22.refs_5_
  194.8 1.3 finish.1
  (59 shorter events, 2.8 us)
Async XLA Ops:
  2.9 12.7 %collective-permute-start = (bf16[400,512]{1,0:T(8,128)(2,1)}, bf16[400,512]{1,0:T(8,128)(2,1)S(1)}, u32[]{:S(2)}, u32[]{:S(2)}) collective-permute-start(bf16[400,512]{1,0:T(8,128)(2,1)} %get-tuple-element.92.refs_1_), channel_id=1, source_target_pairs={{0,2},{1,3},{2,0},{3,1},{4,6},{5,7},{6,4},{7,5},{8,10},{9,11},{10,... | collective-permute-start | bytes 1228808 | tf_op jit(solution)/shard_map/ppermute | solution.py:770
  5.9 11.8 %collective-permute-start.4 = (bf16[400,512]{1,0:T(8,128)(2,1)}, bf16[400,512]{1,0:T(8,128)(2,1)S(1)}, u32[]{:S(2)}, u32[]{:S(2)}) collective-permute-start(bf16[400,512]{1,0:T(8,128)(2,1)} %get-tuple-element.92.refs_1_), channel_id=1, source_target_pairs={{0,1},{1,0},{2,3},{3,2},{4,5},{5,4},{6,7},{7,6},{8,9},{9,8},{10,11... | collective-permute-start | bytes 1228808 | tf_op jit(solution)/shard_map/ppermute | solution.py:770
  5.9 9.7 %copy-start.1 = (bf16[384,512]{1,0:T(8,128)(2,1)S(1)}, bf16[384,512]{1,0:T(8,128)(2,1)}, u32[]{:S(2)}) copy-start(bf16[384,512]{1,0:T(8,128)(2,1)} %get-tuple-element.96.refs_1_) | copy-start | bytes 1179652
  5.9 11.8 %copy-start = (bf16[400,512]{1,0:T(8,128)(2,1)S(1)}, bf16[400,512]{1,0:T(8,128)(2,1)}, u32[]{:S(2)}) copy-start(bf16[400,512]{1,0:T(8,128)(2,1)} %get-tuple-element.92.refs_1_) | copy-start | bytes 1228804
  5.9 11.8 %copy-start.2 = (s32[3]{0:T(128)S(1)}, s32[3]{0:T(128)}, u32[]{:S(2)}) copy-start(s32[3]{0:T(128)} %get-tuple-element.128.scalars_ref.refs_0_) | copy-start | bytes 40
  15.6 2.2 %collective-permute-start.5 = (bf16[400,512]{1,0:T(8,128)(2,1)S(1)}, bf16[400,512]{1,0:T(8,128)(2,1)S(1)}, u32[]{:S(2)}, u32[]{:S(2)}) collective-permute-start(bf16[400,512]{1,0:T(8,128)(2,1)S(1)} %collective-permute-done.refs_2_), channel_id=1, source_target_pairs={{0,1},{1,0},{2,3},{3,2},{4,5},{5,4},{6,7},{7,6},{8,9},{9,8},{10,11... | collective-permute-start | bytes 1228808 | tf_op jit(solution)/shard_map/ppermute | solution.py:770
  15.6 30.1 %collective-permute-start.1 = (bf16[384,512]{1,0:T(8,128)(2,1)S(1)}, bf16[384,512]{1,0:T(8,128)(2,1)S(1)}, u32[]{:S(2)}, u32[]{:S(2)}) collective-permute-start(bf16[384,512]{1,0:T(8,128)(2,1)S(1)} %copy-done.1), channel_id=1, source_target_pairs={{0,2},{1,3},{2,0},{3,1},{4,6},{5,7},{6,4},{7,5},{8,10},{9,11},{10,... | collective-permute-start | bytes 1179656 | tf_op jit(solution)/shard_map/ppermute | solution.py:770
  17.4 28.4 %collective-permute-start.2 = (bf16[384,512]{1,0:T(8,128)(2,1)S(1)}, bf16[384,512]{1,0:T(8,128)(2,1)S(1)}, u32[]{:S(2)}, u32[]{:S(2)}) collective-permute-start(bf16[384,512]{1,0:T(8,128)(2,1)S(1)} %copy-done.1), channel_id=1, source_target_pairs={{0,1},{1,0},{2,3},{3,2},{4,5},{5,4},{6,7},{7,6},{8,9},{9,8},{10,11... | collective-permute-start | bytes 1179656 | tf_op jit(solution)/shard_map/ppermute | solution.py:770
  17.6 28.2 %collective-permute-start.3 = (bf16[384,512]{1,0:T(8,128)(2,1)S(1)}, bf16[384,512]{1,0:T(8,128)(2,1)S(1)}, u32[]{:S(2)}, u32[]{:S(2)}) collective-permute-start(bf16[384,512]{1,0:T(8,128)(2,1)S(1)} %copy-done.1), channel_id=1, source_target_pairs={{0,3},{1,2},{2,1},{3,0},{4,7},{5,6},{6,5},{7,4},{8,11},{9,10},{10,... | collective-permute-start | bytes 1179656 | tf_op jit(solution)/shard_map/ppermute | solution.py:770
  17.8 0.7 copy-start.7
  69.7 30.8 %collective-permute-start.6 = (bf16[2,144,1536]{2,1,0:T(8,128)(2,1)S(1)}, bf16[2,144,1536]{2,1,0:T(8,128)(2,1)S(1)}, u32[]{:S(2)}, u32[]{:S(2)}) collective-permute-start(bf16[2,144,1536]{2,1,0:T(8,128)(2,1)S(1)} %get-tuple-element.108), channel_id=1, source_target_pairs={{0,1},{1,0},{2,3},{3,2},{4,5},{5,4},{6,7},{7,6},{8,9},{9,8},{10,11... | collective-permute-start | bytes 2654216 | tf_op jit(solution)/shard_map/ppermute | solution.py:770
  100.9 25.6 %collective-permute-start.7 = (bf16[1,144,1536]{2,1,0:T(8,128)(2,1)S(1)}, bf16[1,144,1536]{2,1,0:T(8,128)(2,1)S(1)}, u32[]{:S(2)}, u32[]{:S(2)}) collective-permute-start(bf16[1,144,1536]{2,1,0:T(8,128)(2,1)S(1)} %get-tuple-element.110), channel_id=1, source_target_pairs={{0,2},{1,3},{2,0},{3,1},{4,6},{5,7},{6,4},{7,5},{8,10},{9,11},{10,... | collective-permute-start | bytes 1327112 | tf_op jit(solution)/shard_map/ppermute | solution.py:770
  126.5 4.3 %copy-start.8 = (s32[2,1,1200]{2,1,0:T(1,128)S(1)}, s32[2,1,1200]{2,1,0:T(1,128)}, u32[]{:S(2)}) copy-start(s32[2,1,1200]{2,1,0:T(1,128)} %get-tuple-element.100.refs_7_.pos_ref) | copy-start | bytes 28804
  126.6 1.9 collective-permute-start.9
  127.0 29.8 %collective-permute-start.8 = (bf16[1,144,1536]{2,1,0:T(8,128)(2,1)S(1)}, bf16[1,144,1536]{2,1,0:T(8,128)(2,1)S(1)}, u32[]{:S(2)}, u32[]{:S(2)}) collective-permute-start(bf16[1,144,1536]{2,1,0:T(8,128)(2,1)S(1)} %add_convert_fusion.5), channel_id=1, source_target_pairs={{0,16},{4,20},{8,24},{12,28},{16,0},{20,4},{24,8},{28,12},{1,17},{... | collective-permute-start | bytes 1327112 | tf_op jit(solution)/shard_map/ppermute | solution.py:770
  128.6 28.2 %collective-permute-start.10 = (bf16[1,2,144,384]{3,2,1,0:T(8,128)(2,1)S(1)}, bf16[1,2,144,384]{3,2,1,0:T(8,128)(2,1)S(1)}, u32[]{:S(2)}, u32[]{:S(2)}) collective-permute-start(bf16[1,2,144,384]{3,2,1,0:T(8,128)(2,1)S(1)} %get-tuple-element.124), channel_id=1, source_target_pairs={{0,2},{1,3},{2,0},{3,1},{4,6},{5,7},{6,4},{7,5},{8,10},{9,11},{10,... | collective-permute-start | bytes 663560 | tf_op jit(solution)/shard_map/ppermute | solution.py:770
  130.7 32.5 %copy-start.5 = (bf16[2400,512]{1,0:T(8,128)(2,1)S(1)}, bf16[2400,512]{1,0:T(8,128)(2,1)}, u32[]{:S(2)}) copy-start(bf16[2400,512]{1,0:T(8,128)(2,1)} %get-tuple-element.134) | copy-start | bytes 7372804
  130.7 32.5 %copy-start.6 = (bf16[512,1536]{1,0:T(8,128)(2,1)S(1)}, bf16[512,1536]{1,0:T(8,128)(2,1)}, u32[]{:S(2)}) copy-start(bf16[512,1536]{1,0:T(8,128)(2,1)} %get-tuple-element.133.w_ref) | copy-start | bytes 4718596
  156.8 6.5 %copy-start.3 = (bf16[2,2,384,1200]{3,2,1,0:T(8,128)(2,1)S(1)}, bf16[2,2,384,1200]{3,2,1,0:T(8,128)(2,1)}, u32[]{:S(2)}) copy-start(bf16[2,2,384,1200]{3,2,1,0:T(8,128)(2,1)} %get-tuple-element.135) | copy-start | bytes 11059204
  157.0 4.3 %collective-permute-start.11 = (bf16[2,2,144,384]{3,2,1,0:T(8,128)(2,1)S(1)}, bf16[2,2,144,384]{3,2,1,0:T(8,128)(2,1)S(1)}, u32[]{:S(2)}, u32[]{:S(2)}) collective-permute-start(bf16[2,2,144,384]{3,2,1,0:T(8,128)(2,1)S(1)} %get-tuple-element.132), channel_id=1, source_target_pairs={{0,1},{1,0},{2,3},{3,2},{4,5},{5,4},{6,7},{7,6},{8,9},{9,8},{10,11... | collective-permute-start | bytes 1327112 | tf_op jit(solution)/shard_map/ppermute | solution.py:770
  157.1 14.1 %collective-permute-start.12 = (bf16[1,144,1536]{2,1,0:T(8,128)(2,1)S(1)}, bf16[1,144,1536]{2,1,0:T(8,128)(2,1)S(1)}, u32[]{:S(2)}, u32[]{:S(2)}) collective-permute-start(bf16[1,144,1536]{2,1,0:T(8,128)(2,1)S(1)} %add_convert_fusion.3), channel_id=1, source_target_pairs={{0,8},{4,12},{8,0},{12,4},{16,24},{20,28},{24,16},{28,20},{1,9},{5... | collective-permute-start | bytes 1327112 | tf_op jit(solution)/shard_map/ppermute | solution.py:770
  159.9 11.4 %collective-permute-start.13 = (bf16[1,1,144,384]{3,2,1,0:T(8,128)(2,1)S(1)}, bf16[1,1,144,384]{3,2,1,0:T(8,128)(2,1)S(1)}, u32[]{:S(2)}, u32[]{:S(2)}) collective-permute-start(bf16[1,1,144,384]{3,2,1,0:T(8,128)(2,1)S(1)} %get-tuple-element.138), channel_id=1, source_target_pairs={{0,4},{4,0},{8,12},{12,8},{16,20},{20,16},{24,28},{28,24},{1,5},{5... | collective-permute-start | bytes 331784 | tf_op jit(solution)/shard_map/ppermute | solution.py:770
  161.5 9.7 %collective-permute-start.14 = (bf16[1,2,144,384]{3,2,1,0:T(8,128)(2,1)S(1)}, bf16[1,2,144,384]{3,2,1,0:T(8,128)(2,1)S(1)}, u32[]{:S(2)}, u32[]{:S(2)}) collective-permute-start(bf16[1,2,144,384]{3,2,1,0:T(8,128)(2,1)S(1)} %get-tuple-element.139), channel_id=1, source_target_pairs={{0,2},{1,3},{2,0},{3,1},{4,6},{5,7},{6,4},{7,5},{8,10},{9,11},{10,... | collective-permute-start | bytes 663560 | tf_op jit(solution)/shard_map/ppermute | solution.py:770
  163.2 2.1 %copy-start.4 = (bf16[2,2,384,1200]{3,2,1,0:T(8,128)(2,1)S(1)}, bf16[2,2,384,1200]{3,2,1,0:T(8,128)(2,1)}, u32[]{:S(2)}) copy-start(bf16[2,2,384,1200]{3,2,1,0:T(8,128)(2,1)} %get-tuple-element.136) | copy-start | bytes 11059204
  171.3 4.8 %collective-permute-start.15 = (bf16[1,1,144,384]{3,2,1,0:T(8,128)(2,1)S(1)}, bf16[1,1,144,384]{3,2,1,0:T(8,128)(2,1)S(1)}, u32[]{:S(2)}, u32[]{:S(2)}) collective-permute-start(bf16[1,1,144,384]{3,2,1,0:T(8,128)(2,1)S(1)} %broadcast_select_fusion), channel_id=1, source_target_pairs={{0,4},{4,0},{8,12},{12,8},{16,20},{20,16},{24,28},{28,24},{1,5},{5... | collective-permute-start | bytes 331784 | tf_op jit(solution)/shard_map/ppermute | solution.py:770
  172.3 6.6 %collective-permute-start.17 = (bf16[1,1,144,384]{3,2,1,0:T(8,128)(2,1)S(1)}, bf16[1,1,144,384]{3,2,1,0:T(8,128)(2,1)S(1)}, u32[]{:S(2)}, u32[]{:S(2)}) collective-permute-start(bf16[1,1,144,384]{3,2,1,0:T(8,128)(2,1)S(1)} %add_convert_fusion.12), channel_id=1, source_target_pairs={{0,8},{4,12},{8,0},{12,4},{16,24},{20,28},{24,16},{28,20},{1,9},{5... | collective-permute-start | bytes 331784 | tf_op jit(solution)/shard_map/ppermute | solution.py:770
  176.2 4.9 %collective-permute-start.20 = (bf16[1,1,144,384]{3,2,1,0:T(8,128)(2,1)S(1)}, bf16[1,1,144,384]{3,2,1,0:T(8,128)(2,1)S(1)}, u32[]{:S(2)}, u32[]{:S(2)}) collective-permute-start(bf16[1,1,144,384]{3,2,1,0:T(8,128)(2,1)S(1)} %add_convert_fusion.13), channel_id=1, source_target_pairs={{0,8},{4,12},{8,0},{12,4},{16,24},{20,28},{24,16},{28,20},{1,9},{5... | collective-permute-start | bytes 331784 | tf_op jit(solution)/shard_map/ppermute | solution.py:770
  177.4 17.4 %collective-permute-start.16 = (bf16[1,144,1536]{2,1,0:T(8,128)(2,1)S(1)}, bf16[1,144,1536]{2,1,0:T(8,128)(2,1)S(1)}, u32[]{:S(2)}, u32[]{:S(2)}) collective-permute-start(bf16[1,144,1536]{2,1,0:T(8,128)(2,1)S(1)} %add_convert_fusion.1), channel_id=1, source_target_pairs={{0,4},{4,0},{8,12},{12,8},{16,20},{20,16},{24,28},{28,24},{1,5},{5... | collective-permute-start | bytes 1327112 | tf_op jit(solution)/shard_map/ppermute | solution.py:770
  178.9 9.8 %collective-permute-start.18 = (bf16[1,1,144,384]{3,2,1,0:T(8,128)(2,1)S(1)}, bf16[1,1,144,384]{3,2,1,0:T(8,128)(2,1)S(1)}, u32[]{:S(2)}, u32[]{:S(2)}) collective-permute-start(bf16[1,1,144,384]{3,2,1,0:T(8,128)(2,1)S(1)} %add_convert_fusion.11), channel_id=1, source_target_pairs={{0,16},{4,20},{8,24},{12,28},{16,0},{20,4},{24,8},{28,12},{1,17},{... | collective-permute-start | bytes 331784 | tf_op jit(solution)/shard_map/ppermute | solution.py:770
  181.1 8.8 %collective-permute-start.21 = (bf16[1,1,144,384]{3,2,1,0:T(8,128)(2,1)S(1)}, bf16[1,1,144,384]{3,2,1,0:T(8,128)(2,1)S(1)}, u32[]{:S(2)}, u32[]{:S(2)}) collective-permute-start(bf16[1,1,144,384]{3,2,1,0:T(8,128)(2,1)S(1)} %add_convert_fusion.9), channel_id=1, source_target_pairs={{0,16},{4,20},{8,24},{12,28},{16,0},{20,4},{24,8},{28,12},{1,17},{... | collective-permute-start | bytes 331784 | tf_op jit(solution)/shard_map/ppermute | solution.py:770
  188.7 4.9 %collective-permute-start.19 = (bf16[1,144,384]{2,1,0:T(8,128)(2,1)S(1)}, bf16[1,144,384]{2,1,0:T(8,128)(2,1)S(1)}, u32[]{:S(2)}, u32[]{:S(2)}) collective-permute-start(bf16[1,144,384]{2,1,0:T(8,128)(2,1)S(1)} %fusion.refs_2_), channel_id=1, source_target_pairs={{0,4},{4,0},{8,12},{12,8},{16,20},{20,16},{24,28},{28,24},{1,5},{5... | collective-permute-start | bytes 331784 | tf_op jit(solution)/shard_map/ppermute | solution.py:770
  189.9 4.9 %collective-permute-start.22 = (bf16[1,144,384]{2,1,0:T(8,128)(2,1)S(1)}, bf16[1,144,384]{2,1,0:T(8,128)(2,1)S(1)}, u32[]{:S(2)}, u32[]{:S(2)}) collective-permute-start(bf16[1,144,384]{2,1,0:T(8,128)(2,1)S(1)} %fusion.1.refs_4_), channel_id=1, source_target_pairs={{0,4},{4,0},{8,12},{12,8},{16,20},{20,16},{24,28},{28,24},{1,5},{5... | collective-permute-start | bytes 331784 | tf_op jit(solution)/shard_map/ppermute | solution.py:770

commit v6 on v5

--- a/solution.py
+++ b/solution.py
@@ -21,7 +21,7 @@
 ONES = 16
 EXTRA = 16
 LANES = 128
-CUT = 512
+CUT = 256
 LOG2E = 1.4426950408889634
 TRIPLE = 3 * LANES
 GROUPS = ((0, 2), (2, 2))
@@ -134,7 +134,7 @@
             in_specs=[pl.BlockSpec(flags.shape, lambda i, s: (0, 0)), one(length, width)],
             out_specs=[one(padded, width), one(width + ONES, length), one(1, length)],
         ),
-        compiler_params=params(60),
+        compiler_params=params(50),
         cost_estimate=cost(cells * 2e9, cells * 6e6),
         name="gather_known",
     )(scalars, flags, x)
@@ -683,7 +683,7 @@
                 pltpu.VMEM((2, CHUNK, length), BF16),
             ],
         ),
-        compiler_params=params(51),
+        compiler_params=params(52),
         cost_estimate=cost(cells * count * 6e9, cells * count * 7e6),
         name="attend_back",
     )(scalars, pos, xt, qkv, kvt, e, more, stats, datt)
@@ -711,7 +711,7 @@
         in_specs=[pl.BlockSpec(w.shape, lambda i: (0, 0)), block]
         + [pl.BlockSpec((1,) + part.shape[1:], lambda i: (i, 0, 0)) for part in parts],
         out_specs=block,
-        compiler_params=params(28),
+        compiler_params=params(48),
         cost_estimate=cost(cells * 2e9, cells * 8e6),
         name="input_grad",
     )(w, dhid, *parts)

time: 199 us -> 198 us (level)
  Pallas kernels: 119 us -> 148 us
  starting transfers between devices: 53.2 us -> 25.9 us
  waiting for transfers between devices: 18.7 us -> 15.6 us
    pallas_call x1, Pallas kernels: 27.2 us -> 55.8 us  [attend(): pl.pallas_call(functools.partial(attend_kernel, held=held, cells=cells),...]
    ppermute x23, starting transfers between devices: 53.2 us -> 25.9 us  [swap(): return lax.ppermute(values, axis, [(i, i ^ mask) for i in range(size)])]
    ppermute x23, waiting for transfers between devices: 18.7 us -> 15.6 us  [swap(): return lax.ppermute(values, axis, [(i, i ^ mask) for i in range(size)])]
    pallas_call x1, Pallas kernels: 5.86 us -> 8.01 us  [input_grad(): pl.pallas_call(input_kernel, out_shape=jax.ShapeDtypeStruct(dhid.shape, B...]
  transfers between devices with their start and end apart: 23 -> 23, of which waited for: 9 -> 8; matrix products, arithmetic and copies ran while one was open for 0% -> 0% of each run, Pallas kernels for 47% -> 62%
where the time goes in v6:
time: 198 us; the launch traced here: 195 us
  Pallas kernels  148 us (75%)
  starting transfers between devices  25.9 us (13%)
  waiting for transfers between devices  15.6 us (8%)
  local copies, waits for them, and re-layouts  3.22 us (2%)
    pallas_call x1, Pallas kernels, attend(): pl.pallas_call(functools.partial(attend_kernel, held=held, cells=cells),...  55.8 us
    pallas_call x2, Pallas kernels, attend_back(): pl.pallas_call(functools.partial(back_kernel, shards=shards, cells=cells,...  51.3 us
    ppermute x23, starting transfers between devices, swap(): return lax.ppermute(values, axis, [(i, i ^ mask) for i in range(size)])  25.9 us
    pallas_call x1, Pallas kernels, middle(): pl.pallas_call(functools.partial(middle_kernel, held=held, cells=cells),...  24 us
    ppermute x23, waiting for transfers between devices, swap(): return lax.ppermute(values, axis, [(i, i ^ mask) for i in range(size)])  15.6 us
    pallas_call x1, Pallas kernels, input_grad(): pl.pallas_call(input_kernel, out_shape=jax.ShapeDtypeStruct(dhid.shape, B...  8.01 us
    pallas_call x1, Pallas kernels, gather_known(): pl.pallas_call(gather_kernel, out_shape=(jax.ShapeDtypeStruct((cells, pad...  5.7 us
  transfers between devices with their start and end apart: 23, of which 8 were waited for; matrix products, arithmetic and copies ran while one was open for 0% of the time, Pallas kernels for 62%

profile of v6, /device:TPU:0, one launch (start us, length us, event | category | flops | bytes accessed | tf_op | source)
XLA Modules:
  0.0 195.3 jit_solution(8674982103598780136)
XLA Ops:
  0.7 2.2 %pack.1 = (bf16[400,512]{1,0:T(8,128)(2,1)}, bf16[384,512]{1,0:T(8,128)(2,1)}, s32[3]{0:T(128)}) custom-call(s32[2,1200]{1,0:T(2,128)} %flags_ref.1, bf16[128,512]{1,0:T(8,128)(2,1)} %refs_1_.1, bf16[128,512]{1,0:T(8,128)(2,1)} %refs_2_.1, bf16[128,512]{1,0:T(8,128)(2,1)} %refs_3_.1, bf16[128,512]{1,0:T(8,128)(2,1)} %refs_4_.1, bf16[128,512]{1,0:T(8,128)(2,1)} %refs_5_.1, ...), custom_call_target="tpu_custom_call" | custom-call | tf_op jit(solution)/shard_map/pack/pallas_call | solution.py:81
  2.9 3.0 %collective-permute-start = (bf16[400,512]{1,0:T(8,128)(2,1)}, bf16[400,512]{1,0:T(8,128)(2,1)S(1)}, u32[]{:S(2)}, u32[]{:S(2)}) collective-permute-start(bf16[400,512]{1,0:T(8,128)(2,1)} %get-tuple-element.92.refs_1_), channel_id=1, source_target_pairs={{0,2},{1,3},{2,0},{3,1},{4,6},{5,7},{6,4},{7,5},{8,10},{9,11},{10,... | collective-permute-start | bytes 1228808 | tf_op jit(solution)/shard_map/ppermute | solution.py:770
  5.9 0.7 copy-done
  6.6 1.7 copy-done.1
  8.3 0.7 copy-done.4
  9.0 5.7 %gather_known.1 = (bf16[2,1344,512]{2,1,0:T(8,128)(2,1)}, bf16[2,528,1200]{2,1,0:T(8,128)(2,1)}, s32[2,1,1200]{2,1,0:T(1,128)S(1)}) custom-call(s32[3]{0:T(128)S(1)} %copy-done.4, s32[2,1200]{1,0:T(2,128)S(1)} %copy-done, bf16[2,1200,512]{2,1,0:T(8,128)(2,1)S(1)} %copy-done.1), custom_call_target="tpu_custom_call" | custom-call | flops 4000000000 | bytes 12000000 | tf_op jit(solution)/shard_map/gather_known/pallas_call | solution.py:124
  14.7 0.9 collective-permute-done.refs_2_
  15.6 1.7 collective-permute-start.1
  17.8 55.8 %attend.1 = (bf16[512,1536]{1,0:T(8,128)(2,1)}, f32[16,512]{1,0:T(8,128)S(1)}, bf16[2,4,512,1200]{3,2,1,0:T(8,128)(2,1)}, bf16[2,4,2,256,672]{4,3,2,1,0:T(8,128)...) custom-call(s32[3]{0:T(128)S(1)} %copy-done.5, ...), custom_call_target="tpu_custom_call" | custom-call | flops 20000000000 | bytes 50000000 | tf_op jit(solution)/shard_map/attend/pallas_call | solution.py:320
  73.6 24.0 %middle.1 = (bf16[2400,512]{1,0:T(8,128)(2,1)}, bf16[2400,512]{1,0:T(8,128)(2,1)}, bf16[2400,512]{1,0:T(8,128)(2,1)}, bf16[2,144,1536]{2,1,0:T(8,128)(2,1)S(1)}, bf16[2,144,1536]{2,1,0:T(8,128)(2,1)S(1)}) custom-call(s32[3]{0:T(128)S(1)} %copy-done.5, bf16[384,512]{1,0:T(8,128)(2,1)S(1)} %copy-done.3, bf16[384,512]{1,0:T(8,128)(2,1)S(1)} %collective-permute-done.1.refs_2_, ...), custom_call_target="tpu_custom_call" | custom-call | flops 12000000000 | bytes 19200000 | tf_op jit(solution)/shard_map/middle/pallas_call | solution.py:482
  97.8 2.2 %collective-permute-done.6 = bf16[2,144,1536]{2,1,0:T(8,128)(2,1)S(1)} collective-permute-done((bf16[2,144,1536]{2,1,0:T(8,128)(2,1)S(1)}, bf16[2,144,1536]{2,1,0:T(8,128)(2,1)S(1)}, u32[]{:S(2)}, u32[]{:S(2)}) %collective-permute-start.6) | collective-permute-done | bytes 884768 | tf_op jit(solution)/shard_map/ppermute | solution.py:770
  100.3 1.8 collective-permute-start.7
  102.1 25.5 %attend_back.2 = (bf16[2,2,384,1200]{3,2,1,0:T(8,128)(2,1)}, bf16[2,2,144,384]{3,2,1,0:T(8,128)(2,1)S(1)}, bf16[2,2,144,384]{3,2,1,0:T(8,128)(2,1)S(1)}) custom-call(s32[3]{0:T(128)S(1)} %copy-done.5, s32[2,1,1200]{2,1,0:T(1,128)S(1)} %get-tuple-element.100.refs_7_.pos_ref, bf16[2,528,1200]{2,1,0:T(8,128)(2,1)} %get-tuple-element.93.refs_5_.xt_ref, ...), custom_call_target="tpu_custom_call" | custom-call | flops 24000000000 | bytes 28000000 | tf_op jit(solution)/shard_map/attend_back/pallas_call | solution.py:649
  127.8 2.6 %collective-permute-start.8 = (bf16[1,144,1536]{2,1,0:T(8,128)(2,1)S(1)}, bf16[1,144,1536]{2,1,0:T(8,128)(2,1)S(1)}, u32[]{:S(2)}, u32[]{:S(2)}) collective-permute-start(bf16[1,144,1536]{2,1,0:T(8,128)(2,1)S(1)} %add_convert_fusion.5), channel_id=1, source_target_pairs={{0,16},{4,20},{8,24},{12,28},{16,0},{20,4},{24,8},{28,12},{1,17},{... | collective-permute-start | bytes 1327112 | tf_op jit(solution)/shard_map/ppermute | solution.py:770
  131.1 25.8 %attend_back.3 = (bf16[2,2,384,1200]{3,2,1,0:T(8,128)(2,1)}, bf16[2,2,144,384]{3,2,1,0:T(8,128)(2,1)S(1)}, bf16[2,2,144,384]{3,2,1,0:T(8,128)(2,1)S(1)}) custom-call(s32[3]{0:T(128)S(1)} %copy-done.5, s32[2,1,1200]{2,1,0:T(1,128)S(1)} %get-tuple-element.100.refs_7_.pos_ref, bf16[2,528,1200]{2,1,0:T(8,128)(2,1)} %get-tuple-element.93.refs_5_.xt_ref, ...), custom_call_target="tpu_custom_call" | custom-call | flops 24000000000 | bytes 28000000 | tf_op jit(solution)/shard_map/attend_back/pallas_call | solution.py:649
  157.2 1.6 collective-permute-start.12
  158.8 1.5 collective-permute-start.13
  160.5 1.7 collective-permute-start.14
  162.2 8.0 %input_grad.1 = bf16[2,1200,512]{2,1,0:T(8,128)(2,1)} custom-call(bf16[512,1536]{1,0:T(8,128)(2,1)S(1)} %copy-done.7, bf16[2,1200,512]{2,1,0:T(8,128)(2,1)S(1)} %bitcast.17, bf16[2,768,1200]{2,1,0:T(8,128)(2,1)} %bitcast.19, bf16[2,768,1200]{2,1,0:T(8,128)(2,1)} %bitcast.20), custom_call_target="tpu_custom_call" | custom-call | flops 4000000000 | bytes 16000000 | tf_op jit(solution)/shard_map/input_grad/pallas_call | solution.py:707
  170.3 1.2 collective-permute-start.15
  171.5 1.6 collective-permute-start.17
  173.2 1.9 collective-permute-done.15
  175.1 1.2 collective-permute-start.20
  176.4 1.5 collective-permute-start.16
  177.9 1.7 collective-permute-start.18
  180.1 2.4 %collective-permute-start.21 = (bf16[1,1,144,384]{3,2,1,0:T(8,128)(2,1)S(1)}, bf16[1,1,144,384]{3,2,1,0:T(8,128)(2,1)S(1)}, u32[]{:S(2)}, u32[]{:S(2)}) collective-permute-start(bf16[1,1,144,384]{3,2,1,0:T(8,128)(2,1)S(1)} %add_convert_fusion.9), channel_id=1, source_target_pairs={{0,16},{4,20},{8,24},{12,28},{16,0},{20,4},{24,8},{28,12},{1,17},{... | collective-permute-start | bytes 331784 | tf_op jit(solution)/shard_map/ppermute | solution.py:770
  182.4 5.3 %collective-permute-done.18 = bf16[1,1,144,384]{3,2,1,0:T(8,128)(2,1)S(1)} collective-permute-done((bf16[1,1,144,384]{3,2,1,0:T(8,128)(2,1)S(1)}, bf16[1,1,144,384]{3,2,1,0:T(8,128)(2,1)S(1)}, u32[]{:S(2)}, u32[]{:S(2)}) %collective-permute-start.18) | collective-permute-done | bytes 110624 | tf_op jit(solution)/shard_map/ppermute | solution.py:770
  187.8 1.1 collective-permute-done.21
  188.9 1.0 collective-permute-start.22
  189.9 2.7 %collective-permute-done.19.refs_3_ = bf16[1,144,384]{2,1,0:T(8,128)(2,1)S(1)} collective-permute-done((bf16[1,144,384]{2,1,0:T(8,128)(2,1)S(1)}, bf16[1,144,384]{2,1,0:T(8,128)(2,1)S(1)}, u32[]{:S(2)}, u32[]{:S(2)}) %collective-permute-start.19) | collective-permute-done | bytes 110624 | tf_op jit(solution)/shard_map/ppermute | solution.py:770
  192.6 1.2 collective-permute-done.22.refs_5_
  193.8 1.3 finish.1
  (57 shorter events, 3.1 us)
Async XLA Ops:
  2.9 12.7 %collective-permute-start = (bf16[400,512]{1,0:T(8,128)(2,1)}, bf16[400,512]{1,0:T(8,128)(2,1)S(1)}, u32[]{:S(2)}, u32[]{:S(2)}) collective-permute-start(bf16[400,512]{1,0:T(8,128)(2,1)} %get-tuple-element.92.refs_1_), channel_id=1, source_target_pairs={{0,2},{1,3},{2,0},{3,1},{4,6},{5,7},{6,4},{7,5},{8,10},{9,11},{10,... | collective-permute-start | bytes 1228808 | tf_op jit(solution)/shard_map/ppermute | solution.py:770
  5.9 11.8 %collective-permute-start.4 = (bf16[400,512]{1,0:T(8,128)(2,1)}, bf16[400,512]{1,0:T(8,128)(2,1)S(1)}, u32[]{:S(2)}, u32[]{:S(2)}) collective-permute-start(bf16[400,512]{1,0:T(8,128)(2,1)} %get-tuple-element.92.refs_1_), channel_id=1, source_target_pairs={{0,1},{1,0},{2,3},{3,2},{4,5},{5,4},{6,7},{7,6},{8,9},{9,8},{10,11... | collective-permute-start | bytes 1228808 | tf_op jit(solution)/shard_map/ppermute | solution.py:770
  5.9 0.7 copy-start
  6.6 1.7 copy-start.1
  8.3 0.7 copy-start.4
  9.0 6.6 %copy-start.3 = (bf16[384,512]{1,0:T(8,128)(2,1)S(1)}, bf16[384,512]{1,0:T(8,128)(2,1)}, u32[]{:S(2)}) copy-start(bf16[384,512]{1,0:T(8,128)(2,1)} %get-tuple-element.96.refs_1_) | copy-start | bytes 1179652
  9.0 8.8 %copy-start.2 = (bf16[400,512]{1,0:T(8,128)(2,1)S(1)}, bf16[400,512]{1,0:T(8,128)(2,1)}, u32[]{:S(2)}) copy-start(bf16[400,512]{1,0:T(8,128)(2,1)} %get-tuple-element.92.refs_1_) | copy-start | bytes 1228804
  9.0 8.8 %copy-start.5 = (s32[3]{0:T(128)S(1)}, s32[3]{0:T(128)}, u32[]{:S(2)}) copy-start(s32[3]{0:T(128)} %get-tuple-element.128.scalars_ref.refs_0_) | copy-start | bytes 40
  15.6 2.2 %collective-permute-start.5 = (bf16[400,512]{1,0:T(8,128)(2,1)S(1)}, bf16[400,512]{1,0:T(8,128)(2,1)S(1)}, u32[]{:S(2)}, u32[]{:S(2)}) collective-permute-start(bf16[400,512]{1,0:T(8,128)(2,1)S(1)} %collective-permute-done.refs_2_), channel_id=1, source_target_pairs={{0,1},{1,0},{2,3},{3,2},{4,5},{5,4},{6,7},{7,6},{8,9},{9,8},{10,11... | collective-permute-start | bytes 1228808 | tf_op jit(solution)/shard_map/ppermute | solution.py:770
  15.6 57.9 %collective-permute-start.1 = (bf16[384,512]{1,0:T(8,128)(2,1)S(1)}, bf16[384,512]{1,0:T(8,128)(2,1)S(1)}, u32[]{:S(2)}, u32[]{:S(2)}) collective-permute-start(bf16[384,512]{1,0:T(8,128)(2,1)S(1)} %copy-done.3), channel_id=1, source_target_pairs={{0,2},{1,3},{2,0},{3,1},{4,6},{5,7},{6,4},{7,5},{8,10},{9,11},{10,... | collective-permute-start | bytes 1179656 | tf_op jit(solution)/shard_map/ppermute | solution.py:770
  17.4 56.2 %collective-permute-start.2 = (bf16[384,512]{1,0:T(8,128)(2,1)S(1)}, bf16[384,512]{1,0:T(8,128)(2,1)S(1)}, u32[]{:S(2)}, u32[]{:S(2)}) collective-permute-start(bf16[384,512]{1,0:T(8,128)(2,1)S(1)} %copy-done.3), channel_id=1, source_target_pairs={{0,1},{1,0},{2,3},{3,2},{4,5},{5,4},{6,7},{7,6},{8,9},{9,8},{10,11... | collective-permute-start | bytes 1179656 | tf_op jit(solution)/shard_map/ppermute | solution.py:770
  17.6 56.0 %collective-permute-start.3 = (bf16[384,512]{1,0:T(8,128)(2,1)S(1)}, bf16[384,512]{1,0:T(8,128)(2,1)S(1)}, u32[]{:S(2)}, u32[]{:S(2)}) collective-permute-start(bf16[384,512]{1,0:T(8,128)(2,1)S(1)} %copy-done.3), channel_id=1, source_target_pairs={{0,3},{1,2},{2,1},{3,0},{4,7},{5,6},{6,5},{7,4},{8,11},{9,10},{10,... | collective-permute-start | bytes 1179656 | tf_op jit(solution)/shard_map/ppermute | solution.py:770
  97.5 2.4 %collective-permute-start.6 = (bf16[2,144,1536]{2,1,0:T(8,128)(2,1)S(1)}, bf16[2,144,1536]{2,1,0:T(8,128)(2,1)S(1)}, u32[]{:S(2)}, u32[]{:S(2)}) collective-permute-start(bf16[2,144,1536]{2,1,0:T(8,128)(2,1)S(1)} %get-tuple-element.108), channel_id=1, source_target_pairs={{0,1},{1,0},{2,3},{3,2},{4,5},{5,4},{6,7},{7,6},{8,9},{9,8},{10,11... | collective-permute-start | bytes 2654216 | tf_op jit(solution)/shard_map/ppermute | solution.py:770
  100.3 27.3 %collective-permute-start.7 = (bf16[1,144,1536]{2,1,0:T(8,128)(2,1)S(1)}, bf16[1,144,1536]{2,1,0:T(8,128)(2,1)S(1)}, u32[]{:S(2)}, u32[]{:S(2)}) collective-permute-start(bf16[1,144,1536]{2,1,0:T(8,128)(2,1)S(1)} %get-tuple-element.110), channel_id=1, source_target_pairs={{0,2},{1,3},{2,0},{3,1},{4,6},{5,7},{6,4},{7,5},{8,10},{9,11},{10,... | collective-permute-start | bytes 1327112 | tf_op jit(solution)/shard_map/ppermute | solution.py:770
  127.7 2.7 %collective-permute-start.9 = (bf16[2,2,144,384]{3,2,1,0:T(8,128)(2,1)S(1)}, bf16[2,2,144,384]{3,2,1,0:T(8,128)(2,1)S(1)}, u32[]{:S(2)}, u32[]{:S(2)}) collective-permute-start(bf16[2,2,144,384]{3,2,1,0:T(8,128)(2,1)S(1)} %get-tuple-element.123), channel_id=1, source_target_pairs={{0,1},{1,0},{2,3},{3,2},{4,5},{5,4},{6,7},{7,6},{8,9},{9,8},{10,11... | collective-permute-start | bytes 1327112 | tf_op jit(solution)/shard_map/ppermute | solution.py:770
  127.8 29.1 %collective-permute-start.8 = (bf16[1,144,1536]{2,1,0:T(8,128)(2,1)S(1)}, bf16[1,144,1536]{2,1,0:T(8,128)(2,1)S(1)}, u32[]{:S(2)}, u32[]{:S(2)}) collective-permute-start(bf16[1,144,1536]{2,1,0:T(8,128)(2,1)S(1)} %add_convert_fusion.5), channel_id=1, source_target_pairs={{0,16},{4,20},{8,24},{12,28},{16,0},{20,4},{24,8},{28,12},{1,17},{... | collective-permute-start | bytes 1327112 | tf_op jit(solution)/shard_map/ppermute | solution.py:770
  130.6 26.3 %collective-permute-start.10 = (bf16[1,2,144,384]{3,2,1,0:T(8,128)(2,1)S(1)}, bf16[1,2,144,384]{3,2,1,0:T(8,128)(2,1)S(1)}, u32[]{:S(2)}, u32[]{:S(2)}) collective-permute-start(bf16[1,2,144,384]{3,2,1,0:T(8,128)(2,1)S(1)} %get-tuple-element.124), channel_id=1, source_target_pairs={{0,2},{1,3},{2,0},{3,1},{4,6},{5,7},{6,4},{7,5},{8,10},{9,11},{10,... | collective-permute-start | bytes 663560 | tf_op jit(solution)/shard_map/ppermute | solution.py:770
  156.9 5.3 %copy-start.6 = (bf16[2400,512]{1,0:T(8,128)(2,1)S(1)}, bf16[2400,512]{1,0:T(8,128)(2,1)}, u32[]{:S(2)}) copy-start(bf16[2400,512]{1,0:T(8,128)(2,1)} %get-tuple-element.134) | copy-start | bytes 7372804
  156.9 5.3 %copy-start.7 = (bf16[512,1536]{1,0:T(8,128)(2,1)S(1)}, bf16[512,1536]{1,0:T(8,128)(2,1)}, u32[]{:S(2)}) copy-start(bf16[512,1536]{1,0:T(8,128)(2,1)} %get-tuple-element.133.w_ref) | copy-start | bytes 4718596
  157.1 3.2 %collective-permute-start.11 = (bf16[2,2,144,384]{3,2,1,0:T(8,128)(2,1)S(1)}, bf16[2,2,144,384]{3,2,1,0:T(8,128)(2,1)S(1)}, u32[]{:S(2)}, u32[]{:S(2)}) collective-permute-start(bf16[2,2,144,384]{3,2,1,0:T(8,128)(2,1)S(1)} %get-tuple-element.132), channel_id=1, source_target_pairs={{0,1},{1,0},{2,3},{3,2},{4,5},{5,4},{6,7},{7,6},{8,9},{9,8},{10,11... | collective-permute-start | bytes 1327112 | tf_op jit(solution)/shard_map/ppermute | solution.py:770
  157.2 13.0 %collective-permute-start.12 = (bf16[1,144,1536]{2,1,0:T(8,128)(2,1)S(1)}, bf16[1,144,1536]{2,1,0:T(8,128)(2,1)S(1)}, u32[]{:S(2)}, u32[]{:S(2)}) collective-permute-start(bf16[1,144,1536]{2,1,0:T(8,128)(2,1)S(1)} %add_convert_fusion.3), channel_id=1, source_target_pairs={{0,8},{4,12},{8,0},{12,4},{16,24},{20,28},{24,16},{28,20},{1,9},{5... | collective-permute-start | bytes 1327112 | tf_op jit(solution)/shard_map/ppermute | solution.py:770
  158.8 11.3 %collective-permute-start.13 = (bf16[1,1,144,384]{3,2,1,0:T(8,128)(2,1)S(1)}, bf16[1,1,144,384]{3,2,1,0:T(8,128)(2,1)S(1)}, u32[]{:S(2)}, u32[]{:S(2)}) collective-permute-start(bf16[1,1,144,384]{3,2,1,0:T(8,128)(2,1)S(1)} %get-tuple-element.138), channel_id=1, source_target_pairs={{0,4},{4,0},{8,12},{12,8},{16,20},{20,16},{24,28},{28,24},{1,5},{5... | collective-permute-start | bytes 331784 | tf_op jit(solution)/shard_map/ppermute | solution.py:770
  160.5 9.7 %collective-permute-start.14 = (bf16[1,2,144,384]{3,2,1,0:T(8,128)(2,1)S(1)}, bf16[1,2,144,384]{3,2,1,0:T(8,128)(2,1)S(1)}, u32[]{:S(2)}, u32[]{:S(2)}) collective-permute-start(bf16[1,2,144,384]{3,2,1,0:T(8,128)(2,1)S(1)} %get-tuple-element.139), channel_id=1, source_target_pairs={{0,2},{1,3},{2,0},{3,1},{4,6},{5,7},{6,4},{7,5},{8,10},{9,11},{10,... | collective-permute-start | bytes 663560 | tf_op jit(solution)/shard_map/ppermute | solution.py:770
  170.3 4.8 %collective-permute-start.15 = (bf16[1,1,144,384]{3,2,1,0:T(8,128)(2,1)S(1)}, bf16[1,1,144,384]{3,2,1,0:T(8,128)(2,1)S(1)}, u32[]{:S(2)}, u32[]{:S(2)}) collective-permute-start(bf16[1,1,144,384]{3,2,1,0:T(8,128)(2,1)S(1)} %broadcast_select_fusion), channel_id=1, source_target_pairs={{0,4},{4,0},{8,12},{12,8},{16,20},{20,16},{24,28},{28,24},{1,5},{5... | collective-permute-start | bytes 331784 | tf_op jit(solution)/shard_map/ppermute | solution.py:770
  171.5 6.3 %collective-permute-start.17 = (bf16[1,1,144,384]{3,2,1,0:T(8,128)(2,1)S(1)}, bf16[1,1,144,384]{3,2,1,0:T(8,128)(2,1)S(1)}, u32[]{:S(2)}, u32[]{:S(2)}) collective-permute-start(bf16[1,1,144,384]{3,2,1,0:T(8,128)(2,1)S(1)} %add_convert_fusion.12), channel_id=1, source_target_pairs={{0,8},{4,12},{8,0},{12,4},{16,24},{20,28},{24,16},{28,20},{1,9},{5... | collective-permute-start | bytes 331784 | tf_op jit(solution)/shard_map/ppermute | solution.py:770
  175.1 4.9 %collective-permute-start.20 = (bf16[1,1,144,384]{3,2,1,0:T(8,128)(2,1)S(1)}, bf16[1,1,144,384]{3,2,1,0:T(8,128)(2,1)S(1)}, u32[]{:S(2)}, u32[]{:S(2)}) collective-permute-start(bf16[1,1,144,384]{3,2,1,0:T(8,128)(2,1)S(1)} %add_convert_fusion.13), channel_id=1, source_target_pairs={{0,8},{4,12},{8,0},{12,4},{16,24},{20,28},{24,16},{28,20},{1,9},{5... | collective-permute-start | bytes 331784 | tf_op jit(solution)/shard_map/ppermute | solution.py:770
  176.4 17.4 %collective-permute-start.16 = (bf16[1,144,1536]{2,1,0:T(8,128)(2,1)S(1)}, bf16[1,144,1536]{2,1,0:T(8,128)(2,1)S(1)}, u32[]{:S(2)}, u32[]{:S(2)}) collective-permute-start(bf16[1,144,1536]{2,1,0:T(8,128)(2,1)S(1)} %add_convert_fusion.1), channel_id=1, source_target_pairs={{0,4},{4,0},{8,12},{12,8},{16,20},{20,16},{24,28},{28,24},{1,5},{5... | collective-permute-start | bytes 1327112 | tf_op jit(solution)/shard_map/ppermute | solution.py:770
  177.9 9.8 %collective-permute-start.18 = (bf16[1,1,144,384]{3,2,1,0:T(8,128)(2,1)S(1)}, bf16[1,1,144,384]{3,2,1,0:T(8,128)(2,1)S(1)}, u32[]{:S(2)}, u32[]{:S(2)}) collective-permute-start(bf16[1,1,144,384]{3,2,1,0:T(8,128)(2,1)S(1)} %add_convert_fusion.11), channel_id=1, source_target_pairs={{0,16},{4,20},{8,24},{12,28},{16,0},{20,4},{24,8},{28,12},{1,17},{... | collective-permute-start | bytes 331784 | tf_op jit(solution)/shard_map/ppermute | solution.py:770
  180.1 8.8 %collective-permute-start.21 = (bf16[1,1,144,384]{3,2,1,0:T(8,128)(2,1)S(1)}, bf16[1,1,144,384]{3,2,1,0:T(8,128)(2,1)S(1)}, u32[]{:S(2)}, u32[]{:S(2)}) collective-permute-start(bf16[1,1,144,384]{3,2,1,0:T(8,128)(2,1)S(1)} %add_convert_fusion.9), channel_id=1, source_target_pairs={{0,16},{4,20},{8,24},{12,28},{16,0},{20,4},{24,8},{28,12},{1,17},{... | collective-permute-start | bytes 331784 | tf_op jit(solution)/shard_map/ppermute | solution.py:770
  187.7 4.9 %collective-permute-start.19 = (bf16[1,144,384]{2,1,0:T(8,128)(2,1)S(1)}, bf16[1,144,384]{2,1,0:T(8,128)(2,1)S(1)}, u32[]{:S(2)}, u32[]{:S(2)}) collective-permute-start(bf16[1,144,384]{2,1,0:T(8,128)(2,1)S(1)} %fusion.refs_2_), channel_id=1, source_target_pairs={{0,4},{4,0},{8,12},{12,8},{16,20},{20,16},{24,28},{28,24},{1,5},{5... | collective-permute-start | bytes 331784 | tf_op jit(solution)/shard_map/ppermute | solution.py:770
  188.9 4.9 %collective-permute-start.22 = (bf16[1,144,384]{2,1,0:T(8,128)(2,1)S(1)}, bf16[1,144,384]{2,1,0:T(8,128)(2,1)S(1)}, u32[]{:S(2)}, u32[]{:S(2)}) collective-permute-start(bf16[1,144,384]{2,1,0:T(8,128)(2,1)S(1)} %fusion.1.refs_4_), channel_id=1, source_target_pairs={{0,4},{4,0},{8,12},{12,8},{16,20},{20,16},{24,28},{28,24},{1,5},{5... | collective-permute-start | bytes 331784 | tf_op jit(solution)/shard_map/ppermute | solution.py:770

commit v7 on v6

--- a/solution.py
+++ b/solution.py
@@ -422,7 +422,7 @@
         below = 0.5 * (1.0 + lax.erf(pre_act * (0.5**0.5)))
         activated = (pre_act * below).astype(BF16)
         product = dot(activated, w[2])
-        slope = below + pre_act * (jnp.exp(-0.5 * pre_act * pre_act) * 0.3989422804014327)
+        slope = below + pre_act * (jnp.exp2(pre_act * pre_act * (-0.5 * LOG2E)) * 0.3989422804014327)
         yield
         norm_two, scale_two = normalize(first_norm + (product + down_bias))
         result_ref[rows, :] = (norm_two * gain_two + shift_two).astype(BF16)

time: 198 us -> 199 us (level)
  starting transfers between devices: 25.9 us -> 54.8 us
  Pallas kernels: 148 us -> 120 us
    ppermute x23, starting transfers between devices: 25.9 us -> 54.8 us  [swap(): return lax.ppermute(values, axis, [(i, i ^ mask) for i in range(size)])]
    pallas_call x1, Pallas kernels: 55.8 us -> 27.2 us  [attend(): pl.pallas_call(functools.partial(attend_kernel, held=held, cells=cells),...]
  transfers between devices with their start and end apart: 23 -> 23, of which waited for: 8 -> 8; matrix products, arithmetic and copies ran while one was open for 0% -> 0% of each run, Pallas kernels for 62% -> 47%
where the time goes in v7:
time: 199 us; the launch traced here: 196 us
  Pallas kernels  120 us (60%)
  starting transfers between devices  54.8 us (28%)
  waiting for transfers between devices  15.6 us (8%)
  local copies, waits for them, and re-layouts  3.22 us (2%)
    ppermute x23, starting transfers between devices, swap(): return lax.ppermute(values, axis, [(i, i ^ mask) for i in range(size)])  54.8 us
    pallas_call x2, Pallas kernels, attend_back(): pl.pallas_call(functools.partial(back_kernel, shards=shards, cells=cells,...  51.3 us
    pallas_call x1, Pallas kernels, attend(): pl.pallas_call(functools.partial(attend_kernel, held=held, cells=cells),...  27.2 us
    pallas_call x1, Pallas kernels, middle(): pl.pallas_call(functools.partial(middle_kernel, held=held, cells=cells),...  24.2 us
    ppermute x23, waiting for transfers between devices, swap(): return lax.ppermute(values, axis, [(i, i ^ mask) for i in range(size)])  15.6 us
    pallas_call x1, Pallas kernels, input_grad(): pl.pallas_call(input_kernel, out_shape=jax.ShapeDtypeStruct(dhid.shape, B...  8.01 us
    pallas_call x1, Pallas kernels, gather_known(): pl.pallas_call(gather_kernel, out_shape=(jax.ShapeDtypeStruct((cells, pad...  5.7 us
  transfers between devices with their start and end apart: 23, of which 8 were waited for; matrix products, arithmetic and copies ran while one was open for 0% of the time, Pallas kernels for 47%

profile of v7, /device:TPU:0, one launch (start us, length us, event | category | flops | bytes accessed | tf_op | source)
XLA Modules:
  0.0 195.8 jit_solution(4310407158009297244)
XLA Ops:
  0.7 2.2 %pack.1 = (bf16[400,512]{1,0:T(8,128)(2,1)}, bf16[384,512]{1,0:T(8,128)(2,1)}, s32[3]{0:T(128)}) custom-call(s32[2,1200]{1,0:T(2,128)} %flags_ref.1, bf16[128,512]{1,0:T(8,128)(2,1)} %refs_1_.1, bf16[128,512]{1,0:T(8,128)(2,1)} %refs_2_.1, bf16[128,512]{1,0:T(8,128)(2,1)} %refs_3_.1, bf16[128,512]{1,0:T(8,128)(2,1)} %refs_4_.1, bf16[128,512]{1,0:T(8,128)(2,1)} %refs_5_.1, ...), custom_call_target="tpu_custom_call" | custom-call | tf_op jit(solution)/shard_map/pack/pallas_call | solution.py:81
  2.9 3.0 %collective-permute-start = (bf16[400,512]{1,0:T(8,128)(2,1)}, bf16[400,512]{1,0:T(8,128)(2,1)S(1)}, u32[]{:S(2)}, u32[]{:S(2)}) collective-permute-start(bf16[400,512]{1,0:T(8,128)(2,1)} %get-tuple-element.92.refs_1_), channel_id=1, source_target_pairs={{0,2},{1,3},{2,0},{3,1},{4,6},{5,7},{6,4},{7,5},{8,10},{9,11},{10,... | collective-permute-start | bytes 1228808 | tf_op jit(solution)/shard_map/ppermute | solution.py:770
  5.9 0.7 copy-done
  6.6 1.7 copy-done.1
  8.3 0.7 copy-done.4
  9.0 5.7 %gather_known.1 = (bf16[2,1344,512]{2,1,0:T(8,128)(2,1)}, bf16[2,528,1200]{2,1,0:T(8,128)(2,1)}, s32[2,1,1200]{2,1,0:T(1,128)S(1)}) custom-call(s32[3]{0:T(128)S(1)} %copy-done.4, s32[2,1200]{1,0:T(2,128)S(1)} %copy-done, bf16[2,1200,512]{2,1,0:T(8,128)(2,1)S(1)} %copy-done.1), custom_call_target="tpu_custom_call" | custom-call | flops 4000000000 | bytes 12000000 | tf_op jit(solution)/shard_map/gather_known/pallas_call | solution.py:124
  14.7 0.9 collective-permute-done.refs_2_
  15.6 1.7 collective-permute-start.1
  17.8 27.2 %attend.1 = (bf16[512,1536]{1,0:T(8,128)(2,1)}, f32[16,512]{1,0:T(8,128)S(1)}, bf16[2,4,512,1200]{3,2,1,0:T(8,128)(2,1)}, bf16[2,4,2,256,672]{4,3,2,1,0:T(8,128)...) custom-call(s32[3]{0:T(128)S(1)} %copy-done.5, ...), custom_call_target="tpu_custom_call" | custom-call | flops 20000000000 | bytes 50000000 | tf_op jit(solution)/shard_map/attend/pallas_call | solution.py:320
  45.0 24.2 %middle.1 = (bf16[2400,512]{1,0:T(8,128)(2,1)}, bf16[2400,512]{1,0:T(8,128)(2,1)}, bf16[2400,512]{1,0:T(8,128)(2,1)}, bf16[2,144,1536]{2,1,0:T(8,128)(2,1)S(1)}, bf16[2,144,1536]{2,1,0:T(8,128)(2,1)S(1)}) custom-call(s32[3]{0:T(128)S(1)} %copy-done.5, bf16[384,512]{1,0:T(8,128)(2,1)S(1)} %copy-done.3, bf16[384,512]{1,0:T(8,128)(2,1)S(1)} %collective-permute-done.1.refs_2_, ...), custom_call_target="tpu_custom_call" | custom-call | flops 12000000000 | bytes 19200000 | tf_op jit(solution)/shard_map/middle/pallas_call | solution.py:482
  69.5 2.2 %collective-permute-done.6 = bf16[2,144,1536]{2,1,0:T(8,128)(2,1)S(1)} collective-permute-done((bf16[2,144,1536]{2,1,0:T(8,128)(2,1)S(1)}, bf16[2,144,1536]{2,1,0:T(8,128)(2,1)S(1)}, u32[]{:S(2)}, u32[]{:S(2)}) %collective-permute-start.6) | collective-permute-done | bytes 884768 | tf_op jit(solution)/shard_map/ppermute | solution.py:770
  71.9 1.8 collective-permute-start.7
  73.8 25.5 %attend_back.2 = (bf16[2,2,384,1200]{3,2,1,0:T(8,128)(2,1)}, bf16[2,2,144,384]{3,2,1,0:T(8,128)(2,1)S(1)}, bf16[2,2,144,384]{3,2,1,0:T(8,128)(2,1)S(1)}) custom-call(s32[3]{0:T(128)S(1)} %copy-done.5, s32[2,1,1200]{2,1,0:T(1,128)S(1)} %get-tuple-element.100.refs_7_.pos_ref, bf16[2,528,1200]{2,1,0:T(8,128)(2,1)} %get-tuple-element.93.refs_5_.xt_ref, ...), custom_call_target="tpu_custom_call" | custom-call | flops 24000000000 | bytes 28000000 | tf_op jit(solution)/shard_map/attend_back/pallas_call | solution.py:649
  99.5 13.6 %collective-permute-start.8 = (bf16[1,144,1536]{2,1,0:T(8,128)(2,1)S(1)}, bf16[1,144,1536]{2,1,0:T(8,128)(2,1)S(1)}, u32[]{:S(2)}, u32[]{:S(2)}) collective-permute-start(bf16[1,144,1536]{2,1,0:T(8,128)(2,1)S(1)} %add_convert_fusion.5), channel_id=1, source_target_pairs={{0,16},{4,20},{8,24},{12,28},{16,0},{20,4},{24,8},{28,12},{1,17},{... | collective-permute-start | bytes 1327112 | tf_op jit(solution)/shard_map/ppermute | solution.py:770
  113.6 25.8 %attend_back.3 = (bf16[2,2,384,1200]{3,2,1,0:T(8,128)(2,1)}, bf16[2,2,144,384]{3,2,1,0:T(8,128)(2,1)S(1)}, bf16[2,2,144,384]{3,2,1,0:T(8,128)(2,1)S(1)}) custom-call(s32[3]{0:T(128)S(1)} %copy-done.5, s32[2,1,1200]{2,1,0:T(1,128)S(1)} %get-tuple-element.100.refs_7_.pos_ref, bf16[2,528,1200]{2,1,0:T(8,128)(2,1)} %get-tuple-element.93.refs_5_.xt_ref, ...), custom_call_target="tpu_custom_call" | custom-call | flops 24000000000 | bytes 28000000 | tf_op jit(solution)/shard_map/attend_back/pallas_call | solution.py:649
  139.6 19.5 %collective-permute-start.12 = (bf16[1,144,1536]{2,1,0:T(8,128)(2,1)S(1)}, bf16[1,144,1536]{2,1,0:T(8,128)(2,1)S(1)}, u32[]{:S(2)}, u32[]{:S(2)}) collective-permute-start(bf16[1,144,1536]{2,1,0:T(8,128)(2,1)S(1)} %add_convert_fusion.3), channel_id=1, source_target_pairs={{0,8},{4,12},{8,0},{12,4},{16,24},{20,28},{24,16},{28,20},{1,9},{5... | collective-permute-start | bytes 1327112 | tf_op jit(solution)/shard_map/ppermute | solution.py:770
  159.2 1.5 collective-permute-start.13
  160.8 0.6 collective-permute-start.14
  161.4 8.0 %input_grad.1 = bf16[2,1200,512]{2,1,0:T(8,128)(2,1)} custom-call(bf16[512,1536]{1,0:T(8,128)(2,1)S(1)} %copy-done.7, bf16[2,1200,512]{2,1,0:T(8,128)(2,1)S(1)} %bitcast.17, bf16[2,768,1200]{2,1,0:T(8,128)(2,1)} %bitcast.19, bf16[2,768,1200]{2,1,0:T(8,128)(2,1)} %bitcast.20), custom_call_target="tpu_custom_call" | custom-call | flops 4000000000 | bytes 16000000 | tf_op jit(solution)/shard_map/input_grad/pallas_call | solution.py:707
  170.0 1.6 collective-permute-start.15
  171.6 1.8 collective-permute-start.17
  173.5 1.4 collective-permute-done.15
  174.9 1.8 collective-permute-start.20
  176.7 1.5 collective-permute-start.16
  178.2 1.8 collective-permute-start.18
  180.0 2.5 %collective-permute-start.21 = (bf16[1,1,144,384]{3,2,1,0:T(8,128)(2,1)S(1)}, bf16[1,1,144,384]{3,2,1,0:T(8,128)(2,1)S(1)}, u32[]{:S(2)}, u32[]{:S(2)}) collective-permute-start(bf16[1,1,144,384]{3,2,1,0:T(8,128)(2,1)S(1)} %add_convert_fusion.9), channel_id=1, source_target_pairs={{0,16},{4,20},{8,24},{12,28},{16,0},{20,4},{24,8},{28,12},{1,17},{... | collective-permute-start | bytes 331784 | tf_op jit(solution)/shard_map/ppermute | solution.py:770
  182.5 5.5 %collective-permute-done.18 = bf16[1,1,144,384]{3,2,1,0:T(8,128)(2,1)S(1)} collective-permute-done((bf16[1,1,144,384]{3,2,1,0:T(8,128)(2,1)S(1)}, bf16[1,1,144,384]{3,2,1,0:T(8,128)(2,1)S(1)}, u32[]{:S(2)}, u32[]{:S(2)}) %collective-permute-start.18) | collective-permute-done | bytes 110624 | tf_op jit(solution)/shard_map/ppermute | solution.py:770
  188.1 1.1 collective-permute-done.21
  189.3 1.0 collective-permute-start.22
  190.3 2.8 %collective-permute-done.19.refs_3_ = bf16[1,144,384]{2,1,0:T(8,128)(2,1)S(1)} collective-permute-done((bf16[1,144,384]{2,1,0:T(8,128)(2,1)S(1)}, bf16[1,144,384]{2,1,0:T(8,128)(2,1)S(1)}, u32[]{:S(2)}, u32[]{:S(2)}) %collective-permute-start.19) | collective-permute-done | bytes 110624 | tf_op jit(solution)/shard_map/ppermute | solution.py:770
  193.0 1.2 collective-permute-done.22.refs_5_
  194.2 1.3 finish.1
  (57 shorter events, 3.0 us)
Async XLA Ops:
  2.9 12.7 %collective-permute-start = (bf16[400,512]{1,0:T(8,128)(2,1)}, bf16[400,512]{1,0:T(8,128)(2,1)S(1)}, u32[]{:S(2)}, u32[]{:S(2)}) collective-permute-start(bf16[400,512]{1,0:T(8,128)(2,1)} %get-tuple-element.92.refs_1_), channel_id=1, source_target_pairs={{0,2},{1,3},{2,0},{3,1},{4,6},{5,7},{6,4},{7,5},{8,10},{9,11},{10,... | collective-permute-start | bytes 1228808 | tf_op jit(solution)/shard_map/ppermute | solution.py:770
  5.9 11.8 %collective-permute-start.4 = (bf16[400,512]{1,0:T(8,128)(2,1)}, bf16[400,512]{1,0:T(8,128)(2,1)S(1)}, u32[]{:S(2)}, u32[]{:S(2)}) collective-permute-start(bf16[400,512]{1,0:T(8,128)(2,1)} %get-tuple-element.92.refs_1_), channel_id=1, source_target_pairs={{0,1},{1,0},{2,3},{3,2},{4,5},{5,4},{6,7},{7,6},{8,9},{9,8},{10,11... | collective-permute-start | bytes 1228808 | tf_op jit(solution)/shard_map/ppermute | solution.py:770
  5.9 0.7 copy-start
  6.6 1.7 copy-start.1
  8.3 0.7 copy-start.4
  9.0 6.6 %copy-start.3 = (bf16[384,512]{1,0:T(8,128)(2,1)S(1)}, bf16[384,512]{1,0:T(8,128)(2,1)}, u32[]{:S(2)}) copy-start(bf16[384,512]{1,0:T(8,128)(2,1)} %get-tuple-element.96.refs_1_) | copy-start | bytes 1179652
  9.0 8.8 %copy-start.2 = (bf16[400,512]{1,0:T(8,128)(2,1)S(1)}, bf16[400,512]{1,0:T(8,128)(2,1)}, u32[]{:S(2)}) copy-start(bf16[400,512]{1,0:T(8,128)(2,1)} %get-tuple-element.92.refs_1_) | copy-start | bytes 1228804
  9.0 8.8 %copy-start.5 = (s32[3]{0:T(128)S(1)}, s32[3]{0:T(128)}, u32[]{:S(2)}) copy-start(s32[3]{0:T(128)} %get-tuple-element.128.scalars_ref.refs_0_) | copy-start | bytes 40
  15.6 2.2 %collective-permute-start.5 = (bf16[400,512]{1,0:T(8,128)(2,1)S(1)}, bf16[400,512]{1,0:T(8,128)(2,1)S(1)}, u32[]{:S(2)}, u32[]{:S(2)}) collective-permute-start(bf16[400,512]{1,0:T(8,128)(2,1)S(1)} %collective-permute-done.refs_2_), channel_id=1, source_target_pairs={{0,1},{1,0},{2,3},{3,2},{4,5},{5,4},{6,7},{7,6},{8,9},{9,8},{10,11... | collective-permute-start | bytes 1228808 | tf_op jit(solution)/shard_map/ppermute | solution.py:770
  15.6 29.4 %collective-permute-start.1 = (bf16[384,512]{1,0:T(8,128)(2,1)S(1)}, bf16[384,512]{1,0:T(8,128)(2,1)S(1)}, u32[]{:S(2)}, u32[]{:S(2)}) collective-permute-start(bf16[384,512]{1,0:T(8,128)(2,1)S(1)} %copy-done.3), channel_id=1, source_target_pairs={{0,2},{1,3},{2,0},{3,1},{4,6},{5,7},{6,4},{7,5},{8,10},{9,11},{10,... | collective-permute-start | bytes 1179656 | tf_op jit(solution)/shard_map/ppermute | solution.py:770
  17.4 27.6 %collective-permute-start.2 = (bf16[384,512]{1,0:T(8,128)(2,1)S(1)}, bf16[384,512]{1,0:T(8,128)(2,1)S(1)}, u32[]{:S(2)}, u32[]{:S(2)}) collective-permute-start(bf16[384,512]{1,0:T(8,128)(2,1)S(1)} %copy-done.3), channel_id=1, source_target_pairs={{0,1},{1,0},{2,3},{3,2},{4,5},{5,4},{6,7},{7,6},{8,9},{9,8},{10,11... | collective-permute-start | bytes 1179656 | tf_op jit(solution)/shard_map/ppermute | solution.py:770
  17.6 27.4 %collective-permute-start.3 = (bf16[384,512]{1,0:T(8,128)(2,1)S(1)}, bf16[384,512]{1,0:T(8,128)(2,1)S(1)}, u32[]{:S(2)}, u32[]{:S(2)}) collective-permute-start(bf16[384,512]{1,0:T(8,128)(2,1)S(1)} %copy-done.3), channel_id=1, source_target_pairs={{0,3},{1,2},{2,1},{3,0},{4,7},{5,6},{6,5},{7,4},{8,11},{9,10},{10,... | collective-permute-start | bytes 1179656 | tf_op jit(solution)/shard_map/ppermute | solution.py:770
  69.2 2.4 %collective-permute-start.6 = (bf16[2,144,1536]{2,1,0:T(8,128)(2,1)S(1)}, bf16[2,144,1536]{2,1,0:T(8,128)(2,1)S(1)}, u32[]{:S(2)}, u32[]{:S(2)}) collective-permute-start(bf16[2,144,1536]{2,1,0:T(8,128)(2,1)S(1)} %get-tuple-element.108), channel_id=1, source_target_pairs={{0,1},{1,0},{2,3},{3,2},{4,5},{5,4},{6,7},{7,6},{8,9},{9,8},{10,11... | collective-permute-start | bytes 2654216 | tf_op jit(solution)/shard_map/ppermute | solution.py:770
  71.9 27.3 %collective-permute-start.7 = (bf16[1,144,1536]{2,1,0:T(8,128)(2,1)S(1)}, bf16[1,144,1536]{2,1,0:T(8,128)(2,1)S(1)}, u32[]{:S(2)}, u32[]{:S(2)}) collective-permute-start(bf16[1,144,1536]{2,1,0:T(8,128)(2,1)S(1)} %get-tuple-element.110), channel_id=1, source_target_pairs={{0,2},{1,3},{2,0},{3,1},{4,6},{5,7},{6,4},{7,5},{8,10},{9,11},{10,... | collective-permute-start | bytes 1327112 | tf_op jit(solution)/shard_map/ppermute | solution.py:770
  99.4 13.7 %collective-permute-start.9 = (bf16[2,2,144,384]{3,2,1,0:T(8,128)(2,1)S(1)}, bf16[2,2,144,384]{3,2,1,0:T(8,128)(2,1)S(1)}, u32[]{:S(2)}, u32[]{:S(2)}) collective-permute-start(bf16[2,2,144,384]{3,2,1,0:T(8,128)(2,1)S(1)} %get-tuple-element.123), channel_id=1, source_target_pairs={{0,1},{1,0},{2,3},{3,2},{4,5},{5,4},{6,7},{7,6},{8,9},{9,8},{10,11... | collective-permute-start | bytes 1327112 | tf_op jit(solution)/shard_map/ppermute | solution.py:770
  99.5 39.9 %collective-permute-start.8 = (bf16[1,144,1536]{2,1,0:T(8,128)(2,1)S(1)}, bf16[1,144,1536]{2,1,0:T(8,128)(2,1)S(1)}, u32[]{:S(2)}, u32[]{:S(2)}) collective-permute-start(bf16[1,144,1536]{2,1,0:T(8,128)(2,1)S(1)} %add_convert_fusion.5), channel_id=1, source_target_pairs={{0,16},{4,20},{8,24},{12,28},{16,0},{20,4},{24,8},{28,12},{1,17},{... | collective-permute-start | bytes 1327112 | tf_op jit(solution)/shard_map/ppermute | solution.py:770
  113.2 26.1 %collective-permute-start.10 = (bf16[1,2,144,384]{3,2,1,0:T(8,128)(2,1)S(1)}, bf16[1,2,144,384]{3,2,1,0:T(8,128)(2,1)S(1)}, u32[]{:S(2)}, u32[]{:S(2)}) collective-permute-start(bf16[1,2,144,384]{3,2,1,0:T(8,128)(2,1)S(1)} %get-tuple-element.124), channel_id=1, source_target_pairs={{0,2},{1,3},{2,0},{3,1},{4,6},{5,7},{6,4},{7,5},{8,10},{9,11},{10,... | collective-permute-start | bytes 663560 | tf_op jit(solution)/shard_map/ppermute | solution.py:770
  139.3 22.0 %copy-start.6 = (bf16[2400,512]{1,0:T(8,128)(2,1)S(1)}, bf16[2400,512]{1,0:T(8,128)(2,1)}, u32[]{:S(2)}) copy-start(bf16[2400,512]{1,0:T(8,128)(2,1)} %get-tuple-element.134) | copy-start | bytes 7372804
  139.3 22.0 %copy-start.7 = (bf16[512,1536]{1,0:T(8,128)(2,1)S(1)}, bf16[512,1536]{1,0:T(8,128)(2,1)}, u32[]{:S(2)}) copy-start(bf16[512,1536]{1,0:T(8,128)(2,1)} %get-tuple-element.133.w_ref) | copy-start | bytes 4718596
  139.6 21.1 %collective-permute-start.11 = (bf16[2,2,144,384]{3,2,1,0:T(8,128)(2,1)S(1)}, bf16[2,2,144,384]{3,2,1,0:T(8,128)(2,1)S(1)}, u32[]{:S(2)}, u32[]{:S(2)}) collective-permute-start(bf16[2,2,144,384]{3,2,1,0:T(8,128)(2,1)S(1)} %get-tuple-element.132), channel_id=1, source_target_pairs={{0,1},{1,0},{2,3},{3,2},{4,5},{5,4},{6,7},{7,6},{8,9},{9,8},{10,11... | collective-permute-start | bytes 1327112 | tf_op jit(solution)/shard_map/ppermute | solution.py:770
  139.6 30.3 %collective-permute-start.12 = (bf16[1,144,1536]{2,1,0:T(8,128)(2,1)S(1)}, bf16[1,144,1536]{2,1,0:T(8,128)(2,1)S(1)}, u32[]{:S(2)}, u32[]{:S(2)}) collective-permute-start(bf16[1,144,1536]{2,1,0:T(8,128)(2,1)S(1)} %add_convert_fusion.3), channel_id=1, source_target_pairs={{0,8},{4,12},{8,0},{12,4},{16,24},{20,28},{24,16},{28,20},{1,9},{5... | collective-permute-start | bytes 1327112 | tf_op jit(solution)/shard_map/ppermute | solution.py:770
  159.2 10.2 %collective-permute-start.13 = (bf16[1,1,144,384]{3,2,1,0:T(8,128)(2,1)S(1)}, bf16[1,1,144,384]{3,2,1,0:T(8,128)(2,1)S(1)}, u32[]{:S(2)}, u32[]{:S(2)}) collective-permute-start(bf16[1,1,144,384]{3,2,1,0:T(8,128)(2,1)S(1)} %get-tuple-element.138), channel_id=1, source_target_pairs={{0,4},{4,0},{8,12},{12,8},{16,20},{20,16},{24,28},{28,24},{1,5},{5... | collective-permute-start | bytes 331784 | tf_op jit(solution)/shard_map/ppermute | solution.py:770
  160.8 9.1 %collective-permute-start.14 = (bf16[1,2,144,384]{3,2,1,0:T(8,128)(2,1)S(1)}, bf16[1,2,144,384]{3,2,1,0:T(8,128)(2,1)S(1)}, u32[]{:S(2)}, u32[]{:S(2)}) collective-permute-start(bf16[1,2,144,384]{3,2,1,0:T(8,128)(2,1)S(1)} %get-tuple-element.139), channel_id=1, source_target_pairs={{0,2},{1,3},{2,0},{3,1},{4,6},{5,7},{6,4},{7,5},{8,10},{9,11},{10,... | collective-permute-start | bytes 663560 | tf_op jit(solution)/shard_map/ppermute | solution.py:770
  170.0 4.9 %collective-permute-start.15 = (bf16[1,1,144,384]{3,2,1,0:T(8,128)(2,1)S(1)}, bf16[1,1,144,384]{3,2,1,0:T(8,128)(2,1)S(1)}, u32[]{:S(2)}, u32[]{:S(2)}) collective-permute-start(bf16[1,1,144,384]{3,2,1,0:T(8,128)(2,1)S(1)} %broadcast_select_fusion), channel_id=1, source_target_pairs={{0,4},{4,0},{8,12},{12,8},{16,20},{20,16},{24,28},{28,24},{1,5},{5... | collective-permute-start | bytes 331784 | tf_op jit(solution)/shard_map/ppermute | solution.py:770
  171.6 6.6 %collective-permute-start.17 = (bf16[1,1,144,384]{3,2,1,0:T(8,128)(2,1)S(1)}, bf16[1,1,144,384]{3,2,1,0:T(8,128)(2,1)S(1)}, u32[]{:S(2)}, u32[]{:S(2)}) collective-permute-start(bf16[1,1,144,384]{3,2,1,0:T(8,128)(2,1)S(1)} %add_convert_fusion.12), channel_id=1, source_target_pairs={{0,8},{4,12},{8,0},{12,4},{16,24},{20,28},{24,16},{28,20},{1,9},{5... | collective-permute-start | bytes 331784 | tf_op jit(solution)/shard_map/ppermute | solution.py:770
  174.9 5.0 %collective-permute-start.20 = (bf16[1,1,144,384]{3,2,1,0:T(8,128)(2,1)S(1)}, bf16[1,1,144,384]{3,2,1,0:T(8,128)(2,1)S(1)}, u32[]{:S(2)}, u32[]{:S(2)}) collective-permute-start(bf16[1,1,144,384]{3,2,1,0:T(8,128)(2,1)S(1)} %add_convert_fusion.13), channel_id=1, source_target_pairs={{0,8},{4,12},{8,0},{12,4},{16,24},{20,28},{24,16},{28,20},{1,9},{5... | collective-permute-start | bytes 331784 | tf_op jit(solution)/shard_map/ppermute | solution.py:770
  176.7 17.5 %collective-permute-start.16 = (bf16[1,144,1536]{2,1,0:T(8,128)(2,1)S(1)}, bf16[1,144,1536]{2,1,0:T(8,128)(2,1)S(1)}, u32[]{:S(2)}, u32[]{:S(2)}) collective-permute-start(bf16[1,144,1536]{2,1,0:T(8,128)(2,1)S(1)} %add_convert_fusion.1), channel_id=1, source_target_pairs={{0,4},{4,0},{8,12},{12,8},{16,20},{20,16},{24,28},{28,24},{1,5},{5... | collective-permute-start | bytes 1327112 | tf_op jit(solution)/shard_map/ppermute | solution.py:770
  178.2 9.8 %collective-permute-start.18 = (bf16[1,1,144,384]{3,2,1,0:T(8,128)(2,1)S(1)}, bf16[1,1,144,384]{3,2,1,0:T(8,128)(2,1)S(1)}, u32[]{:S(2)}, u32[]{:S(2)}) collective-permute-start(bf16[1,1,144,384]{3,2,1,0:T(8,128)(2,1)S(1)} %add_convert_fusion.11), channel_id=1, source_target_pairs={{0,16},{4,20},{8,24},{12,28},{16,0},{20,4},{24,8},{28,12},{1,17},{... | collective-permute-start | bytes 331784 | tf_op jit(solution)/shard_map/ppermute | solution.py:770
  180.0 9.2 %collective-permute-start.21 = (bf16[1,1,144,384]{3,2,1,0:T(8,128)(2,1)S(1)}, bf16[1,1,144,384]{3,2,1,0:T(8,128)(2,1)S(1)}, u32[]{:S(2)}, u32[]{:S(2)}) collective-permute-start(bf16[1,1,144,384]{3,2,1,0:T(8,128)(2,1)S(1)} %add_convert_fusion.9), channel_id=1, source_target_pairs={{0,16},{4,20},{8,24},{12,28},{16,0},{20,4},{24,8},{28,12},{1,17},{... | collective-permute-start | bytes 331784 | tf_op jit(solution)/shard_map/ppermute | solution.py:770
  188.1 5.0 %collective-permute-start.19 = (bf16[1,144,384]{2,1,0:T(8,128)(2,1)S(1)}, bf16[1,144,384]{2,1,0:T(8,128)(2,1)S(1)}, u32[]{:S(2)}, u32[]{:S(2)}) collective-permute-start(bf16[1,144,384]{2,1,0:T(8,128)(2,1)S(1)} %fusion.refs_2_), channel_id=1, source_target_pairs={{0,4},{4,0},{8,12},{12,8},{16,20},{20,16},{24,28},{28,24},{1,5},{5... | collective-permute-start | bytes 331784 | tf_op jit(solution)/shard_map/ppermute | solution.py:770
  189.3 5.0 %collective-permute-start.22 = (bf16[1,144,384]{2,1,0:T(8,128)(2,1)S(1)}, bf16[1,144,384]{2,1,0:T(8,128)(2,1)S(1)}, u32[]{:S(2)}, u32[]{:S(2)}) collective-permute-start(bf16[1,144,384]{2,1,0:T(8,128)(2,1)S(1)} %fusion.1.refs_4_), channel_id=1, source_target_pairs={{0,4},{4,0},{8,12},{12,8},{16,20},{20,16},{24,28},{28,24},{1,5},{5... | collective-permute-start | bytes 331784 | tf_op jit(solution)/shard_map/ppermute | solution.py:770
